TPU v7x, 32 devices: a whole 2x2x4 slice. The times are simulated.
32 devices in a mesh: dp: 16 (over z, y, x), mp: 2 (over core).
Axes of the slice: x: 2, y: 2, z: 4, core: 2. Of those that a mesh axis runs over, the one named last changes fastest.
Arguments:
- content_in: bfloat16 [32, 512, 768], P('dp', 'mp'), may hold values from -6 to 6
- query_in: bfloat16 [32, 512, 768], P('dp', 'mp'), may hold values from -6 to 6
- doc_lengths: int32 [32], P('dp'), may hold values from 64 to 512, as said below
- order_ranks: int32 [32, 512], P('dp'), may hold values from 0 to 511, each once within a row
- segment_ids: int32 [32, 512], P('dp'), may hold values from 0 to 3, never falling along the last dimension, each value on 1 to 256 neighbouring positions
- target_flags: int32 [32, 512], P('dp'), may hold values 0 or 1
- query_weight: bfloat16 [768, 768], P(None, 'mp'), may hold values from -0.21875 to 0.21875
- key_weight: bfloat16 [768, 768], P(None, 'mp'), may hold values from -0.21875 to 0.21875
- value_weight: bfloat16 [768, 768], P(None, 'mp'), may hold values from -0.21875 to 0.21875
- out_weight: bfloat16 [768, 768], P('mp'), may hold values from -0.875 to 0.875
- rel_weight: bfloat16 [768, 768], P(None, 'mp'), may hold values from -0.21875 to 0.21875
- content_bias: bfloat16 [768], P('mp'), may hold values from -3 to 3
- position_bias: bfloat16 [768], P('mp'), may hold values from -3 to 3
- segment_bias: bfloat16 [768], P('mp'), may hold values from -3 to 3
- segment_embed: bfloat16 [2, 768], P(None, 'mp'), may hold values from -5 to 5
- first_gain: bfloat16 [768], replicated, may hold values from 0.5 to 1.5
- first_shift: bfloat16 [768], replicated, may hold values from -2 to 2
- up_weight: bfloat16 [768, 3072], P(None, 'mp'), may hold values from -0.21875 to 0.21875
- up_bias: bfloat16 [3072], P('mp'), may hold values from -2 to 2
- down_weight: bfloat16 [3072, 768], P('mp'), may hold values from -0.109375 to 0.109375
- down_bias: bfloat16 [768], replicated, may hold values from -2 to 2
- second_gain: bfloat16 [768], replicated, may hold values from 0.5 to 1.5
- second_shift: bfloat16 [768], replicated, may hold values from -2 to 2
- content_cot: bfloat16 [32, 512, 768], P('dp', 'mp'), may hold values from -6 to 6
- query_cot: bfloat16 [32, 512, 768], P('dp', 'mp'), may hold values from -6 to 6
Outputs:
- content_out: bfloat16 [32, 512, 768], P('dp', 'mp')
- query_out: bfloat16 [32, 512, 768], P('dp', 'mp')
- content_grad: bfloat16 [32, 512, 768], P('dp', 'mp')
- query_grad: bfloat16 [32, 512, 768], P('dp', 'mp')
- query_weight_grad: float32 [768, 768], P(None, 'mp')
- key_weight_grad: float32 [768, 768], P(None, 'mp')
- value_weight_grad: float32 [768, 768], P(None, 'mp')
- out_weight_grad: float32 [768, 768], P('mp')
- rel_weight_grad: float32 [768, 768], P(None, 'mp')
- content_bias_grad: float32 [768], P('mp')
- position_bias_grad: float32 [768], P('mp')
- segment_bias_grad: float32 [768], P('mp')
- segment_embed_grad: float32 [2, 768], P(None, 'mp')
- first_gain_grad: float32 [768], replicated
- first_shift_grad: float32 [768], replicated
- up_weight_grad: float32 [768, 3072], P(None, 'mp')
- up_bias_grad: float32 [3072], P('mp')
- down_weight_grad: float32 [3072, 768], P('mp')
- down_bias_grad: float32 [768], replicated
- second_gain_grad: float32 [768], replicated
- second_shift_grad: float32 [768], replicated
Inputs may be any that keep to these rules, and one draw needn't show every extreme that they name: `doc_lengths`: each document's true length; positions from it on are padding that no query attends to. Document 0 has 512 tokens and document 1 has 64. `order_ranks`: each document's row is a permutation of 0 to 511. `segment_ids`: never falling along a document; each segment at most 256 positions.
All inputs are finite; a program needn't handle non-finite values. No bound on the sum of `target_flags` on one device may be relied on, other than what follows from the above.
Results may differ from a plain program's by a relative error of at most 0.02.
Values may be sent and summed in bfloat16 or wider, within the bound.
A program may use at most 320 MiB of HBM per device.

v0:
```python
import jax
import jax.numpy as jnp
from jax import lax
from jax.sharding import PartitionSpec as P

DH = 64
MICRO = 2


epsilon = 1e-06
highest = lax.Precision.HIGHEST


def layer_norm(value_in, gain, shift):
    center = value_in - jnp.mean(value_in, axis=-1, keepdims=True)
    spread = jnp.mean(center * center, axis=-1, keepdims=True)
    return center * lax.rsqrt(spread + epsilon) * gain + shift


def gelu_tanh(value_in):
    return jax.nn.gelu(value_in, approximate=True)


def positions(seq_len, width):
    column = jnp.arange(2 * seq_len - 1).astype(jnp.float32)
    distance = seq_len - 1.0 - column
    freq_exp = jnp.arange(0, width, 2).astype(jnp.float32) / width
    inverse = 1.0 / 10000.0**freq_exp
    angle = distance[:, None] * inverse[None, :]
    return jnp.concatenate([jnp.sin(angle), jnp.cos(angle)], axis=1)


def skew_rows(table):
    length = table.shape[-2]
    leading = table.shape[:-2]
    flat = table.reshape(leading + (length * (2 * length - 1),))
    middle = flat[..., length - 1 : length - 1 + length * (2 * length - 2)]
    return middle.reshape(leading + (length, 2 * length - 2))[..., :length]


def doc_masks(length, rank_row, segment_row, target_row):
    seq_len = rank_row.shape[0]
    places = jnp.arange(seq_len, dtype=jnp.int32)
    target_live = target_row * (places >= 2).astype(jnp.int32)
    visible = (places[None, :] < length) & (
        (target_live[None, :] == 0) | (rank_row[None, :] < rank_row[:, None])
    )
    diagonal = places[:, None] == places[None, :]
    return (
        visible | diagonal,
        visible & jnp.logical_not(diagonal),
        segment_row[:, None] == segment_row[None, :],
    )


def dot_plain(left_op, right_op):
    return jnp.dot(left_op, right_op, preferred_element_type=jnp.float32)


def dot_left(left_op, right_op):
    return lax.dot_general(
        left_op, right_op, (((0,), (0,)), ((), ())), preferred_element_type=jnp.float32
    )


def dot_right(left_op, right_op):
    return lax.dot_general(
        left_op, right_op, (((1,), (1,)), ((), ())), preferred_element_type=jnp.float32
    )


def doc_scores(parts, key_rows, rel_keys, embed, same, mask):
    content_part = jnp.einsum(
        "qhd,khd->hqk", parts[0], key_rows, preferred_element_type=jnp.float32
    )
    rel_part = skew_rows(
        jnp.einsum("qhd,thd->hqt", parts[1], rel_keys, preferred_element_type=jnp.float32)
    )
    paired = jnp.einsum("qhd,shd->hqs", parts[2], embed, precision=highest)
    seg_part = jnp.where(same[None], paired[..., 0:1], paired[..., 1:2])
    return jnp.where(mask[None], (content_part + rel_part + seg_part) * 0.125, -1e30)


def doc_forward(parts, key_rows, values, rel_keys, embed, same, mask):
    scores = doc_scores(parts, key_rows, rel_keys, embed, same, mask)
    row_max = jnp.max(scores, axis=-1, keepdims=True)
    exp_terms = jnp.exp(scores - row_max)
    row_total = jnp.sum(exp_terms, axis=-1, keepdims=True)
    attn_low = (exp_terms / row_total).astype(jnp.bfloat16)
    vec = jnp.einsum("hqk,khd->qhd", attn_low, values, preferred_element_type=jnp.float32)
    return (vec.astype(jnp.bfloat16), row_max[..., 0] + jnp.log(row_total[..., 0]))


def doc_backward(parts, key_rows, values, rel_keys, embed, same, mask, norm_log, grad_vec):
    scores = doc_scores(parts, key_rows, rel_keys, embed, same, mask)
    attn_prob = jnp.exp(scores - norm_log[..., None])
    attn_low = attn_prob.astype(jnp.bfloat16)
    grad_prob = jnp.einsum("qhd,khd->hqk", grad_vec, values, preferred_element_type=jnp.float32)
    grad_values = jnp.einsum("hqk,qhd->khd", attn_low, grad_vec, preferred_element_type=jnp.float32)
    row_inner = jnp.sum(grad_prob * attn_prob, axis=-1, keepdims=True)
    grad_score = (attn_prob * (grad_prob - row_inner)).astype(jnp.bfloat16) * 0.125
    grad_content = jnp.einsum(
        "hqk,khd->qhd", grad_score, key_rows, preferred_element_type=jnp.float32
    )
    grad_keys = jnp.einsum("hqk,qhd->khd", grad_score, parts[0], preferred_element_type=jnp.float32)
    full_shape = grad_score.shape[:-1] + (2 * grad_score.shape[-1] - 1,)
    skew_pull = jax.vjp(skew_rows, jnp.zeros(full_shape, jnp.float32))[1]
    score_wide = grad_score.astype(jnp.float32)
    grad_full = skew_pull(score_wide)[0].astype(jnp.bfloat16)
    grad_position = jnp.einsum(
        "hqt,thd->qhd", grad_full, rel_keys, preferred_element_type=jnp.float32
    )
    grad_rel = jnp.einsum("hqt,qhd->thd", grad_full, parts[1], preferred_element_type=jnp.float32)
    grad_same = jnp.sum(jnp.where(same[None], score_wide, 0.0), axis=-1)
    grad_other = jnp.sum(jnp.where(same[None], 0.0, score_wide), axis=-1)
    grad_segment = (
        jnp.transpose(grad_same)[:, :, None] * embed[0][None]
        + jnp.transpose(grad_other)[:, :, None] * embed[1][None]
    )
    grad_embed = jnp.stack(
        [
            jnp.einsum("hq,qhd->hd", grad_same, parts[2], precision=highest),
            jnp.einsum("hq,qhd->hd", grad_other, parts[2], precision=highest),
        ]
    )
    return (grad_content, grad_position, grad_segment, grad_keys, grad_values, grad_rel, grad_embed)


def on_device(
    content_in,
    query_in,
    doc_lengths,
    order_ranks,
    segment_ids,
    target_flags,
    query_weight,
    key_weight,
    value_weight,
    out_weight,
    rel_weight,
    content_bias,
    position_bias,
    segment_bias,
    segment_embed,
    first_gain,
    first_shift,
    up_weight,
    up_bias,
    down_weight,
    down_bias,
    second_gain,
    second_shift,
    content_cot,
    query_cot,
):
    docs_dev, half, width = content_in.shape
    seq_len = order_ranks.shape[1]
    per_micro = docs_dev // MICRO
    local_rows = per_micro * half
    full_rows = per_micro * seq_len
    rel_count = 2 * seq_len - 1
    query_use, key_use, value_use, rel_use, out_use = (
        query_weight,
        key_weight,
        value_weight,
        rel_weight,
        out_weight,
    )
    local_cols = query_use.shape[1]
    local_heads = local_cols // DH
    pos_low = positions(seq_len, width).astype(jnp.bfloat16)
    rel_keys = dot_plain(pos_low, rel_use).astype(jnp.bfloat16).reshape(rel_count, local_heads, DH)
    embed = segment_embed.astype(jnp.float32).reshape(2, local_heads, DH)
    bias_content = content_bias.astype(jnp.float32)
    bias_position = position_bias.astype(jnp.float32)
    bias_segment = segment_bias.astype(jnp.float32)
    gain_first = first_gain.astype(jnp.float32)
    shift_first = first_shift.astype(jnp.float32)
    gain_second = second_gain.astype(jnp.float32)
    shift_second = second_shift.astype(jnp.float32)
    bias_down = down_bias.astype(jnp.float32)
    up_use, up_bias_use, down_use = (up_weight, up_bias, down_weight)
    up_bias_wide = up_bias_use.astype(jnp.float32)

    def split_heads(value_in):
        return value_in.reshape(per_micro, seq_len, local_heads, DH)

    def micro_meta(meta, micro_index):
        return meta.reshape((MICRO, per_micro) + meta.shape[1:])[micro_index]

    def micro_rows(tokens, micro_index):
        return tokens.reshape(MICRO, per_micro, half, width)[micro_index]

    def query_parts(proj):
        return (
            split_heads((proj + bias_content).astype(jnp.bfloat16)),
            split_heads((proj + bias_position).astype(jnp.bfloat16)),
            split_heads(proj + bias_segment),
        )

    acc_query = jnp.zeros(query_use.shape, jnp.float32)
    acc_key = jnp.zeros(key_use.shape, jnp.float32)
    acc_value = jnp.zeros(value_use.shape, jnp.float32)
    acc_out = jnp.zeros(out_use.shape, jnp.float32)
    acc_rel = jnp.zeros((rel_count, local_cols), jnp.float32)
    acc_bias_content = jnp.zeros((local_cols,), jnp.float32)
    acc_bias_position = jnp.zeros((local_cols,), jnp.float32)
    acc_bias_segment = jnp.zeros((local_cols,), jnp.float32)
    acc_embed = jnp.zeros((2, local_cols), jnp.float32)
    acc_gain_first = jnp.zeros((width,), jnp.float32)
    acc_shift_first = jnp.zeros((width,), jnp.float32)
    acc_up = jnp.zeros(up_use.shape, jnp.float32)
    acc_up_bias = jnp.zeros(up_bias_use.shape, jnp.float32)
    acc_down = jnp.zeros(down_use.shape, jnp.float32)
    acc_down_bias = jnp.zeros((width,), jnp.float32)
    acc_gain_second = jnp.zeros((width,), jnp.float32)
    acc_shift_second = jnp.zeros((width,), jnp.float32)
    outs_content = []
    outs_query = []
    grads_content = []
    grads_query = []
    for micro_index in range(MICRO):
        content_rows = micro_rows(content_in, micro_index)
        query_rows = micro_rows(query_in, micro_index)
        content_local = content_rows.reshape(local_rows, width)
        query_local = query_rows.reshape(local_rows, width)
        cot_content = (
            micro_rows(content_cot, micro_index).reshape(local_rows, width).astype(jnp.float32)
        )
        cot_query = (
            micro_rows(query_cot, micro_index).reshape(local_rows, width).astype(jnp.float32)
        )
        lengths = micro_meta(doc_lengths, micro_index)
        ranks = micro_meta(order_ranks, micro_index)
        segments = micro_meta(segment_ids, micro_index)
        targets = micro_meta(target_flags, micro_index)
        content_wide, query_wide = (
            lax.all_gather(content_rows, "mp", axis=1, tiled=True),
            lax.all_gather(query_rows, "mp", axis=1, tiled=True),
        )
        content_all = content_wide.reshape(full_rows, width)
        query_all = query_wide.reshape(full_rows, width)
        proj_content = dot_plain(content_all, query_use)
        proj_query = dot_plain(query_all, query_use)
        key_rows = split_heads(dot_plain(content_all, key_use).astype(jnp.bfloat16))
        values = split_heads(dot_plain(content_all, value_use).astype(jnp.bfloat16))
        parts_content = query_parts(proj_content)
        parts_query = query_parts(proj_query)

        def attend_forward(entry):
            (
                content_parts,
                stream_parts,
                key_doc,
                value_doc,
                length,
                rank_row,
                segment_row,
                target_row,
            ) = entry
            mask_content, mask_query, same = doc_masks(length, rank_row, segment_row, target_row)
            vec_content, log_content = doc_forward(
                content_parts, key_doc, value_doc, rel_keys, embed, same, mask_content
            )
            vec_query, log_query = doc_forward(
                stream_parts, key_doc, value_doc, rel_keys, embed, same, mask_query
            )
            return (vec_content, vec_query, log_content, log_query)

        vec_content, vec_query, log_content, log_query = lax.map(
            attend_forward,
            (parts_content, parts_query, key_rows, values, lengths, ranks, segments, targets),
        )
        flat_content = vec_content.reshape(full_rows, local_cols)
        flat_query = vec_query.reshape(full_rows, local_cols)
        mixed_content, mixed_query = (
            lax.psum_scatter(
                dot_plain(flat_content, out_use).reshape(per_micro, seq_len, width),
                "mp",
                scatter_dimension=1,
                tiled=True,
            ),
            lax.psum_scatter(
                dot_plain(flat_query, out_use).reshape(per_micro, seq_len, width),
                "mp",
                scatter_dimension=1,
                tiled=True,
            ),
        )
        pre_content = mixed_content.reshape(local_rows, width) + content_local.astype(jnp.float32)
        pre_query = mixed_query.reshape(local_rows, width) + query_local.astype(jnp.float32)
        first_content = layer_norm(pre_content, gain_first, shift_first).astype(jnp.bfloat16)
        first_query = layer_norm(pre_query, gain_first, shift_first).astype(jnp.bfloat16)
        first_all_content, first_all_query = (
            lax.all_gather(first_content, "mp", axis=0, tiled=True),
            lax.all_gather(first_query, "mp", axis=0, tiled=True),
        )
        ffn_rows = jnp.concatenate([first_all_content, first_all_query], axis=0)
        hidden = dot_plain(ffn_rows, up_use) + up_bias_wide
        act = gelu_tanh(hidden).astype(jnp.bfloat16)
        down_part = dot_plain(act, down_use)
        split_at = down_part.shape[0] // 2
        down_content, down_query = (
            lax.psum_scatter(down_part[:split_at], "mp", scatter_dimension=0, tiled=True),
            lax.psum_scatter(down_part[split_at:], "mp", scatter_dimension=0, tiled=True),
        )
        pre2_content = first_content.astype(jnp.float32) + down_content + bias_down
        pre2_query = first_query.astype(jnp.float32) + down_query + bias_down
        norm_content, pull_content = jax.vjp(layer_norm, pre2_content, gain_second, shift_second)
        norm_query, pull_query = jax.vjp(layer_norm, pre2_query, gain_second, shift_second)
        outs_content.append(norm_content.astype(jnp.bfloat16))
        outs_query.append(norm_query.astype(jnp.bfloat16))
        grad_pre2_content, gain_term_c, shift_term_c = pull_content(cot_content)
        grad_pre2_query, gain_term_q, shift_term_q = pull_query(cot_query)
        acc_gain_second = acc_gain_second + gain_term_c + gain_term_q
        acc_shift_second = acc_shift_second + shift_term_c + shift_term_q
        acc_down_bias = (
            acc_down_bias + jnp.sum(grad_pre2_content, axis=0) + jnp.sum(grad_pre2_query, axis=0)
        )
        grad_down_content = grad_pre2_content.astype(jnp.bfloat16)
        grad_down_query = grad_pre2_query.astype(jnp.bfloat16)
        grad_all_content, grad_all_query = (
            lax.all_gather(grad_down_content, "mp", axis=0, tiled=True),
            lax.all_gather(grad_down_query, "mp", axis=0, tiled=True),
        )
        down_grad_rows = jnp.concatenate([grad_all_content, grad_all_query], axis=0)
        acc_down = acc_down + dot_left(act, down_grad_rows)
        grad_act = dot_right(down_grad_rows, down_use)
        gelu_pull = jax.vjp(gelu_tanh, hidden)[1]
        grad_hidden = gelu_pull(grad_act)[0].astype(jnp.bfloat16)
        acc_up_bias = acc_up_bias + jnp.sum(grad_hidden.astype(jnp.float32), axis=0)
        acc_up = acc_up + dot_left(ffn_rows, grad_hidden)
        back_rows = dot_right(grad_hidden, up_use)
        back_content, back_query = (
            lax.psum_scatter(back_rows[:split_at], "mp", scatter_dimension=0, tiled=True),
            lax.psum_scatter(back_rows[split_at:], "mp", scatter_dimension=0, tiled=True),
        )
        first_pull_c = jax.vjp(layer_norm, pre_content, gain_first, shift_first)[1]
        first_pull_q = jax.vjp(layer_norm, pre_query, gain_first, shift_first)[1]
        grad_pre_content, gain_term_c, shift_term_c = first_pull_c(back_content + grad_pre2_content)
        grad_pre_query, gain_term_q, shift_term_q = first_pull_q(back_query + grad_pre2_query)
        acc_gain_first = acc_gain_first + gain_term_c + gain_term_q
        acc_shift_first = acc_shift_first + shift_term_c + shift_term_q
        mixed_wide_c, mixed_wide_q = (
            lax.all_gather(
                grad_pre_content.astype(jnp.bfloat16).reshape(per_micro, half, width),
                "mp",
                axis=1,
                tiled=True,
            ),
            lax.all_gather(
                grad_pre_query.astype(jnp.bfloat16).reshape(per_micro, half, width),
                "mp",
                axis=1,
                tiled=True,
            ),
        )
        mixed_grad_content = mixed_wide_c.reshape(full_rows, width)
        mixed_grad_query = mixed_wide_q.reshape(full_rows, width)
        acc_out = (
            acc_out
            + dot_left(flat_content, mixed_grad_content)
            + dot_left(flat_query, mixed_grad_query)
        )
        grad_vec_content = split_heads(dot_right(mixed_grad_content, out_use).astype(jnp.bfloat16))
        grad_vec_query = split_heads(dot_right(mixed_grad_query, out_use).astype(jnp.bfloat16))

        def attend_backward(entry):
            (
                content_parts,
                stream_parts,
                key_doc,
                value_doc,
                length,
                rank_row,
                segment_row,
                target_row,
                norm_content_log,
                norm_query_log,
                grad_content_vec,
                grad_query_vec,
            ) = entry
            mask_content, mask_query, same = doc_masks(length, rank_row, segment_row, target_row)
            back_c = doc_backward(
                content_parts,
                key_doc,
                value_doc,
                rel_keys,
                embed,
                same,
                mask_content,
                norm_content_log,
                grad_content_vec,
            )
            back_q = doc_backward(
                stream_parts,
                key_doc,
                value_doc,
                rel_keys,
                embed,
                same,
                mask_query,
                norm_query_log,
                grad_query_vec,
            )
            proj_grad_c = back_c[0] + back_c[1] + back_c[2]
            proj_grad_q = back_q[0] + back_q[1] + back_q[2]
            bias_terms = (
                jnp.sum(back_c[0] + back_q[0], axis=0),
                jnp.sum(back_c[1] + back_q[1], axis=0),
                jnp.sum(back_c[2] + back_q[2], axis=0),
            )
            return (
                proj_grad_c,
                proj_grad_q,
                back_c[3] + back_q[3],
                back_c[4] + back_q[4],
                back_c[5] + back_q[5],
                back_c[6] + back_q[6],
                bias_terms,
            )

        proj_grad_c, proj_grad_q, key_grad, value_grad, rel_grad, embed_grad, bias_terms = lax.map(
            attend_backward,
            (
                parts_content,
                parts_query,
                key_rows,
                values,
                lengths,
                ranks,
                segments,
                targets,
                log_content,
                log_query,
                grad_vec_content,
                grad_vec_query,
            ),
        )
        acc_rel = acc_rel + jnp.sum(rel_grad, axis=0).reshape(rel_count, local_cols)
        acc_embed = acc_embed + jnp.sum(embed_grad, axis=0).reshape(2, local_cols)
        acc_bias_content = acc_bias_content + jnp.sum(bias_terms[0], axis=0).reshape(local_cols)
        acc_bias_position = acc_bias_position + jnp.sum(bias_terms[1], axis=0).reshape(local_cols)
        acc_bias_segment = acc_bias_segment + jnp.sum(bias_terms[2], axis=0).reshape(local_cols)
        low_proj_c = proj_grad_c.reshape(full_rows, local_cols).astype(jnp.bfloat16)
        low_proj_q = proj_grad_q.reshape(full_rows, local_cols).astype(jnp.bfloat16)
        low_key = key_grad.reshape(full_rows, local_cols).astype(jnp.bfloat16)
        low_value = value_grad.reshape(full_rows, local_cols).astype(jnp.bfloat16)
        again_wide_c, again_wide_q = (
            lax.all_gather(content_rows, "mp", axis=1, tiled=True),
            lax.all_gather(query_rows, "mp", axis=1, tiled=True),
        )
        again_content = again_wide_c.reshape(full_rows, width)
        again_query = again_wide_q.reshape(full_rows, width)
        acc_query = (
            acc_query + dot_left(again_content, low_proj_c) + dot_left(again_query, low_proj_q)
        )
        acc_key = acc_key + dot_left(again_content, low_key)
        acc_value = acc_value + dot_left(again_content, low_value)
        back_all_content = (
            dot_right(low_proj_c, query_use)
            + dot_right(low_key, key_use)
            + dot_right(low_value, value_use)
        )
        back_all_query = dot_right(low_proj_q, query_use)
        input_content, input_query = (
            lax.psum_scatter(
                back_all_content.reshape(per_micro, seq_len, width).astype(jnp.bfloat16),
                "mp",
                scatter_dimension=1,
                tiled=True,
            ).astype(jnp.float32),
            lax.psum_scatter(
                back_all_query.reshape(per_micro, seq_len, width).astype(jnp.bfloat16),
                "mp",
                scatter_dimension=1,
                tiled=True,
            ).astype(jnp.float32),
        )
        grads_content.append(
            (input_content.reshape(local_rows, width) + grad_pre_content).astype(jnp.bfloat16)
        )
        grads_query.append(
            (input_query.reshape(local_rows, width) + grad_pre_query).astype(jnp.bfloat16)
        )
    acc_rel_weight = jnp.dot(jnp.transpose(pos_low.astype(jnp.float32)), acc_rel, precision=highest)
    small_grads = lax.psum(
        (acc_gain_first, acc_shift_first, acc_gain_second, acc_shift_second, acc_down_bias), "mp"
    )
    up_grad, up_bias_grad, down_grad = (acc_up, acc_up_bias, acc_down)
    summed = lax.psum(
        (
            acc_query,
            acc_key,
            acc_value,
            acc_out,
            acc_rel_weight,
            acc_bias_content,
            acc_bias_position,
            acc_bias_segment,
            acc_embed,
            small_grads[0],
            small_grads[1],
            up_grad,
            up_bias_grad,
            down_grad,
            small_grads[4],
            small_grads[2],
            small_grads[3],
        ),
        "dp",
    )

    def stacked(pieces):
        return jnp.stack(pieces, axis=0)

    return (
        stacked(outs_content),
        stacked(outs_query),
        stacked(grads_content),
        stacked(grads_query),
        summed[0],
        summed[1],
        summed[2],
        summed[3],
        summed[4],
        summed[5],
        summed[6],
        summed[7],
        summed[8],
        summed[9],
        summed[10],
        summed[11],
        summed[12],
        summed[13],
        summed[14],
        summed[15],
        summed[16],
    )


def solution(mesh):
    placed = (
        P("dp", "mp", None),
        P("dp", "mp", None),
        P("dp"),
        P("dp", None),
        P("dp", None),
        P("dp", None),
        P(None, "mp"),
        P(None, "mp"),
        P(None, "mp"),
        P("mp", None),
        P(None, "mp"),
        P("mp"),
        P("mp"),
        P("mp"),
        P(None, "mp"),
        P(),
        P(),
        P(None, "mp"),
        P("mp"),
        P("mp", None),
        P(),
        P(),
        P(),
        P("dp", "mp", None),
        P("dp", "mp", None),
    )
    return jax.shard_map(
        on_device,
        mesh=mesh,
        in_specs=placed,
        out_specs=(
            P("dp", "mp", None),
            P("dp", "mp", None),
            P("dp", "mp", None),
            P("dp", "mp", None),
            P(None, "mp"),
            P(None, "mp"),
            P(None, "mp"),
            P("mp", None),
            P(None, "mp"),
            P("mp"),
            P("mp"),
            P("mp"),
            P(None, "mp"),
            P(),
            P(),
            P(None, "mp"),
            P("mp"),
            P("mp", None),
            P(),
            P(),
            P(),
        ),
        check_vma=False,
    )
```

profile of v0, /device:TPU:0, one launch (start us, length us, event | category | flops | bytes accessed | tf_op | source)
XLA Modules:
  0.0 1557.4 jit_solution(5586328239896935444)
XLA Ops:
  53.2 13.6 reshape.1196
  66.9 14.0 reshape.1131
  80.9 12.9 slice.259
  93.7 13.1 reshape.1198
  106.8 14.6 reshape.1132
  157.0 13.9 reshape.1204
  171.0 14.0 reshape.1120
  185.0 12.9 slice.250
  197.9 13.1 reshape.1206
  211.0 14.2 reshape.1121
  261.9 14.5 reshape.1208
  276.4 14.0 reshape.1126
  290.5 12.9 slice.254
  303.3 13.1 reshape.1210
  316.4 14.2 reshape.1127
  362.6 14.1 reshape.1200
  376.7 14.0 reshape.1136
  390.7 12.9 slice.263
  403.5 13.1 reshape.1202
  416.6 14.2 reshape.1137
  525.2 13.2 reduce-scatter.21.cloned.1.call-done
  562.9 15.7 %convert_reduce_fusion.1 = (f32[1536]{0:T(1024)}, bf16[1024,1536]{1,0:T(8,128)(2,1)}, f32[1536]{0:T(1024)}, bf16[1024,1536]{1,0:T(8,128)(2,1)S(1)}) fusion(f32[1024,1536]{1,0:T(8,128)} %get-tuple-element.571, f32[1536]{0:T(1024)S(1)} %copy-done.193, f32[1024,1536]{1,0:T(8,128)S(1)} %fusion.260, f32[1024,1536]{1,0:T(8,128)} %copy-done.211, ...), kind=kOutput, calls=%fused_computation.39 | convolution fusion | flops 2488267776 | bytes 29116416 | tf_op jit(solution)/shard_map/dot_general | solution.py:67
  780.5 15.4 reshape.1214
  795.9 13.9 convert_element_type.544
  847.3 15.4 reshape.1222
  862.7 13.9 convert_element_type.569
  917.7 15.4 reshape.1218
  933.1 13.9 convert_element_type.515
  984.7 15.4 reshape.1226
  1000.1 13.9 convert_element_type.562
  1125.9 82.2 %all-reduce.8 = (f32[384]{0:T(512)}, f32[384]{0:T(512)}, f32[384]{0:T(512)}, f32[2,384]{1,0:T(2,128)}, f32[768]{0:T(1024)}, /*index=5*/f32[768]{0:T(1024)}, f32[...) all-reduce(f32[384]{0:T(512)S(1)} %add.877, ...), channel_id=1, replica_groups=mesh['dp'=16,'mp'=2] {'dp'}, use_global_device_ids=true, to_apply=%region_75.76 | all-reduce | flops 7296 | bytes 58368 | tf_op jit(solution)/shard_map/psum | solution.py:491
  1215.0 319.3 %all-reduce.13.cloned.1.call-done = (f32[768,384]{0,1:T(8,128)}, f32[768,384]{0,1:T(8,128)}, f32[768,384]{0,1:T(8,128)}, f32[384,768]{1,0:T(8,128)}, f32[768,384...) async-done(((f32[768,384]{0,1:T(8,128)}, f32[768,384]{0,1:T(8,128)}, f32[768,384]{0,1:T(8,128)}, f32[384,768]{1,0:T(8,128)}, f32[768,384]{1,0:T(8,128)}, ...) | async-done | bytes 15335440 | tf_op jit(solution)/shard_map/psum | solution.py:491
  (818 shorter events, 719.3 us)
Async XLA Ops:
  7.2 476.0 %copy-start = (bf16[1536,768]{1,0:T(8,128)(2,1)S(1)}, bf16[1536,768]{1,0:T(8,128)(2,1)}, u32[]{:S(2)}) copy-start(bf16[1536,768]{1,0:T(8,128)(2,1)} %param.44) | copy-start | bytes 7077892
  7.2 25.6 %copy-start.8 = (bf16[768,384]{1,0:T(8,128)(2,1)S(1)}, bf16[768,384]{1,0:T(8,128)(2,1)}, u32[]{:S(2)}) copy-start(bf16[768,384]{1,0:T(8,128)(2,1)} %param.31) | copy-start | bytes 1769476
  7.2 450.1 %reduce-scatter.23.cloned.1.call-start = ((), (), s32[]{:S(2)}) async-start(), calls=%async_computation.19 | async-start | bytes 2359296 | tf_op jit(solution)/shard_map/reduce_scatter | solution.py:277
  25.5 111.9 %copy-start.57 = (bf16[512,384]{0,1:T(8,128)(2,1)}, bf16[512,384]{0,1:T(8,128)(2,1)S(1)}, u32[]{:S(2)}) copy-start(bf16[512,384]{0,1:T(8,128)(2,1)S(1)} %convolution_convert_fusion.7) | copy-start | bytes 1179652
  46.9 309.4 %copy-start.6 = (bf16[1023,384]{0,1:T(8,128)(2,1)}, bf16[1023,384]{0,1:T(8,128)(2,1)S(1)}, u32[]{:S(2)}) copy-start(bf16[1023,384]{0,1:T(8,128)(2,1)S(1)} %convolution_convert_fusion) | copy-start | bytes 2356996
  147.8 309.5 %reduce-scatter.17.cloned.1.call-start = ((), (), s32[]{:S(2)}) async-start(), calls=%async_computation.16 | async-start | bytes 2359296 | tf_op jit(solution)/shard_map/reduce_scatter | solution.py:277
  242.0 103.7 %copy-start.55 = (bf16[512,384]{0,1:T(8,128)(2,1)}, bf16[512,384]{0,1:T(8,128)(2,1)S(1)}, u32[]{:S(2)}) copy-start(bf16[512,384]{0,1:T(8,128)(2,1)S(1)} %convolution_convert_fusion.9) | copy-start | bytes 1179652
  254.5 206.9 %reduce-scatter.19.cloned.1.call-start = ((), (), s32[]{:S(2)}) async-start(), calls=%async_computation.17 | async-start | bytes 2359296 | tf_op jit(solution)/shard_map/reduce_scatter | solution.py:283
  356.2 111.1 %reduce-scatter.25.cloned.1.call-start = ((), (), s32[]{:S(2)}) async-start(), calls=%async_computation.20 | async-start | bytes 2359296 | tf_op jit(solution)/shard_map/reduce_scatter | solution.py:283
  455.4 57.0 %reduce-scatter.31.cloned.1.call-start = ((), (), s32[]{:S(2)}) async-start(), calls=%async_computation.23 | async-start | bytes 2359296 | tf_op jit(solution)/shard_map/reduce_scatter | solution.py:305
  489.2 23.2 %reduce-scatter.27.cloned.1.call-start = ((), (), s32[]{:S(2)}) async-start(), calls=%async_computation.21 | async-start | bytes 2359296 | tf_op jit(solution)/shard_map/reduce_scatter | solution.py:304
  489.8 35.4 %reduce-scatter.29.cloned.1.call-start = ((), (), s32[]{:S(2)}) async-start(), calls=%async_computation.22 | async-start | bytes 2359296 | tf_op jit(solution)/shard_map/reduce_scatter | solution.py:305
  507.6 30.8 %reduce-scatter.21.cloned.1.call-start = ((), (), s32[]{:S(2)}) async-start(), calls=%async_computation.18 | async-start | bytes 2359296 | tf_op jit(solution)/shard_map/reduce_scatter | solution.py:304
  508.4 108.7 %reduce-scatter.41.cloned.1.call-start = ((), (), s32[]{:S(2)}) async-start(), calls=%async_computation.28 | async-start | bytes 2359296 | tf_op jit(solution)/shard_map/reduce_scatter | solution.py:336
  583.1 34.0 %reduce-scatter.33.cloned.1.call-start = ((), (), s32[]{:S(2)}) async-start(), calls=%async_computation.24 | async-start | bytes 2359296 | tf_op jit(solution)/shard_map/reduce_scatter | solution.py:335
  590.6 31.1 %reduce-scatter.39.cloned.1.call-start = ((), (), s32[]{:S(2)}) async-start(), calls=%async_computation.27 | async-start | bytes 2359296 | tf_op jit(solution)/shard_map/reduce_scatter | solution.py:335
  591.3 39.7 %reduce-scatter.35.cloned.1.call-start = ((), (), s32[]{:S(2)}) async-start(), calls=%async_computation.25 | async-start | bytes 2359296 | tf_op jit(solution)/shard_map/reduce_scatter | solution.py:336
  593.4 53.0 %copy-start.146 = (f32[6,512]{1,0:T(8,128)}, f32[6,512]{1,0:T(8,128)S(1)}, u32[]{:S(2)}) copy-start(f32[6,512]{1,0:T(8,128)S(1)} %log_add_fusion.2) | copy-start | bytes 36868
  593.4 55.0 %copy-start.142 = (f32[6,512]{1,0:T(8,128)}, f32[6,512]{1,0:T(8,128)S(1)}, u32[]{:S(2)}) copy-start(f32[6,512]{1,0:T(8,128)S(1)} %log_add_fusion.3) | copy-start | bytes 36868
  601.4 606.7 %reduce-scatter.47.cloned.1.call-start = ((), (), s32[]{:S(2)}) async-start(), calls=%async_computation.31 | async-start | bytes 1179648 | tf_op jit(solution)/shard_map/reduce_scatter | solution.py:473
  676.4 351.0 %copy-start.50 = (f32[6,64,512]{2,1,0:T(8,128)}, f32[6,64,512]{2,1,0:T(8,128)S(1)}, u32[]{:S(2)}) copy-start(f32[6,64,512]{2,1,0:T(8,128)S(1)} %fusion.256) | copy-start | bytes 2359300
  1032.8 176.5 %reduce-scatter.45.cloned.1.call-start = ((), (), s32[]{:S(2)}) async-start(), calls=%async_computation.30 | async-start | bytes 1179648 | tf_op jit(solution)/shard_map/reduce_scatter | solution.py:473
  1049.7 162.0 %reduce-scatter.43.cloned.1.call-start = ((), (), s32[]{:S(2)}) async-start(), calls=%async_computation.29 | async-start | bytes 1179648 | tf_op jit(solution)/shard_map/reduce_scatter | solution.py:467
  1065.3 147.6 %reduce-scatter.37.cloned.1.call-start = ((), (), s32[]{:S(2)}) async-start(), calls=%async_computation.26 | async-start | bytes 1179648 | tf_op jit(solution)/shard_map/reduce_scatter | solution.py:467
  1086.3 448.0 %all-reduce.13.cloned.1.call-start = ((), (), s32[]{:S(2)}) async-start(), calls=%async_computation.32 | async-start | bytes 30670848 | tf_op jit(solution)/shard_map/psum | solution.py:491
  1103.6 18.7 %copy-start.174 = (f32[768]{0:T(1024)S(1)}, f32[768]{0:T(1024)}, u32[]{:S(2)}) copy-start(f32[768]{0:T(1024)} %add_add_fusion.17) | copy-start | bytes 9220
  1103.6 22.2 %copy-start.158 = (f32[1536]{0:T(1024)S(1)}, f32[1536]{0:T(1024)}, u32[]{:S(2)}) copy-start(f32[1536]{0:T(1024)} %add.896) | copy-start | bytes 18436
  1106.6 105.1 %copy-start.190 = (f32[256]{0:T(256)S(1)}, f32[256]{0:T(256)}, u32[]{:S(2)}) copy-start(f32[256]{0:T(256)} %copy-done.189) | copy-start | bytes 3076
  1108.1 100.0 %copy-start.44 = (f32[256,768]{1,0:T(8,128)S(1)}, f32[256,768]{1,0:T(8,128)}, u32[]{:S(2)}) copy-start(f32[256,768]{1,0:T(8,128)} %get-tuple-element.533) | copy-start | bytes 2359300
  1109.8 103.1 %copy-start.187 = (f32[256]{0:T(256)S(1)}, f32[256]{0:T(256)}, u32[]{:S(2)}) copy-start(f32[256]{0:T(256)} %copy-done.186) | copy-start | bytes 3076
  1110.6 102.3 %copy-start.46 = (f32[256,768]{1,0:T(8,128)S(1)}, f32[256,768]{1,0:T(8,128)}, u32[]{:S(2)}) copy-start(f32[256,768]{1,0:T(8,128)} %copy-done.45) | copy-start | bytes 2359300
  1113.9 97.8 %copy-start.48 = (f32[256,768]{1,0:T(8,128)S(1)}, f32[256,768]{1,0:T(8,128)}, u32[]{:S(2)}) copy-start(f32[256,768]{1,0:T(8,128)} %get-tuple-element.531) | copy-start | bytes 2359300
  (214 other events, 1437.5 us)
Sparse Core Ops, SparseCore 0:
  147.9 11.6 reduce-scatter.22
  254.7 11.7 reduce-scatter.16
  356.3 11.5 reduce-scatter.18
  455.6 11.6 reduce-scatter.24
  489.3 10.2 reduce-scatter.30
  501.8 10.2 reduce-scatter.26
  514.9 10.2 reduce-scatter.28
  528.1 10.2 reduce-scatter.20
  583.2 10.2 reduce-scatter.40
  595.7 10.2 reduce-scatter.32
  608.3 10.2 reduce-scatter.38
  620.7 10.2 reduce-scatter.34
  1032.9 9.4 reduce-scatter.46
  1049.8 9.4 reduce-scatter.44
  1065.4 9.4 reduce-scatter.42
  1086.5 9.4 reduce-scatter.36
  1104.0 430.2 all-reduce.12
where the time goes:
time: 1570 us; the launch traced here: 1560 us
  local copies, waits for them, and re-layouts  658 us (42%)
  waiting for transfers between devices  363 us (23%)
  matrix products  314 us (20%)
  blocking collectives  125 us (8%)
  other arithmetic  78.7 us (5%)
  between operations  17.3 us (1%)
    psum x1, waiting for transfers between devices, on_device(): lax.psum((acc_query, acc_key, acc_value, acc_out, acc_rel_weight, acc_bia...  319 us
    unnamed x497, local copies, waits for them, and re-layouts  292 us
    reshape x8, local copies, waits for them, and re-layouts, skew_rows(): return middle.reshape(leading + (length, 2 * length - 2))[..., :length]  107 us
    psum x1, blocking collectives, on_device(): lax.psum((acc_query, acc_key, acc_value, acc_out, acc_rel_weight, acc_bia...  82.2 us
    reshape x4, local copies, waits for them, and re-layouts, skew_rows(): flat = table.reshape(leading + (length * (2 * length - 1),))  56.1 us
    convert_element_type x4, local copies, waits for them, and re-layouts, doc_backward(): grad_full = skew_pull(score_wide)[0].astype(jnp.bfloat16)  55.6 us
    slice x4, local copies, waits for them, and re-layouts, skew_rows(): middle = flat[..., length - 1:length - 1 + length * (2 * length - 2)]  51.4 us
    dot_general x16, matrix products, dot_right(): lax.dot_general(left_op, right_op, (((1,), (1,)), ((), ())), preferred_el...  46.2 us
  transfers between devices with their start and end apart: 17, of which 5 were waited for; matrix products, arithmetic and copies ran while one was open for 29% of the time, Pallas kernels for 0%

commit v1 on v0

v1 whole, which is shorter than its diff:
```python
import jax
import jax.numpy as jnp
import ml_dtypes
import numpy as np
from jax import lax
from jax.experimental import pallas as pl
from jax.experimental.pallas import tpu as pltpu
from jax.sharding import PartitionSpec as P

DH = 64
PAIR = 2 * DH
ROWS = 256
NEG = -1e30


def nt(left_op, right_op):
    return lax.dot_general(
        left_op, right_op, (((1,), (1,)), ((), ())), preferred_element_type=jnp.float32
    )


def nn(left_op, right_op):
    return jnp.dot(left_op, right_op, preferred_element_type=jnp.float32)


def lane_ids(rows):
    return lax.broadcasted_iota(jnp.int32, (rows, PAIR), 1)


def attend_forward_body(
    len_ref, rank_col, rank_row, live_row, seg_hot, proj_c, proj_q, key_ref, value_ref, rel_ref,
    bias_ref, embed_ref, vec_c, vec_q, prob_ref, mask_scr, ext_scr,
):
    seq_len = key_ref.shape[0]
    blocks = seq_len // ROWS
    wide = seq_len + ROWS

    @pl.when(pl.program_id(1) == 0)
    def _():
        length = len_ref[pl.program_id(0)]
        for block in range(blocks):
            rows = pl.ds(block * ROWS, ROWS)
            place_j = lax.broadcasted_iota(jnp.int32, (ROWS, seq_len), 1)
            place_i = lax.broadcasted_iota(jnp.int32, (ROWS, seq_len), 0) + block * ROWS
            visible = (place_j < length) & (
                (live_row[...] == 0) | (rank_row[...] < rank_col[rows, :])
            )
            diagonal = place_i == place_j
            mask_scr[0, rows, :] = jnp.where(visible | diagonal, 0.0, NEG)
            mask_scr[1, rows, :] = jnp.where(visible & jnp.logical_not(diagonal), 0.0, NEG)

    ext_scr[:, :PAIR] = key_ref[...]
    ext_scr[:, PAIR:] = seg_hot[...]
    lane = lane_ids(ROWS)
    diff = embed_ref[0:1, :] - embed_ref[1:2, :]
    for stream in range(2):
        proj_ref = (proj_c, proj_q)[stream]
        vec_ref = (vec_c, vec_q)[stream]
        for block in range(blocks):
            rows = pl.ds(block * ROWS, ROWS)
            proj = proj_ref[rows, :]
            query_c = ((proj + bias_ref[0:1, :]) * 0.125).astype(jnp.bfloat16)
            query_p = ((proj + bias_ref[1:2, :]) * 0.125).astype(jnp.bfloat16)
            seg_gap = (proj + bias_ref[2:3, :]) * (diff * 0.125)
            hot = seg_hot[rows, :].astype(jnp.float32)
            window = rel_ref[pl.ds(seq_len - (block + 1) * ROWS, wide), :]
            vec_pair = None
            for head in range(2):
                own = (lane >= DH) if head else (lane < DH)
                zero = jnp.zeros((), jnp.bfloat16)
                gap = jnp.sum(jnp.where(own, seg_gap, 0.0), axis=1, keepdims=True)
                gap_high = gap.astype(jnp.bfloat16).astype(jnp.float32)
                seg_part = (jnp.where(lane < 4, gap_high, gap - gap_high) * hot).astype(jnp.bfloat16)
                left = jnp.concatenate([jnp.where(own, query_c, zero), seg_part], axis=1)
                scores = nt(left, ext_scr[...])
                table = nt(jnp.where(own, query_p, zero), window)
                table = pltpu.roll(table, 1, 1, stride=1, stride_axis=0)
                scores = scores + table[:, ROWS:] + mask_scr[stream, rows, :]
                top = jnp.max(scores, axis=1, keepdims=True)
                terms = jnp.exp(scores - top)
                total = jnp.sum(terms, axis=1, keepdims=True)
                prob = (terms * (1.0 / total)).astype(jnp.bfloat16)
                prob_ref[stream, head, rows, :] = prob
                part = nn(prob, value_ref[...])
                vec_pair = part if head == 0 else jnp.where(own, part, vec_pair)
            vec_ref[rows, :] = vec_pair.astype(jnp.bfloat16)


def attend_forward(lengths, rank_col, rank_row, live_row, seg_hot, proj_c, proj_q, keys, values, rel_keys, bias, embed):
    docs, seq_len, width = proj_c.shape
    pairs = width // PAIR
    per_doc = lambda d, p, *_: (d, 0, 0)
    per_pair = lambda d, p, *_: (d, 0, p)
    shared = lambda d, p, *_: (0, p)
    tile = pl.BlockSpec((None, seq_len, PAIR), per_pair)
    return pl.pallas_call(
        attend_forward_body,
        out_shape=(
            jax.ShapeDtypeStruct((docs, seq_len, width), jnp.bfloat16),
            jax.ShapeDtypeStruct((docs, seq_len, width), jnp.bfloat16),
            jax.ShapeDtypeStruct((docs, pairs, 2, 2, seq_len, seq_len), jnp.bfloat16),
        ),
        grid_spec=pltpu.PrefetchScalarGridSpec(
            num_scalar_prefetch=1,
            grid=(docs, pairs),
            in_specs=[
                pl.BlockSpec((None, seq_len, 1), per_doc),
                pl.BlockSpec((None, 1, seq_len), per_doc),
                pl.BlockSpec((None, 1, seq_len), per_doc),
                pl.BlockSpec((None, seq_len, PAIR), per_doc),
                tile, tile, tile, tile,
                pl.BlockSpec((2 * seq_len, PAIR), shared),
                pl.BlockSpec((3, PAIR), shared),
                pl.BlockSpec((2, PAIR), shared),
            ],
            out_specs=[
                tile, tile,
                pl.BlockSpec((None, None, 2, 2, seq_len, seq_len), lambda d, p, *_: (d, p, 0, 0, 0, 0)),
            ],
            scratch_shapes=[
                pltpu.VMEM((2, seq_len, seq_len), jnp.float32),
                pltpu.VMEM((seq_len, 2 * PAIR), jnp.bfloat16),
            ],
        ),
        name="attend_forward",
    )(lengths, rank_col, rank_row, live_row, seg_hot, proj_c, proj_q, keys, values, rel_keys, bias, embed)


def shear_left(value_in):
    rows, wide = value_in.shape
    pack = 16
    groups = []
    for group in range(rows // pack):
        piece = value_in[group * pack : (group + 1) * pack]
        groups.append(pltpu.roll(piece, wide - 1 - group * pack, 1))
    moved = jnp.concatenate(groups, axis=0)
    place = lax.broadcasted_iota(jnp.int32, (rows, wide), 0)
    step = 1
    while step < pack:
        moved = jnp.where((place & step) != 0, pltpu.roll(moved, wide - step, 1), moved)
        step = step * 2
    return moved


def attend_backward_body(
    seg_hot, proj_c, proj_q, key_ref, value_ref, rel_ref, bias_ref, embed_ref, vec_c, vec_q,
    grad_c, grad_q, prob_ref, gproj_c, gproj_q, gkey_ref, gvalue_ref, grel_ref, small_ref,
    ext_scr, key_acc, value_acc, rel_acc,
):
    seq_len = key_ref.shape[0]
    blocks = seq_len // ROWS
    wide = seq_len + ROWS
    ext_scr[:, :PAIR] = (key_ref[...].astype(jnp.float32) * 0.125).astype(jnp.bfloat16)
    ext_scr[:, PAIR:] = (seg_hot[...].astype(jnp.float32) * 0.125).astype(jnp.bfloat16)
    key_acc[...] = jnp.zeros_like(key_acc)
    value_acc[...] = jnp.zeros_like(value_acc)
    rel_acc[...] = jnp.zeros_like(rel_acc)
    lane = lane_ids(ROWS)
    first = lane < DH
    sums = [jnp.zeros((1, PAIR), jnp.float32) for _ in range(5)]
    for stream in range(2):
        proj_ref = (proj_c, proj_q)[stream]
        vec_ref = (vec_c, vec_q)[stream]
        grad_ref = (grad_c, grad_q)[stream]
        gproj_ref = (gproj_c, gproj_q)[stream]
        for block in range(blocks):
            rows = pl.ds(block * ROWS, ROWS)
            start = seq_len - (block + 1) * ROWS
            proj = proj_ref[rows, :]
            query_ct = jnp.transpose(((proj + bias_ref[0:1, :]) * 0.125).astype(jnp.bfloat16))
            query_pt = jnp.transpose(((proj + bias_ref[1:2, :]) * 0.125).astype(jnp.bfloat16))
            query_s = proj + bias_ref[2:3, :]
            hot = jnp.where(lane < 4, seg_hot[rows, :].astype(jnp.float32), 0.0)
            grad = grad_ref[rows, :]
            grad_t = jnp.transpose(grad)
            inner = grad.astype(jnp.float32) * vec_ref[rows, :].astype(jnp.float32)
            window = (rel_ref[pl.ds(start, wide), :].astype(jnp.float32) * 0.125).astype(jnp.bfloat16)
            parts = []
            for head in range(2):
                own = (lane >= DH) if head else first
                low, high = head * DH, (head + 1) * DH
                prob = prob_ref[stream, head, rows, :]
                grad_prob = nt(jnp.where(own, grad, jnp.zeros((), jnp.bfloat16)), value_ref[...])
                row_inner = jnp.sum(jnp.where(own, inner, 0.0), axis=1, keepdims=True)
                gscore = (prob.astype(jnp.float32) * (grad_prob - row_inner)).astype(jnp.bfloat16)
                value_acc[low:high, :] += nn(grad_t[low:high, :], prob)
                key_acc[low:high, :] += nn(query_ct[low:high, :], gscore)
                both = nn(gscore, ext_scr[...])
                table = jnp.concatenate([jnp.zeros((ROWS, ROWS), jnp.bfloat16), gscore], axis=1)
                table = shear_left(table)
                gpos = nn(table, window)
                rel_acc[low:high, start : start + wide] += nn(query_pt[low:high, :], table)
                tail = both[:, PAIR:]
                tail = jnp.where(lane < 4, tail, 0.0)
                g_same = jnp.sum(tail * hot, axis=1, keepdims=True)
                g_other = jnp.sum(tail, axis=1, keepdims=True) - g_same
                parts.append((both[:, :PAIR], gpos, g_same, g_other))
            g_content = jnp.where(first, parts[0][0], parts[1][0])
            g_position = jnp.where(first, parts[0][1], parts[1][1])
            g_same = jnp.where(first, parts[0][2], parts[1][2])
            g_other = jnp.where(first, parts[0][3], parts[1][3])
            g_segment = g_same * embed_ref[0:1, :] + g_other * embed_ref[1:2, :]
            gproj_ref[rows, :] = (g_content + g_position + g_segment).astype(jnp.bfloat16)
            terms = (g_content, g_position, g_segment, g_same * query_s, g_other * query_s)
            sums = [kept + jnp.sum(term, axis=0, keepdims=True) for kept, term in zip(sums, terms)]
    gkey_ref[...] = jnp.transpose(key_acc[...]).astype(jnp.bfloat16)
    gvalue_ref[...] = jnp.transpose(value_acc[...]).astype(jnp.bfloat16)
    grel_ref[...] = rel_acc[...].astype(jnp.bfloat16)
    small_ref[...] = jnp.concatenate(sums + [jnp.zeros((3, PAIR), jnp.float32)], axis=0)


def attend_backward(seg_hot, proj_c, proj_q, keys, values, rel_keys, bias, embed, vec_c, vec_q, grad_c, grad_q, prob):
    docs, seq_len, width = proj_c.shape
    pairs = width // PAIR
    per_doc = lambda d, p: (d, 0, 0)
    per_pair = lambda d, p: (d, 0, p)
    shared = lambda d, p: (0, p)
    tile = pl.BlockSpec((None, seq_len, PAIR), per_pair)
    low = jax.ShapeDtypeStruct((docs, seq_len, width), jnp.bfloat16)
    return pl.pallas_call(
        attend_backward_body,
        out_shape=(
            low, low, low, low,
            jax.ShapeDtypeStruct((docs, width, 2 * seq_len), jnp.bfloat16),
            jax.ShapeDtypeStruct((docs, 8, width), jnp.float32),
        ),
        grid_spec=pltpu.PrefetchScalarGridSpec(
            num_scalar_prefetch=0,
            grid=(docs, pairs),
            in_specs=[
                pl.BlockSpec((None, seq_len, PAIR), per_doc),
                tile, tile, tile, tile,
                pl.BlockSpec((2 * seq_len, PAIR), shared),
                pl.BlockSpec((3, PAIR), shared),
                pl.BlockSpec((2, PAIR), shared),
                tile, tile, tile, tile,
                pl.BlockSpec((None, None, 2, 2, seq_len, seq_len), lambda d, p: (d, p, 0, 0, 0, 0)),
            ],
            out_specs=[
                tile, tile, tile, tile,
                pl.BlockSpec((None, PAIR, 2 * seq_len), lambda d, p: (d, p, 0)),
                pl.BlockSpec((None, 8, PAIR), per_pair),
            ],
            scratch_shapes=[
                pltpu.VMEM((seq_len, 2 * PAIR), jnp.bfloat16),
                pltpu.VMEM((PAIR, seq_len), jnp.float32),
                pltpu.VMEM((PAIR, seq_len), jnp.float32),
                pltpu.VMEM((PAIR, 2 * seq_len), jnp.float32),
            ],
        ),
        name="attend_backward",
    )(seg_hot, proj_c, proj_q, keys, values, rel_keys, bias, embed, vec_c, vec_q, grad_c, grad_q, prob)


epsilon = 1e-06


def layer_norm(value_in, gain, shift):
    center = value_in - jnp.mean(value_in, axis=-1, keepdims=True)
    spread = jnp.mean(center * center, axis=-1, keepdims=True)
    return center * lax.rsqrt(spread + epsilon) * gain + shift


def gelu_tanh(value_in):
    return jax.nn.gelu(value_in, approximate=True)


def position_table(seq_len, width):
    distance = seq_len - 1.0 - np.arange(2 * seq_len - 1, dtype=np.float32)
    freq_exp = np.arange(0, width, 2).astype(np.float32) / np.float32(width)
    inverse = np.float32(1.0) / np.float32(10000.0) ** freq_exp
    angle = (distance[:, None] * inverse[None, :]).astype(np.float32)
    table = np.concatenate([np.sin(angle), np.cos(angle)], axis=1)
    table = np.concatenate([table, np.zeros((1, width), np.float32)], axis=0)
    return table.astype(ml_dtypes.bfloat16)


def dot_left(left_op, right_op):
    return lax.dot_general(
        left_op, right_op, (((0,), (0,)), ((), ())), preferred_element_type=jnp.float32
    )


def on_device(
    content_in,
    query_in,
    doc_lengths,
    order_ranks,
    segment_ids,
    target_flags,
    query_weight,
    key_weight,
    value_weight,
    out_weight,
    rel_weight,
    content_bias,
    position_bias,
    segment_bias,
    segment_embed,
    first_gain,
    first_shift,
    up_weight,
    up_bias,
    down_weight,
    down_bias,
    second_gain,
    second_shift,
    content_cot,
    query_cot,
):
    docs_dev, half, width = content_in.shape
    seq_len = order_ranks.shape[1]
    mine = lax.axis_index("mp")
    wide_f = lambda value: value.astype(jnp.float32)
    low_f = lambda value: value.astype(jnp.bfloat16)

    def swap(value):
        return lax.ppermute(value, "mp", [(0, 1), (1, 0)])

    def gather_doc(value):
        keep = lax.dynamic_index_in_dim(value, mine, 0, keepdims=False)
        came = swap(lax.dynamic_index_in_dim(value, 1 - mine, 0, keepdims=False))
        head = jnp.where(mine == 0, keep, came)
        tail = jnp.where(mine == 0, came, keep)
        return jnp.concatenate([head, tail], axis=0)

    def return_doc(value):
        pair = value.reshape(2, half, width)
        keep = lax.dynamic_index_in_dim(pair, mine, 0, keepdims=False)
        came = swap(lax.dynamic_index_in_dim(pair, 1 - mine, 0, keepdims=False))
        return jnp.stack([jnp.where(mine == 0, keep, came), jnp.where(mine == 0, came, keep)])

    def both(value, axis):
        return jnp.concatenate([value, swap(value)], axis=axis)

    content = gather_doc(content_in)
    query = gather_doc(query_in)
    query_use = both(query_weight, 1)
    key_use = both(key_weight, 1)
    value_use = both(value_weight, 1)
    rel_use = both(rel_weight, 1)
    vectors = both(
        jnp.concatenate(
            [
                wide_f(content_bias)[None],
                wide_f(position_bias)[None],
                wide_f(segment_bias)[None],
                wide_f(segment_embed),
            ],
            axis=0,
        ),
        1,
    )
    bias, embed = vectors[:3], vectors[3:]
    out_use = both(out_weight, 0)
    up_use = both(up_weight, 1)
    down_use = both(down_weight, 0)
    up_bias_use = both(wide_f(up_bias)[None], 1)
    cot = jnp.concatenate([gather_doc(content_cot), gather_doc(query_cot)], axis=0)

    lengths = lax.dynamic_slice_in_dim(doc_lengths, mine, 1, 0)
    ranks = lax.dynamic_slice_in_dim(order_ranks, mine, 1, 0)
    segments = lax.dynamic_slice_in_dim(segment_ids, mine, 1, 0)
    targets = lax.dynamic_slice_in_dim(target_flags, mine, 1, 0)
    live = targets * (jnp.arange(seq_len) >= 2).astype(jnp.int32)[None]
    lanes = jnp.arange(PAIR)
    seg_hot = low_f((segments[:, :, None] == lanes % 4) & (lanes < 8))
    table = jnp.asarray(position_table(seq_len, width))
    rel_keys = low_f(nn(table, rel_use))
    proj_c = nn(content, query_use)[None]
    proj_q = nn(query, query_use)[None]
    keys = low_f(nn(content, key_use))[None]
    values = low_f(nn(content, value_use))[None]
    vec_c, vec_q, prob = attend_forward(
        lengths, ranks[:, :, None], ranks[:, None, :], live[:, None, :], seg_hot,
        proj_c, proj_q, keys, values, rel_keys, bias, embed,
    )
    vec = jnp.concatenate([vec_c[0], vec_q[0]], axis=0)
    resid = jnp.concatenate([content, query], axis=0)
    gain_first, shift_first = wide_f(first_gain), wide_f(first_shift)
    gain_second, shift_second = wide_f(second_gain), wide_f(second_shift)
    pre1 = nn(vec, out_use) + wide_f(resid)
    first = low_f(layer_norm(pre1, gain_first, shift_first))
    hidden = nn(first, up_use) + up_bias_use
    act = low_f(gelu_tanh(hidden))
    pre2 = wide_f(first) + nn(act, down_use) + wide_f(down_bias)
    norm2, pull2 = jax.vjp(layer_norm, pre2, gain_second, shift_second)
    out_rows = low_f(norm2)
    grad_pre2, g_gain2, g_shift2 = pull2(wide_f(cot))
    g_down_bias = jnp.sum(grad_pre2, axis=0)
    grad_down = low_f(grad_pre2)
    grad_act = nt(grad_down, down_use)
    grad_hidden = low_f(jax.vjp(gelu_tanh, hidden)[1](grad_act)[0])
    g_up_bias = jnp.sum(wide_f(grad_hidden), axis=0)
    back = nt(grad_hidden, up_use)
    grad_pre1, g_gain1, g_shift1 = jax.vjp(layer_norm, pre1, gain_first, shift_first)[1](back + grad_pre2)
    grad_mixed = low_f(grad_pre1)
    grad_vec = low_f(nt(grad_mixed, out_use))

    ff = up_weight.shape[1]
    cols = query_weight.shape[1]

    def merge(left, right, axis):
        if axis == 1:
            split = right.shape[1] // 2
            other = low_f(dot_left(left, right[:, split:]))
            own = dot_left(left, right[:, :split])
        else:
            split = left.shape[1] // 2
            other = low_f(dot_left(left[:, split:], right))
            own = dot_left(left[:, :split], right)
        return low_f(own + wide_f(swap(other)))

    g_down = lax.psum(merge(act, grad_down, 0), "dp")
    g_up = lax.psum(merge(first, grad_hidden, 1), "dp")
    g_out = lax.psum(merge(vec, grad_mixed, 0), "dp")

    gproj_c, gproj_q, gkeys, gvalues, grel, small = attend_backward(
        seg_hot, proj_c, proj_q, keys, values, rel_keys, bias, embed, vec_c, vec_q,
        grad_vec[None, :seq_len], grad_vec[None, seq_len:], prob,
    )
    gproj = jnp.concatenate([gproj_c[0], gproj_q[0]], axis=0)
    g_query = lax.psum(merge(resid, gproj, 1), "dp")
    g_key = lax.psum(merge(content, gkeys[0], 1), "dp")
    g_value = lax.psum(merge(content, gvalues[0], 1), "dp")
    g_rel = lax.psum(merge(table, jnp.transpose(grel[0]), 1), "dp")
    content_grad = low_f(
        nt(gproj_c[0], query_use) + nt(gkeys[0], key_use) + nt(gvalues[0], value_use) + grad_pre1[:seq_len]
    )
    query_grad = low_f(nt(gproj_q[0], query_use) + grad_pre1[seq_len:])

    small = small[0]
    pack_split = jnp.concatenate([small[:5].reshape(-1, 2, cols).transpose(1, 0, 2).reshape(2, -1), g_up_bias.reshape(2, ff)], axis=1)
    pack_same = jnp.stack([g_gain1, g_shift1, g_gain2, g_shift2, g_down_bias]).reshape(-1)
    got = swap(jnp.concatenate([pack_split[1], pack_same]))
    tiny = lax.psum(jnp.concatenate([pack_split[0], pack_same]) + got, "dp")
    at = 5 * cols
    split_part = tiny[:at].reshape(5, cols)
    same_part = tiny[at + ff :].reshape(5, width)
    return (
        return_doc(out_rows[:seq_len]),
        return_doc(out_rows[seq_len:]),
        return_doc(content_grad),
        return_doc(query_grad),
        wide_f(g_query),
        wide_f(g_key),
        wide_f(g_value),
        wide_f(g_out),
        wide_f(g_rel),
        split_part[0],
        split_part[1],
        split_part[2],
        split_part[3:5],
        same_part[0],
        same_part[1],
        wide_f(g_up),
        tiny[at : at + ff],
        wide_f(g_down),
        same_part[4],
        same_part[2],
        same_part[3],
    )


def solution(mesh):
    placed = (
        P("dp", "mp", None),
        P("dp", "mp", None),
        P("dp"),
        P("dp", None),
        P("dp", None),
        P("dp", None),
        P(None, "mp"),
        P(None, "mp"),
        P(None, "mp"),
        P("mp", None),
        P(None, "mp"),
        P("mp"),
        P("mp"),
        P("mp"),
        P(None, "mp"),
        P(),
        P(),
        P(None, "mp"),
        P("mp"),
        P("mp", None),
        P(),
        P(),
        P(),
        P("dp", "mp", None),
        P("dp", "mp", None),
    )
    return jax.shard_map(
        on_device,
        mesh=mesh,
        in_specs=placed,
        out_specs=(
            P("dp", "mp", None),
            P("dp", "mp", None),
            P("dp", "mp", None),
            P("dp", "mp", None),
            P(None, "mp"),
            P(None, "mp"),
            P(None, "mp"),
            P("mp", None),
            P(None, "mp"),
            P("mp"),
            P("mp"),
            P("mp"),
            P(None, "mp"),
            P(),
            P(),
            P(None, "mp"),
            P("mp"),
            P("mp", None),
            P(),
            P(),
            P(),
        ),
        check_vma=False,
    )
```

time: 1570 us -> 531 us (0.34)
  local copies, waits for them, and re-layouts: 658 us -> 50.4 us
  waiting for transfers between devices: 363 us -> 140 us
  matrix products: 314 us -> 96.2 us
  Pallas kernels: 0 us -> 91.8 us
  blocking collectives: 125 us -> 81.9 us
  other arithmetic: 78.7 us -> 41.5 us
    unnamed x497 -> x192, local copies, waits for them, and re-layouts: 292 us -> 15.5 us
    psum x1, waiting for transfers between devices: 319 us -> 139 us  [on_device(): g_query = lax.psum(merge(resid, gproj, 1), 'dp')]
    dot_general x78 -> x15, matrix products: 229 us -> 63.9 us  [the longest x7 34.3 us: nt(): lax.dot_general(left_op, right_op, (((1,), (1,)), ((), ())), preferred_el...]
    reshape x13 -> x7, local copies, waits for them, and re-layouts: 164 us -> 6.53 us  [the longest x4 3.12 us: layer_norm(): return center * lax.rsqrt(spread + epsilon) * gain + shift]
    pallas_call x0 -> x2, Pallas kernels: none -> 91.8 us  [the longest x1 56.1 us: attend_backward(): pl.pallas_call(attend_backward_body, out_shape=(low, low, low, low, jax.S...]
    slice x22 -> x5, local copies, waits for them, and re-layouts: 92.2 us -> 3.86 us  [the longest x1 1.47 us: on_device(): out_rows[seq_len:]]
    convert_element_type x4 -> x0, local copies, waits for them, and re-layouts: 55.6 us -> none  [doc_backward(): grad_full = skew_pull(score_wide)[0].astype(jnp.bfloat16)]
    pad x8 -> x0, local copies, waits for them, and re-layouts: 51.9 us -> none  [the longest x4 34.2 us: skew_rows(): middle = flat[..., length - 1:length - 1 + length * (2 * length - 2)]]
  transfers between devices with their start and end apart: 17 -> 26, of which waited for: 5 -> 2; matrix products, arithmetic and copies ran while one was open for 29% -> 20% of each run, Pallas kernels for 0% -> 7%
where the time goes in v1:
time: 531 us; the launch traced here: 525 us
  waiting for transfers between devices  140 us (26%)
  matrix products  96.2 us (18%)
  Pallas kernels  91.8 us (17%)
  blocking collectives  81.9 us (15%)
  local copies, waits for them, and re-layouts  50.4 us (9%)
  other arithmetic  41.5 us (8%)
  between operations  15.7 us (3%)
  starting transfers between devices  7.4 us (1%)
    psum x1, waiting for transfers between devices, on_device(): g_query = lax.psum(merge(resid, gproj, 1), 'dp')  139 us
    psum x1, blocking collectives, on_device(): tiny = lax.psum(jnp.concatenate([pack_split[0], pack_same]) + got, 'dp')  81.9 us
    pallas_call x1, Pallas kernels, attend_backward(): pl.pallas_call(attend_backward_body, out_shape=(low, low, low, low, jax.S...  56.1 us
    pallas_call x1, Pallas kernels, attend_forward(): pl.pallas_call(attend_forward_body, out_shape=(jax.ShapeDtypeStruct((docs...  35.6 us
    dot_general x7, matrix products, nt(): lax.dot_general(left_op, right_op, (((1,), (1,)), ((), ())), preferred_el...  34.3 us
    dot_general x14, matrix products, dot_left(): lax.dot_general(left_op, right_op, (((0,), (0,)), ((), ())), preferred_el...  32.4 us
    dot_general x8, matrix products, nn(): return jnp.dot(left_op, right_op, preferred_element_type=jnp.float32)  29.6 us
    convert_element_type x12, other arithmetic, on_device(): wide_f = lambda value: value.astype(jnp.float32)  16.1 us
  transfers between devices with their start and end apart: 26, of which 2 were waited for; matrix products, arithmetic and copies ran while one was open for 20% of the time, Pallas kernels for 7%

profile of v1, /device:TPU:0, one launch (start us, length us, event | category | flops | bytes accessed | tf_op | source)
XLA Modules:
  0.0 525.0 jit_solution(11916940869307889824)
XLA Ops:
  14.0 2.0 constant_dynamic-update-slice_fusion.1
  16.0 2.0 constant_dynamic-update-slice_fusion.3
  22.4 3.2 constant_dynamic-update-slice_fusion.9
  25.7 3.3 constant_dynamic-update-slice_fusion.11
  50.5 1.9 convolution_bitcast_fusion.1.proj_c
  52.4 2.0 convolution_bitcast_fusion.proj_q
  54.4 2.6 fusion.23.rel_ref
  57.0 35.6 %attend_forward.1 = (bf16[1,512,768]{2,1,0:T(8,128)(2,1)}, bf16[1,512,768]{2,1,0:T(8,128)(2,1)}, bf16[1,6,2,2,512,512]{5,4,3,2,1,0:T(8,128)(2,1)}) custom-call(s32[1]{0:T(128)} %dynamic_slice.63.len_ref, s32[1,512,1]{2,1,0:T(8,128)} %copy.50.rank_col, s32[1,1,512]{2,1,0:T(1,128)} %get-tuple-element.90.rank_row, s32[1,1,512]{2,1,0:T(1,128)} %get-tuple-element.101.live_row, ...), custom_call_target="tpu_custom_call" | custom-call | tf_op jit(solution)/shard_map/attend_forward/pallas_call | solution.py:96
  93.5 4.0 fusion.97
  98.8 2.6 constant_dynamic-update-slice_fusion.8
  101.4 10.6 %multiply_convert_fusion = (bf16[1024,3072]{1,0:T(8,128)(2,1)S(1)}, f32[1024,3072]{1,0:T(8,128)}) fusion(f32[3072]{0:T(1024)S(1)} %bitcast.170, bf16[1024,768]{1,0:T(8,128)(2,1)S(1)} %add_convert_fusion.3, bf16[768,3072]{1,0:T(8,128)(2,1)S(1)} %constant_dynamic-update-slice_fusion.8), kind=kOutput, calls=%fused_computation.10 | convolution fusion | flops 4863295488 | bytes 25178112 | tf_op jit(solution)/shard_map/dot_general | solution.py:23
  112.1 3.6 constant_dynamic-update-slice_fusion.10
  115.7 5.3 %fusion.98 = (f32[1024]{0:T(1024)S(1)}, f32[1024,768]{1,0:T(8,128)S(1)}) fusion(f32[768]{0:T(1024)S(1)} %copy-done.58, bf16[1024,3072]{1,0:T(8,128)(2,1)S(1)} %get-tuple-element.94, bf16[3072,768]{1,0:T(8,128)(2,1)S(1)} %constant_dynamic-update-slice_fusion.10, bf16[1024,768]{1,0:T(8,128)(2,1)S(1)} %add_convert_fusion.3), kind=kOutput, calls=%fused_computation.206 | convolution fusion | flops 4834982912 | bytes 15735808 | tf_op jit(solution)/shard_map/dot_general | solution.py:23
  121.7 3.1 fusion.10
  124.8 3.6 fusion.93
  128.8 17.5 %convert_reduce_fusion = (f32[3072]{0:T(1024)}, bf16[1024,3072]{1,0:T(8,128)(2,1)}) fusion(f32[1024,3072]{1,0:T(8,128)} %get-tuple-element.95, f32[3072]{0:T(1024)S(1)} %bitcast.171, bf16[1024,768]{1,0:T(8,128)(2,1)S(1)} %get-tuple-element.60, bf16[3072,768]{1,0:T(8,128)(2,1)S(1)} %constant_dynamic-update-slice_fusion.10), kind=kOutput, calls=%fused_computation.9 | convolution fusion | flops 4904186880 | bytes 25190400 | tf_op jit(solution)/shard_map/dot_general | solution.py:17
  146.3 10.3 %multiply_reduce_fusion = (f32[768]{0:T(1024)}, f32[1024]{0:T(1024)S(1)}, f32[768]{0:T(1024)}, f32[1024,768]{1,0:T(8,128)S(1)}) fusion(f32[1024,768]{1,0:T(8,128)S(1)} %get-tuple-element.93, f32[1024]{0:T(1024)S(1)} %fusion.68, f32[1024]{0:T(1024)S(1)} %broadcast_multiply_fusion.1, f32[768]{0:T(1024)S(1)} %copy-done.53, ...), kind=kOutput, calls=%fused_computation.30 | convolution fusion | flops 4839699456 | bytes 20472832 | tf_op jit(solution)/shard_map/dot_general | solution.py:17
  162.7 4.0 convolution_convert_fusion.1
  166.7 4.0 convolution_convert_fusion
  171.9 56.1 %attend_backward.1 = (bf16[1,512,768]{2,1,0:T(8,128)(2,1)}, bf16[1,512,768]{2,1,0:T(8,128)(2,1)}, bf16[1,512,768]{2,1,0:T(8,128)(2,1)}, bf16[1,512,768]{2,1,0:T(...) custom-call(bf16[1,512,128]{2,1,0:T(8,128)(2,1)} %and_convert_fusion.seg_hot, ...), custom_call_target="tpu_custom_call" | custom-call | tf_op jit(solution)/shard_map/attend_backward/pallas_call | solution.py:220
  228.1 1.9 convolution_convert_fusion.9
  230.6 2.8 fusion.29
  238.1 1.8 add_convert_fusion.5
  245.3 4.0 add_convert_fusion
  249.4 4.2 add_convert_fusion.1
  267.8 2.5 fusion.21
  276.1 81.9 %psum.61 = f32[7296]{0:T(1024)S(1)} all-reduce(f32[7296]{0:T(1024)S(1)} %fusion.63), channel_id=1, replica_groups=mesh['dp'=16,'mp'=2] {'dp'}, use_global_device_ids=true, to_apply=%region_19.20 | all-reduce | flops 7296 | bytes 58368 | tf_op jit(solution)/shard_map/psum | solution.py:436
  365.6 138.9 %all-reduce.3.cloned.1.call-done = (bf16[768,384]{1,0:T(8,128)(2,1)}, bf16[768,384]{1,0:T(8,128)(2,1)}, bf16[768,384]{1,0:T(8,128)(2,1)}, bf16[384,768]{1,0:T(8,...) async-done(((bf16[768,384]{1,0:T(8,128)(2,1)}, bf16[768,384]{1,0:T(8,128)(2,1)}, bf16[768,384]{1,0:T(8,128)(2,1)}, ...) | async-done | bytes 7667728 | tf_op jit(solution)/shard_map/psum | solution.py:423
  504.5 2.2 convert_element_type.187
  506.8 2.2 convert_element_type.191
  512.3 2.8 convert_element_type.209
  515.1 2.5 convert_element_type.213
  (338 shorter events, 84.2 us)
Async XLA Ops:
  7.2 497.3 %all-reduce.3.cloned.1.call-start = ((), (), s32[]{:S(2)}) async-start(), calls=%async_computation | async-start | bytes 15335424 | tf_op jit(solution)/shard_map/psum | solution.py:423
  8.7 26.2 %collective-permute-start.9 = (f32[1,1536]{1,0:T(1,128)}, f32[1,1536]{1,0:T(1,128)}, u32[]{:S(2)}, u32[]{:S(2)}) collective-permute-start(f32[1,1536]{1,0:T(1,128)} %reshape.287), channel_id=1, source_target_pairs={{0,1},{1,0},{2,3},{3,2},{4,5},{5,4},{6,7},{7,6},{8,9},{9,8},{10,11... | collective-permute-start | bytes 18440 | tf_op jit(solution)/shard_map/ppermute | solution.py:318
  11.9 24.4 %collective-permute-start.6 = (f32[5,384]{1,0:T(8,128)S(1)}, f32[5,384]{1,0:T(8,128)}, u32[]{:S(2)}, u32[]{:S(2)}) collective-permute-start(f32[5,384]{1,0:T(8,128)S(1)} %maximum_convert_fusion), channel_id=1, source_target_pairs={{0,1},{1,0},{2,3},{3,2},{4,5},{5,4},{6,7},{7,6},{8,9},{9,8},{10,11... | collective-permute-start | bytes 23048 | tf_op jit(solution)/shard_map/ppermute | solution.py:318
  12.0 37.3 %collective-permute-start.1 = (bf16[768,384]{1,0:T(8,128)(2,1)}, bf16[768,384]{1,0:T(8,128)(2,1)}, u32[]{:S(2)}, u32[]{:S(2)}) collective-permute-start(bf16[768,384]{1,0:T(8,128)(2,1)} %param.32), channel_id=1, source_target_pairs={{0,1},{1,0},{2,3},{3,2},{4,5},{5,4},{6,7},{7,6},{8,9},{9,8},{10,11... | collective-permute-start | bytes 1769480 | tf_op jit(solution)/shard_map/ppermute | solution.py:318
  12.4 30.5 %collective-permute-start.3 = (bf16[768,384]{1,0:T(8,128)(2,1)}, bf16[768,384]{1,0:T(8,128)(2,1)}, u32[]{:S(2)}, u32[]{:S(2)}) collective-permute-start(bf16[768,384]{1,0:T(8,128)(2,1)} %param.33), channel_id=1, source_target_pairs={{0,1},{1,0},{2,3},{3,2},{4,5},{5,4},{6,7},{7,6},{8,9},{9,8},{10,11... | collective-permute-start | bytes 1769480 | tf_op jit(solution)/shard_map/ppermute | solution.py:318
  12.5 31.9 %collective-permute-start.4 = (bf16[768,384]{1,0:T(8,128)(2,1)}, bf16[768,384]{1,0:T(8,128)(2,1)}, u32[]{:S(2)}, u32[]{:S(2)}) collective-permute-start(bf16[768,384]{1,0:T(8,128)(2,1)} %param.34), channel_id=1, source_target_pairs={{0,1},{1,0},{2,3},{3,2},{4,5},{5,4},{6,7},{7,6},{8,9},{9,8},{10,11... | collective-permute-start | bytes 1769480 | tf_op jit(solution)/shard_map/ppermute | solution.py:318
  34.8 4.4 collective-permute-start.14
  36.2 3.2 collective-permute-start.13
  39.3 1.9 collective-permute-start.2
  39.4 3.0 collective-permute-start
  41.2 51.4 %collective-permute-start.7 = (bf16[384,768]{1,0:T(8,128)(2,1)}, bf16[384,768]{1,0:T(8,128)(2,1)S(1)}, u32[]{:S(2)}, u32[]{:S(2)}) collective-permute-start(bf16[384,768]{1,0:T(8,128)(2,1)} %param.35), channel_id=1, source_target_pairs={{0,1},{1,0},{2,3},{3,2},{4,5},{5,4},{6,7},{7,6},{8,9},{9,8},{10,11... | collective-permute-start | bytes 1769480 | tf_op jit(solution)/shard_map/ppermute | solution.py:318
  42.4 56.4 %collective-permute-start.8 = (bf16[768,1536]{1,0:T(8,128)(2,1)}, bf16[768,1536]{1,0:T(8,128)(2,1)}, u32[]{:S(2)}, u32[]{:S(2)}) collective-permute-start(bf16[768,1536]{1,0:T(8,128)(2,1)} %param.43), channel_id=1, source_target_pairs={{0,1},{1,0},{2,3},{3,2},{4,5},{5,4},{6,7},{7,6},{8,9},{9,8},{10,11... | collective-permute-start | bytes 7077896 | tf_op jit(solution)/shard_map/ppermute | solution.py:318
  43.0 69.1 %collective-permute-start.10 = (bf16[1536,768]{1,0:T(8,128)(2,1)}, bf16[1536,768]{1,0:T(8,128)(2,1)}, u32[]{:S(2)}, u32[]{:S(2)}) collective-permute-start(bf16[1536,768]{1,0:T(8,128)(2,1)} %param.45), channel_id=1, source_target_pairs={{0,1},{1,0},{2,3},{3,2},{4,5},{5,4},{6,7},{7,6},{8,9},{9,8},{10,11... | collective-permute-start | bytes 7077896 | tf_op jit(solution)/shard_map/ppermute | solution.py:318
  44.4 10.0 %collective-permute-start.5 = (bf16[768,384]{1,0:T(8,128)(2,1)S(1)}, bf16[768,384]{1,0:T(8,128)(2,1)S(1)}, u32[]{:S(2)}, u32[]{:S(2)}) collective-permute-start(bf16[768,384]{1,0:T(8,128)(2,1)S(1)} %copy-done.76), channel_id=1, source_target_pairs={{0,1},{1,0},{2,3},{3,2},{4,5},{5,4},{6,7},{7,6},{8,9},{9,8},{10,11... | collective-permute-start | bytes 1769480 | tf_op jit(solution)/shard_map/ppermute | solution.py:318
  57.0 36.5 %copy-start.38 = (bf16[256,768]{1,0:T(8,128)(2,1)S(1)}, bf16[256,768]{1,0:T(8,128)(2,1)}, u32[]{:S(2)}) copy-start(bf16[256,768]{1,0:T(8,128)(2,1)} %copy-done.37) | copy-start | bytes 1179652
  57.0 36.5 %copy-start.41 = (bf16[256,768]{1,0:T(8,128)(2,1)S(1)}, bf16[256,768]{1,0:T(8,128)(2,1)}, u32[]{:S(2)}) copy-start(bf16[256,768]{1,0:T(8,128)(2,1)} %copy-done.40) | copy-start | bytes 1179652
  98.7 63.9 %copy-start.15 = (bf16[1024,768]{1,0:T(8,128)(2,1)}, bf16[1024,768]{1,0:T(8,128)(2,1)S(1)}, u32[]{:S(2)}) copy-start(bf16[1024,768]{1,0:T(8,128)(2,1)S(1)} %add_convert_fusion.3) | copy-start | bytes 4718596
  128.8 37.9 %copy-start.17 = (bf16[1024,768]{1,0:T(8,128)(2,1)}, bf16[1024,768]{1,0:T(8,128)(2,1)S(1)}, u32[]{:S(2)}) copy-start(bf16[1024,768]{1,0:T(8,128)(2,1)S(1)} %get-tuple-element.60) | copy-start | bytes 4718596
  171.9 56.2 %copy-start.42 = (bf16[256,768]{1,0:T(8,128)(2,1)S(1)}, bf16[256,768]{1,0:T(8,128)(2,1)}, u32[]{:S(2)}) copy-start(bf16[256,768]{1,0:T(8,128)(2,1)} %copy-done.40) | copy-start | bytes 1179652
  230.0 6.1 %collective-permute-start.19 = (bf16[768,384]{1,0:T(8,128)(2,1)S(1)}, bf16[768,384]{1,0:T(8,128)(2,1)S(1)}, u32[]{:S(2)}, u32[]{:S(2)}) collective-permute-start(bf16[768,384]{1,0:T(8,128)(2,1)S(1)} %convolution_convert_fusion.9), channel_id=1, source_target_pairs={{0,1},{1,0},{2,3},{3,2},{4,5},{5,4},{6,7},{7,6},{8,9},{9,8},{10,11... | collective-permute-start | bytes 1769480 | tf_op jit(solution)/shard_map/ppermute | solution.py:318
  230.4 14.5 %collective-permute-start.24 = (bf16[1536,768]{1,0:T(8,128)(2,1)S(1)}, bf16[1536,768]{1,0:T(8,128)(2,1)S(1)}, u32[]{:S(2)}, u32[]{:S(2)}) collective-permute-start(bf16[1536,768]{1,0:T(8,128)(2,1)S(1)} %copy-done.69), channel_id=1, source_target_pairs={{0,1},{1,0},{2,3},{3,2},{4,5},{5,4},{6,7},{7,6},{8,9},{9,8},{10,11... | collective-permute-start | bytes 7077896 | tf_op jit(solution)/shard_map/ppermute | solution.py:318
  233.4 4.5 collective-permute-start.21
  234.5 5.5 %collective-permute-start.18 = (bf16[768,384]{1,0:T(8,128)(2,1)S(1)}, bf16[768,384]{1,0:T(8,128)(2,1)S(1)}, u32[]{:S(2)}, u32[]{:S(2)}) collective-permute-start(bf16[768,384]{1,0:T(8,128)(2,1)S(1)} %convolution_convert_fusion.10), channel_id=1, source_target_pairs={{0,1},{1,0},{2,3},{3,2},{4,5},{5,4},{6,7},{7,6},{8,9},{9,8},{10,11... | collective-permute-start | bytes 1769480 | tf_op jit(solution)/shard_map/ppermute | solution.py:318
  234.7 14.6 %collective-permute-start.23 = (bf16[768,1536]{1,0:T(8,128)(2,1)S(1)}, bf16[768,1536]{1,0:T(8,128)(2,1)S(1)}, u32[]{:S(2)}, u32[]{:S(2)}) collective-permute-start(bf16[768,1536]{1,0:T(8,128)(2,1)S(1)} %copy-done.68), channel_id=1, source_target_pairs={{0,1},{1,0},{2,3},{3,2},{4,5},{5,4},{6,7},{7,6},{8,9},{9,8},{10,11... | collective-permute-start | bytes 7077896 | tf_op jit(solution)/shard_map/ppermute | solution.py:318
  236.1 5.3 %collective-permute-start.20 = (bf16[384,768]{1,0:T(8,128)(2,1)S(1)}, bf16[384,768]{1,0:T(8,128)(2,1)S(1)}, u32[]{:S(2)}, u32[]{:S(2)}) collective-permute-start(bf16[384,768]{1,0:T(8,128)(2,1)S(1)} %copy-done.33), channel_id=1, source_target_pairs={{0,1},{1,0},{2,3},{3,2},{4,5},{5,4},{6,7},{7,6},{8,9},{9,8},{10,11... | collective-permute-start | bytes 1769480 | tf_op jit(solution)/shard_map/ppermute | solution.py:318
  237.9 5.2 collective-permute-start.17
  256.6 103.8 %collective-permute-start.12 = (bf16[256,768]{1,0:T(8,128)(2,1)}, bf16[256,768]{1,0:T(8,128)(2,1)}, u32[]{:S(2)}, u32[]{:S(2)}) collective-permute-start(bf16[256,768]{1,0:T(8,128)(2,1)} %dynamic-slice_bitcast_fusion.4), channel_id=1, source_target_pairs={{0,1},{1,0},{2,3},{3,2},{4,5},{5,4},{6,7},{7,6},{8,9},{9,8},{10,11... | collective-permute-start | bytes 1179656 | tf_op jit(solution)/shard_map/ppermute | solution.py:318
  257.7 104.9 %collective-permute-start.11 = (bf16[256,768]{1,0:T(8,128)(2,1)}, bf16[256,768]{1,0:T(8,128)(2,1)S(1)}, u32[]{:S(2)}, u32[]{:S(2)}) collective-permute-start(bf16[256,768]{1,0:T(8,128)(2,1)} %dynamic-slice_bitcast_fusion.5), channel_id=1, source_target_pairs={{0,1},{1,0},{2,3},{3,2},{4,5},{5,4},{6,7},{7,6},{8,9},{9,8},{10,11... | collective-permute-start | bytes 1179656 | tf_op jit(solution)/shard_map/ppermute | solution.py:318
  267.4 8.7 %collective-permute-start.22 = (f32[7296]{0:T(1024)S(1)}, f32[7296]{0:T(1024)S(1)}, u32[]{:S(2)}, u32[]{:S(2)}) collective-permute-start(f32[7296]{0:T(1024)S(1)} %pad_maximum_fusion.11), channel_id=1, source_target_pairs={{0,1},{1,0},{2,3},{3,2},{4,5},{5,4},{6,7},{7,6},{8,9},{9,8},{10,11... | collective-permute-start | bytes 87560 | tf_op jit(solution)/shard_map/ppermute | solution.py:318
  274.6 87.9 %copy-start.9 = (bf16[512,768]{1,0:T(8,128)(2,1)S(1)}, bf16[512,768]{1,0:T(8,128)(2,1)}, u32[]{:S(2)}) copy-start(bf16[512,768]{1,0:T(8,128)(2,1)} %copy-done.8) | copy-start | bytes 2359300
  275.5 88.0 %collective-permute-start.15 = (bf16[256,768]{1,0:T(8,128)(2,1)S(1)}, bf16[256,768]{1,0:T(8,128)(2,1)S(1)}, u32[]{:S(2)}, u32[]{:S(2)}) collective-permute-start(bf16[256,768]{1,0:T(8,128)(2,1)S(1)} %dynamic-slice_bitcast_fusion.1), channel_id=1, source_target_pairs={{0,1},{1,0},{2,3},{3,2},{4,5},{5,4},{6,7},{7,6},{8,9},{9,8},{10,11... | collective-permute-start | bytes 1179656 | tf_op jit(solution)/shard_map/ppermute | solution.py:318
  275.8 88.8 %collective-permute-start.16 = (bf16[256,768]{1,0:T(8,128)(2,1)}, bf16[256,768]{1,0:T(8,128)(2,1)S(1)}, u32[]{:S(2)}, u32[]{:S(2)}) collective-permute-start(bf16[256,768]{1,0:T(8,128)(2,1)} %dynamic-slice_bitcast_fusion), channel_id=1, source_target_pairs={{0,1},{1,0},{2,3},{3,2},{4,5},{5,4},{6,7},{7,6},{8,9},{9,8},{10,11... | collective-permute-start | bytes 1179656 | tf_op jit(solution)/shard_map/ppermute | solution.py:318
  (87 other events, 399.5 us)
Sparse Core Ops, SparseCore 0:
  253.8 250.7 all-reduce.2

commit v2 on v1

--- a/solution.py
+++ b/solution.py
@@ -1,3 +1,5 @@
+import functools
+
 import jax
 import jax.numpy as jnp
 import ml_dtypes
@@ -252,6 +254,226 @@
     )(seg_hot, proj_c, proj_q, keys, values, rel_keys, bias, embed, vec_c, vec_q, grad_c, grad_q, prob)
 
 
+MESH = pl.DeviceIdType.MESH
+FOLDS = 4
+
+
+def sum_devices_body(dp_size, count, arrays, layout, offsets, *refs):
+    inputs = refs[:arrays]
+    small_in, out_ref, small_out = refs[arrays : arrays + 3]
+    (
+        work, swapped, landed, extra, small_work, small_land, load_sem, store_sem, swap_send, swap_recv,
+        fold_send, fold_recv, spread_send, spread_recv, more_send, more_recv, tiny_send, tiny_recv,
+    ) = refs[arrays + 3 :]
+    rows = work.shape[1]
+    place = lax.axis_index("dp")
+    core = lax.axis_index("mp")
+    strides = [1 + core, 2 - core, 4, 8]
+    more = [16 << step for step in range(8) if (16 << step) < dp_size]
+    bits = [(place // stride) % 2 for stride in strides]
+    partners = [place + (1 - 2 * bit) * stride for bit, stride in zip(bits, strides)]
+    more_partners = [place + (1 - 2 * ((place // stride) % 2)) * stride for stride in more]
+    lengths = [rows >> (fold + 1) for fold in range(FOLDS)]
+    starts, begin = [], 0
+    for bit, length in zip(bits, lengths):
+        begin = begin + bit * length
+        starts.append(begin)
+    land_at = [rows - 2 * length for length in lengths]
+
+    def kept(fold):
+        return pl.ds(pl.multiple_of(starts[fold], 16), lengths[fold])
+
+    def given(fold):
+        return pl.ds(pl.multiple_of(starts[fold] + (1 - 2 * bits[fold]) * lengths[fold], 16), lengths[fold])
+
+    def remote(source, target, send, recv, device):
+        return pltpu.make_async_remote_copy(
+            src_ref=source, dst_ref=target, send_sem=send, recv_sem=recv,
+            device_id=device, device_id_type=MESH,
+        )
+
+    def fold_copy(fold, piece):
+        return remote(
+            work.at[piece, given(fold)],
+            landed.at[piece, pl.ds(land_at[fold], lengths[fold])],
+            fold_send.at[fold, piece], fold_recv.at[fold, piece], {"dp": partners[fold]},
+        )
+
+    def spread_copy(fold, piece):
+        return remote(
+            swapped.at[piece, kept(fold)],
+            swapped.at[piece, kept(fold)],
+            spread_send.at[fold, piece], spread_recv.at[fold, piece], {"dp": partners[fold]},
+        )
+
+    def more_copy(step, piece):
+        return remote(
+            work.at[piece, kept(FOLDS - 1)],
+            extra.at[step, piece],
+            more_send.at[step, piece], more_recv.at[step, piece], {"dp": more_partners[step]},
+        )
+
+    def whole_swap(piece):
+        return remote(
+            work.at[piece], swapped.at[piece], swap_send.at[piece], swap_recv.at[piece], {"mp": 1 - core}
+        )
+
+    def whole_load(piece):
+        return pltpu.make_async_copy(swapped.at[piece], work.at[piece], load_sem.at[piece])
+
+    def store(piece):
+        return pltpu.make_async_copy(swapped.at[piece], out_ref.at[piece], store_sem.at[piece])
+
+    def add_rows(piece, where, other):
+        mine = work[piece, where, :].astype(jnp.float32)
+        work[piece, where, :] = (mine + other.astype(jnp.float32)).astype(jnp.bfloat16)
+
+    tiny_devices = [{"mp": 1 - core}] + [{"dp": partner} for partner in partners + more_partners]
+
+    def tiny_copy(step):
+        return remote(
+            small_in.at[1] if step == 0 else small_work.at[step],
+            small_land.at[step], tiny_send.at[step], tiny_recv.at[step], tiny_devices[step],
+        )
+
+    barrier = pltpu.get_barrier_semaphore()
+    for device in tiny_devices:
+        pl.semaphore_signal(barrier, inc=1, device_id=device, device_id_type=MESH)
+    pl.semaphore_wait(barrier, len(tiny_devices))
+
+    tiny_copy(0).start()
+    small_work[0] = small_in[0]
+    for piece in range(count):
+        for index, row, col, far_row, far_col, height, to_row in layout[piece]:
+            width = work.shape[2]
+            here = pl.ds(to_row, height)
+            remote(
+                inputs[index].at[pl.ds(far_row, height), pl.ds(far_col, width)],
+                swapped.at[piece, here],
+                swap_send.at[piece], swap_recv.at[piece], {"mp": 1 - core},
+            ).start()
+            pltpu.make_async_copy(
+                inputs[index].at[pl.ds(row, height), pl.ds(col, width)], work.at[piece, here], load_sem.at[piece]
+            ).start()
+
+    def stage(number, piece):
+        if number == 0:
+            whole_load(piece).wait()
+            whole_swap(piece).wait_recv()
+            add_rows(piece, pl.ds(0, rows), swapped[piece])
+            fold_copy(0, piece).start()
+        elif number <= FOLDS:
+            fold = number - 1
+            fold_copy(fold, piece).wait_recv()
+            add_rows(piece, kept(fold), landed[piece, pl.ds(land_at[fold], lengths[fold]), :])
+            if fold + 1 < FOLDS:
+                fold_copy(fold + 1, piece).start()
+                return
+            for step in range(len(more)):
+                more_copy(step, piece).start()
+                more_copy(step, piece).wait()
+                add_rows(piece, kept(fold), extra[step, piece])
+            swapped[piece, kept(fold), :] = work[piece, kept(fold), :]
+            spread_copy(fold, piece).start()
+        else:
+            fold = 2 * FOLDS - number
+            remote(
+                swapped.at[piece, kept(fold)], swapped.at[piece, given(fold)],
+                spread_send.at[fold, piece], spread_recv.at[fold, piece], {"dp": partners[fold]},
+            ).wait_recv()
+            if fold > 0:
+                spread_copy(fold - 1, piece).start()
+            else:
+                store(piece).start()
+
+    def advance(tick, carry):
+        for step in range(len(tiny_devices)):
+            @pl.when(tick == step + 1)
+            def _():
+                tiny_copy(step).wait_recv()
+                small_work[step + 1] = small_work[step] + small_land[step]
+                if step + 1 < len(tiny_devices):
+                    tiny_copy(step + 1).start()
+
+        for number in reversed(range(2 * FOLDS + 1)):
+            piece = tick - offsets[number]
+
+            @pl.when((piece >= 0) & (piece < count))
+            def _():
+                stage(number, piece)
+
+        return carry
+
+    lax.fori_loop(0, count + offsets[-1], advance, 0)
+    small_out[...] = small_work[len(tiny_devices)]
+    for step in range(len(tiny_devices)):
+        tiny_copy(step).wait_send()
+
+    def drain(piece, carry):
+        whole_swap(piece).wait_send()
+        for fold in range(FOLDS):
+            fold_copy(fold, piece).wait_send()
+            spread_copy(fold, piece).wait_send()
+        store(piece).wait()
+        return carry
+
+    lax.fori_loop(0, count, drain, 0)
+
+
+def sum_devices(dp_size, grads, layout, small, lag):
+    rows = sum(part[5] for part in layout[0])
+    cols = layout_width(grads, layout)
+    count = len(layout)
+    more = max(1, dp_size.bit_length() - 1 - FOLDS)
+    stages = 2 * FOLDS + 1
+    offsets = [number * lag for number in range(stages)]
+    tiny = dp_size.bit_length()
+    low = jnp.bfloat16
+    dma = pltpu.SemaphoreType.DMA
+    return pl.pallas_call(
+        functools.partial(sum_devices_body, dp_size, count, len(grads), layout, offsets),
+        out_shape=(
+            jax.ShapeDtypeStruct((count, rows, cols), low),
+            jax.ShapeDtypeStruct(small.shape[1:], jnp.float32),
+        ),
+        in_specs=[pl.BlockSpec(memory_space=pl.ANY)] * len(grads) + [pl.BlockSpec(memory_space=pltpu.VMEM)],
+        out_specs=(pl.BlockSpec(memory_space=pl.ANY), pl.BlockSpec(memory_space=pltpu.VMEM)),
+        scratch_shapes=[
+            pltpu.VMEM((count, rows, cols), low),
+            pltpu.VMEM((count, rows, cols), low),
+            pltpu.VMEM((count, rows, cols), low),
+            pltpu.VMEM((more, count, rows >> FOLDS, cols), low),
+            pltpu.VMEM((tiny + 1,) + small.shape[1:], jnp.float32),
+            pltpu.VMEM((tiny,) + small.shape[1:], jnp.float32),
+            dma((count,)), dma((count,)), dma((count,)), dma((count,)),
+            dma((FOLDS, count)), dma((FOLDS, count)), dma((FOLDS, count)), dma((FOLDS, count)),
+            dma((more, count)), dma((more, count)), dma((tiny,)), dma((tiny,)),
+        ],
+        compiler_params=pltpu.CompilerParams(
+            collective_id=0, has_side_effects=True, vmem_limit_bytes=48 << 20
+        ),
+        name="sum_devices",
+    )(*grads, small)
+
+
+def layout_width(grads, layout):
+    return grads[0].shape[1] // 2
+
+
+def piece_layout(up_at, down_at, out_at, square_at, cols, half_ff):
+    width = 2 * cols
+    pieces = []
+    for rblock in range(half_ff // width):
+        for cblock in range(2):
+            pieces.append([(down_at, rblock * width, cblock * cols, half_ff + rblock * width, cblock * cols, width, 0)])
+    for block in range(half_ff // cols):
+        pieces.append([(up_at, 0, block * cols, 0, half_ff + block * cols, width, 0)])
+    pieces.append([(out_at, 0, 0, cols, 0, cols, 0), (out_at, 0, cols, cols, cols, cols, cols)])
+    for index in square_at:
+        pieces.append([(index, 0, 0, 0, cols, width, 0)])
+    return pieces
+
+
 epsilon = 1e-06
 
 
@@ -282,6 +504,7 @@
 
 
 def on_device(
+    dp_size,
     content_in,
     query_in,
     doc_lengths,
@@ -400,62 +623,66 @@
     ff = up_weight.shape[1]
     cols = query_weight.shape[1]
 
-    def merge(left, right, axis):
-        if axis == 1:
-            split = right.shape[1] // 2
-            other = low_f(dot_left(left, right[:, split:]))
-            own = dot_left(left, right[:, :split])
-        else:
-            split = left.shape[1] // 2
-            other = low_f(dot_left(left[:, split:], right))
-            own = dot_left(left[:, :split], right)
-        return low_f(own + wide_f(swap(other)))
-
-    g_down = lax.psum(merge(act, grad_down, 0), "dp")
-    g_up = lax.psum(merge(first, grad_hidden, 1), "dp")
-    g_out = lax.psum(merge(vec, grad_mixed, 0), "dp")
+    g_down = low_f(dot_left(act, grad_down))
+    g_up = low_f(dot_left(first, grad_hidden))
+    g_out = low_f(dot_left(vec, grad_mixed))
 
     gproj_c, gproj_q, gkeys, gvalues, grel, small = attend_backward(
         seg_hot, proj_c, proj_q, keys, values, rel_keys, bias, embed, vec_c, vec_q,
         grad_vec[None, :seq_len], grad_vec[None, seq_len:], prob,
     )
     gproj = jnp.concatenate([gproj_c[0], gproj_q[0]], axis=0)
-    g_query = lax.psum(merge(resid, gproj, 1), "dp")
-    g_key = lax.psum(merge(content, gkeys[0], 1), "dp")
-    g_value = lax.psum(merge(content, gvalues[0], 1), "dp")
-    g_rel = lax.psum(merge(table, jnp.transpose(grel[0]), 1), "dp")
+    g_query = low_f(dot_left(resid, gproj))
+    g_key = low_f(dot_left(content, gkeys[0]))
+    g_value = low_f(dot_left(content, gvalues[0]))
+    g_rel = low_f(lax.dot_general(table, grel[0], (((0,), (1,)), ((), ())), preferred_element_type=jnp.float32))
     content_grad = low_f(
         nt(gproj_c[0], query_use) + nt(gkeys[0], key_use) + nt(gvalues[0], value_use) + grad_pre1[:seq_len]
     )
     query_grad = low_f(nt(gproj_q[0], query_use) + grad_pre1[seq_len:])
 
     small = small[0]
-    pack_split = jnp.concatenate([small[:5].reshape(-1, 2, cols).transpose(1, 0, 2).reshape(2, -1), g_up_bias.reshape(2, ff)], axis=1)
-    pack_same = jnp.stack([g_gain1, g_shift1, g_gain2, g_shift2, g_down_bias]).reshape(-1)
-    got = swap(jnp.concatenate([pack_split[1], pack_same]))
-    tiny = lax.psum(jnp.concatenate([pack_split[0], pack_same]) + got, "dp")
-    at = 5 * cols
-    split_part = tiny[:at].reshape(5, cols)
-    same_part = tiny[at + ff :].reshape(5, width)
+    up_rows = ff // cols
+    halves = jnp.concatenate(
+        [jnp.stack([small[:5, :cols], small[:5, cols:]]), g_up_bias.reshape(2, up_rows, cols)], axis=1
+    )
+    same = jnp.stack([g_gain1, g_shift1, g_gain2, g_shift2, g_down_bias]).reshape(2 * 5, cols)
+    split_rows = 5 + up_rows
+    filler = jnp.zeros((2, (-split_rows - 10) % 8, cols), jnp.float32)
+    packed = jnp.concatenate([halves, jnp.stack([same, same]), filler], axis=1)
+    layout = piece_layout(1, 0, 2, (3, 4, 5, 6), cols, ff)
+    pieces, tiny = sum_devices(
+        dp_size, [g_down, g_up, g_out, g_query, g_key, g_value, g_rel], layout, packed, 2
+    )
+    pieces = wide_f(pieces)
+    down_count = 2 * (ff // width)
+    down_sum = jnp.concatenate(
+        [jnp.concatenate([pieces[at], pieces[at + 1]], axis=1) for at in range(0, down_count, 2)], axis=0
+    )
+    up_sum = jnp.concatenate([pieces[down_count + at] for at in range(up_rows)], axis=1)
+    at = down_count + up_rows
+    out_sum = jnp.concatenate([pieces[at, :cols], pieces[at, cols:]], axis=1)
+    same_part = tiny[split_rows : split_rows + 10].reshape(5, width)
+    split_part = tiny[:5]
     return (
         return_doc(out_rows[:seq_len]),
         return_doc(out_rows[seq_len:]),
         return_doc(content_grad),
         return_doc(query_grad),
-        wide_f(g_query),
-        wide_f(g_key),
-        wide_f(g_value),
-        wide_f(g_out),
-        wide_f(g_rel),
+        pieces[at + 1],
+        pieces[at + 2],
+        pieces[at + 3],
+        out_sum,
+        pieces[at + 4],
         split_part[0],
         split_part[1],
         split_part[2],
         split_part[3:5],
         same_part[0],
         same_part[1],
-        wide_f(g_up),
-        tiny[at : at + ff],
-        wide_f(g_down),
+        up_sum,
+        tiny[5:split_rows].reshape(ff),
+        down_sum,
         same_part[4],
         same_part[2],
         same_part[3],
@@ -491,7 +718,7 @@
         P("dp", "mp", None),
     )
     return jax.shard_map(
-        on_device,
+        functools.partial(on_device, mesh.shape["dp"]),
         mesh=mesh,
         in_specs=placed,
         out_specs=(

time: 531 us -> 449 us (0.85)
  waiting for transfers between devices: 140 us -> 1.32 us
  Pallas kernels: 91.8 us -> 229 us
  blocking collectives: 81.9 us -> 0 us
  between operations: 15.7 us -> 2.1 us
  other arithmetic: 41.5 us -> 48.6 us
  local copies, waits for them, and re-layouts: 50.4 us -> 57.2 us
    psum x1 -> x0, waiting for transfers between devices: 139 us -> none  [on_device(): g_query = lax.psum(merge(resid, gproj, 1), 'dp')]
    pallas_call x0 -> x1, Pallas kernels: none -> 137 us  [sum_devices(): pl.pallas_call(functools.partial(sum_devices_body, dp_size, count, len(gr...]
    psum x1 -> x0, blocking collectives: 81.9 us -> none  [on_device(): tiny = lax.psum(jnp.concatenate([pack_split[0], pack_same]) + got, 'dp')]
    squeeze x0 -> x7, local copies, waits for them, and re-layouts: none -> 13.5 us  [the longest x1 9.12 us: on_device(): pieces[at]]
    concatenate x1 -> x4, other arithmetic: 0.72 us -> 8.95 us  [the longest x1 5.22 us: on_device(): jnp.concatenate([pieces[down_count + at] for at in range(up_rows)], axis=1)]
    dot_general x14 -> x6, matrix products: 32.4 us -> 27.1 us  [dot_left(): lax.dot_general(left_op, right_op, (((0,), (0,)), ((), ())), preferred_el...]
    convert_element_type x12 -> x6, other arithmetic: 16.1 us -> 12.7 us  [on_device(): wide_f = lambda value: value.astype(jnp.float32)]
    unnamed x192 -> x168, local copies, waits for them, and re-layouts: 15.5 us -> 14.4 us
  transfers between devices with their start and end apart: 26 -> 17, of which waited for: 2 -> 2; matrix products, arithmetic and copies ran while one was open for 20% -> 24% of each run, Pallas kernels for 7% -> 8%
where the time goes in v2:
time: 449 us; the launch traced here: 443 us
  Pallas kernels  229 us (51%)
  matrix products  99.2 us (22%)
  local copies, waits for them, and re-layouts  57.2 us (13%)
  other arithmetic  48.6 us (11%)
  starting transfers between devices  4.77 us (1%)
    pallas_call x1, Pallas kernels, sum_devices(): pl.pallas_call(functools.partial(sum_devices_body, dp_size, count, len(gr...  137 us
    pallas_call x1, Pallas kernels, attend_backward(): pl.pallas_call(attend_backward_body, out_shape=(low, low, low, low, jax.S...  56.2 us
    pallas_call x1, Pallas kernels, attend_forward(): pl.pallas_call(attend_forward_body, out_shape=(jax.ShapeDtypeStruct((docs...  35.7 us
    dot_general x7, matrix products, nt(): lax.dot_general(left_op, right_op, (((1,), (1,)), ((), ())), preferred_el...  35.7 us
    dot_general x8, matrix products, nn(): return jnp.dot(left_op, right_op, preferred_element_type=jnp.float32)  34 us
    dot_general x6, matrix products, dot_left(): lax.dot_general(left_op, right_op, (((0,), (0,)), ((), ())), preferred_el...  27.1 us
    unnamed x168, local copies, waits for them, and re-layouts  14.4 us
    convert_element_type x6, other arithmetic, on_device(): wide_f = lambda value: value.astype(jnp.float32)  12.7 us
  transfers between devices with their start and end apart: 17, of which 2 were waited for; matrix products, arithmetic and copies ran while one was open for 24% of the time, Pallas kernels for 8%

profile of v2, /device:TPU:0, one launch (start us, length us, event | category | flops | bytes accessed | tf_op | source)
XLA Modules:
  0.0 442.6 jit_solution(7431367702318621222)
XLA Ops:
  1.3 1.9 dynamic-slice_bitcast_fusion.6
  5.4 3.2 constant_dynamic-update-slice_fusion.11
  11.2 1.9 constant_dynamic-update-slice_fusion.1
  14.0 1.9 constant_dynamic-update-slice_fusion.7
  20.4 1.8 dynamic-slice_bitcast_fusion.3
  43.0 1.9 convolution_bitcast_fusion.1.proj_c
  48.4 1.9 convolution_bitcast_fusion.proj_q
  50.4 2.6 fusion.25.rel_ref
  53.0 35.7 %attend_forward.1 = (bf16[1,512,768]{2,1,0:T(8,128)(2,1)}, bf16[1,512,768]{2,1,0:T(8,128)(2,1)}, bf16[1,6,2,2,512,512]{5,4,3,2,1,0:T(8,128)(2,1)}) custom-call(s32[1]{0:T(128)} %dynamic_slice.63.len_ref, s32[1,512,1]{2,1,0:T(8,128)} %copy.50.rank_col, s32[1,1,512]{2,1,0:T(1,128)} %get-tuple-element.99.rank_row, s32[1,1,512]{2,1,0:T(1,128)} %get-tuple-element.108.live_row, ...), custom_call_target="tpu_custom_call" | custom-call | tf_op jit(solution)/shard_map/attend_forward/pallas_call | solution.py:98
  89.6 3.5 fusion.73
  93.7 2.2 constant_dynamic-update-slice_fusion.8
  95.9 8.4 %fusion.75 = f32[1024,3072]{1,0:T(8,128)} fusion(bf16[768,3072]{1,0:T(8,128)(2,1)S(1)} %constant_dynamic-update-slice_fusion.8, f32[1024,768]{1,0:T(8,128)S(1)} %get-tuple-element.102, f32[768]{0:T(1024)S(1)} %copy-done.61, f32[768]{0:T(1024)S(1)} %convert_element_type.107, f32[1024]{0:T(1024)S(1)} %fusion.56, f32[1024]{0:T(1024)S(1)} %broadcast_multiply_fusion.1), kind=kOutput, calls=%fused_computation.190 | convolution fusion | flops 4835770368 | bytes 20461568 | tf_op jit(solution)/shard_map/dot_general | solution.py:25
  104.4 1.8 constant_dynamic-update-slice_fusion.10
  106.2 12.3 %fusion.74 = (f32[1024]{0:T(1024)S(1)}, f32[1024,768]{1,0:T(8,128)S(1)}) fusion(f32[768]{0:T(1024)S(1)} %copy-done.62, bf16[3072,768]{1,0:T(8,128)(2,1)S(1)} %constant_dynamic-update-slice_fusion.10, f32[1024,3072]{1,0:T(8,128)} %fusion.75, f32[3072]{0:T(1024)S(1)} %bitcast.197, f32[768]{0:T(1024)S(1)} %copy-done.61, f32[768]{0:T(1024)S(1)} %convert_element_type.107, ...), kind=kOutput, calls=%fused_computation.189 | convolution fusion | flops 4870372352 | bytes 23626752 | tf_op jit(solution)/shard_map/dot_general | solution.py:25
  119.2 3.5 fusion.10
  122.8 3.7 fusion.70
  126.4 17.9 %convert_reduce_fusion = (f32[3072]{0:T(1024)}, bf16[1024,3072]{1,0:T(8,128)(2,1)}) fusion(f32[1024,3072]{1,0:T(8,128)} %fusion.75, f32[3072]{0:T(1024)S(1)} %bitcast.198, bf16[3072,768]{1,0:T(8,128)(2,1)} %copy-done.21, f32[1024,768]{1,0:T(8,128)S(1)} %get-tuple-element.55, f32[1024]{0:T(1024)S(1)} %negate_multiply_fusion.1), kind=kOutput, calls=%fused_computation.9 | convolution fusion | flops 4905759744 | bytes 26767360 | tf_op jit(solution)/shard_map/dot_general | solution.py:19
  144.4 12.8 %convolution_convert_fusion.1.refs_0_ = bf16[3072,768]{1,0:T(8,128)(2,1)} fusion(f32[1024,768]{1,0:T(8,128)S(1)} %get-tuple-element.55, f32[1024]{0:T(1024)S(1)} %negate_multiply_fusion.1, f32[1024,3072]{1,0:T(8,128)} %fusion.75, f32[3072]{0:T(1024)S(1)} %bitcast.199), kind=kOutput, calls=%fused_computation.12 | convolution fusion | flops 4867227648 | bytes 20463616 | tf_op jit(solution)/shard_map/dot_general | solution.py:501
  157.2 6.4 %multiply_reduce_fusion = (f32[768]{0:T(1024)}, f32[1024]{0:T(1024)S(1)}, f32[768]{0:T(1024)}, f32[1024,768]{1,0:T(8,128)S(1)}) fusion(f32[1024,768]{1,0:T(8,128)S(1)} %get-tuple-element.102, f32[1024]{0:T(1024)S(1)} %fusion.56, f32[1024]{0:T(1024)S(1)} %broadcast_multiply_fusion.1, f32[768]{0:T(1024)S(1)} %copy-done.55, ...), kind=kOutput, calls=%fused_computation.24 | convolution fusion | flops 4839699456 | bytes 20472832 | tf_op jit(solution)/shard_map/dot_general | solution.py:19
  163.6 7.8 %convolution_convert_fusion.refs_1_ = bf16[768,3072]{1,0:T(8,128)(2,1)} fusion(bf16[1024,3072]{1,0:T(8,128)(2,1)S(1)} %copy-done.74, f32[1024,768]{1,0:T(8,128)S(1)} %get-tuple-element.102, f32[768]{0:T(1024)S(1)} %copy-done.61, f32[768]{0:T(1024)S(1)} %copy-done.55, f32[1024]{0:T(1024)S(1)} %fusion.56, f32[1024]{0:T(1024)S(1)} %broadcast_multiply_fusion.1), kind=kOutput, calls=%fused_computation.11 | convolution fusion | flops 4838129664 | bytes 14170112 | tf_op jit(solution)/shard_map/dot_general | solution.py:501
  179.4 56.2 %attend_backward.1 = (bf16[1,512,768]{2,1,0:T(8,128)(2,1)}, bf16[1,512,768]{2,1,0:T(8,128)(2,1)}, bf16[1,512,768]{2,1,0:T(8,128)(2,1)}, bf16[1,512,768]{2,1,0:T(...) custom-call(bf16[1,512,128]{2,1,0:T(8,128)(2,1)} %and_convert_fusion.seg_hot, ...), custom_call_target="tpu_custom_call" | custom-call | tf_op jit(solution)/shard_map/attend_backward/pallas_call | solution.py:222
  235.6 3.3 fusion.43
  240.4 2.0 fusion.67
  242.4 1.7 fusion.11
  245.0 2.5 fusion.26.refs_6_
  252.8 3.4 fusion.19.refs_3_
  256.3 137.4 %sum_devices.1 = (bf16[13,768,384]{2,1,0:T(8,128)(2,1)}, f32[24,384]{1,0:T(8,128)S(1)}) custom-call(bf16[3072,768]{1,0:T(8,128)(2,1)} %convolution_convert_fusion.1.refs_0_, bf16[768,3072]{1,0:T(8,128)(2,1)} %convolution_convert_fusion.refs_1_, bf16[768,768]{1,0:T(8,128)(2,1)S(1)} %convolution_convert_fusion.6.refs_2_, bf16[768,768]{1,0:T(8,128)(2,1)S(1)} %fusion.19.refs_3_, ...), custom_call_target="tpu_custom_call" | custom-call | tf_op jit(solution)/shard_map/sum_devices/pallas_call | solution.py:433
  397.2 3.0 fusion.12
  403.2 6.8 %convert_element_type.132 = f32[13,768,384]{2,1,0:T(8,128)} convert(bf16[13,768,384]{2,1,0:T(8,128)(2,1)S(1)} %copy-done.6) | non-fusion elementwise | flops 3833856 | bytes 23003136 | tf_op jit(solution)/shard_map/convert_element_type | solution.py:537
  410.0 9.1 %slice_bitcast_fusion.3 = (f32[768,384]{1,0:T(8,128)S(1)}, f32[768,384]{1,0:T(8,128)S(1)}, f32[768,384]{1,0:T(8,128)S(1)}, f32[768,384]{1,0:T(8,128)}, f32[768,3...) fusion(f32[13,768,384]{2,1,0:T(8,128)} %convert_element_type.132), kind=kLoop, calls=%fused_computation.67 | loop fusion | bytes 28311552 | tf_op jit(solution)/shard_map/squeeze | solution.py:660
  419.1 5.2 %pad_maximum_fusion = f32[768,1536]{1,0:T(8,128)} fusion(f32[768,384]{1,0:T(8,128)} %get-tuple-element.60, f32[768,384]{1,0:T(8,128)} %get-tuple-element.61, f32[768,384]{1,0:T(8,128)} %get-tuple-element.62, f32[768,384]{1,0:T(8,128)} %get-tuple-element.63), kind=kLoop, calls=%fused_computation.18 | loop fusion | flops 3538944 | bytes 9437184 | tf_op jit(solution)/shard_map/concatenate | solution.py:662
  424.4 2.6 maximum_maximum_fusion
  (288 shorter events, 74.3 us)
Async XLA Ops:
  0.7 21.5 %copy-start = (s32[2,512]{1,0:T(2,128)S(1)}, s32[2,512]{1,0:T(2,128)}, u32[]{:S(2)}) copy-start(s32[2,512]{1,0:T(2,128)} %param.30) | copy-start | bytes 12292
  0.7 103.6 %collective-permute-start.10 = (bf16[1536,768]{1,0:T(8,128)(2,1)}, bf16[1536,768]{1,0:T(8,128)(2,1)}, u32[]{:S(2)}, u32[]{:S(2)}) collective-permute-start(bf16[1536,768]{1,0:T(8,128)(2,1)} %param.45), channel_id=1, source_target_pairs={{0,1},{1,0},{2,3},{3,2},{4,5},{5,4},{6,7},{7,6},{8,9},{9,8},{10,11... | collective-permute-start | bytes 7077896 | tf_op jit(solution)/shard_map/ppermute | solution.py:541
  1.2 92.5 %collective-permute-start.8 = (bf16[768,1536]{1,0:T(8,128)(2,1)}, bf16[768,1536]{1,0:T(8,128)(2,1)}, u32[]{:S(2)}, u32[]{:S(2)}) collective-permute-start(bf16[768,1536]{1,0:T(8,128)(2,1)} %param.43), channel_id=1, source_target_pairs={{0,1},{1,0},{2,3},{3,2},{4,5},{5,4},{6,7},{7,6},{8,9},{9,8},{10,11... | collective-permute-start | bytes 7077896 | tf_op jit(solution)/shard_map/ppermute | solution.py:541
  3.2 34.1 %collective-permute-start.2 = (bf16[256,768]{1,0:T(8,128)(2,1)}, bf16[256,768]{1,0:T(8,128)(2,1)}, u32[]{:S(2)}, u32[]{:S(2)}) collective-permute-start(bf16[256,768]{1,0:T(8,128)(2,1)} %dynamic-slice_bitcast_fusion.6), channel_id=1, source_target_pairs={{0,1},{1,0},{2,3},{3,2},{4,5},{5,4},{6,7},{7,6},{8,9},{9,8},{10,11... | collective-permute-start | bytes 1179656 | tf_op jit(solution)/shard_map/ppermute | solution.py:541
  3.6 37.4 %collective-permute-start.1 = (bf16[768,384]{1,0:T(8,128)(2,1)}, bf16[768,384]{1,0:T(8,128)(2,1)}, u32[]{:S(2)}, u32[]{:S(2)}) collective-permute-start(bf16[768,384]{1,0:T(8,128)(2,1)} %param.32), channel_id=1, source_target_pairs={{0,1},{1,0},{2,3},{3,2},{4,5},{5,4},{6,7},{7,6},{8,9},{9,8},{10,11... | collective-permute-start | bytes 1769480 | tf_op jit(solution)/shard_map/ppermute | solution.py:541
  5.0 29.2 %collective-permute-start.9 = (f32[1,1536]{1,0:T(1,128)}, f32[1,1536]{1,0:T(1,128)}, u32[]{:S(2)}, u32[]{:S(2)}) collective-permute-start(f32[1,1536]{1,0:T(1,128)} %reshape.259), channel_id=1, source_target_pairs={{0,1},{1,0},{2,3},{3,2},{4,5},{5,4},{6,7},{7,6},{8,9},{9,8},{10,11... | collective-permute-start | bytes 18440 | tf_op jit(solution)/shard_map/ppermute | solution.py:541
  13.2 24.1 %copy-start.27 = (bf16[2,256,768]{2,1,0:T(8,128)(2,1)S(1)}, bf16[2,256,768]{2,1,0:T(8,128)(2,1)}, u32[]{:S(2)}) copy-start(bf16[2,256,768]{2,1,0:T(8,128)(2,1)} %param.27) | copy-start | bytes 2359300
  31.1 75.1 %copy-start.54 = (f32[768]{0:T(1024)}, f32[768]{0:T(1024)S(1)}, u32[]{:S(2)}) copy-start(f32[768]{0:T(1024)S(1)} %convert_element_type.107) | copy-start | bytes 9220
  34.2 1.4 collective-permute-start.6
  35.6 3.0 collective-permute-start
  37.2 1.9 collective-permute-start.14
  38.6 2.0 collective-permute-start.13
  39.2 3.3 collective-permute-start.3
  40.6 48.1 %collective-permute-start.7 = (bf16[384,768]{1,0:T(8,128)(2,1)}, bf16[384,768]{1,0:T(8,128)(2,1)S(1)}, u32[]{:S(2)}, u32[]{:S(2)}) collective-permute-start(bf16[384,768]{1,0:T(8,128)(2,1)} %param.35), channel_id=1, source_target_pairs={{0,1},{1,0},{2,3},{3,2},{4,5},{5,4},{6,7},{7,6},{8,9},{9,8},{10,11... | collective-permute-start | bytes 1769480 | tf_op jit(solution)/shard_map/ppermute | solution.py:541
  41.0 5.6 %collective-permute-start.4 = (bf16[768,384]{1,0:T(8,128)(2,1)S(1)}, bf16[768,384]{1,0:T(8,128)(2,1)S(1)}, u32[]{:S(2)}, u32[]{:S(2)}) collective-permute-start(bf16[768,384]{1,0:T(8,128)(2,1)S(1)} %copy-done.35), channel_id=1, source_target_pairs={{0,1},{1,0},{2,3},{3,2},{4,5},{5,4},{6,7},{7,6},{8,9},{9,8},{10,11... | collective-permute-start | bytes 1769480 | tf_op jit(solution)/shard_map/ppermute | solution.py:541
  42.4 7.9 %collective-permute-start.5 = (bf16[768,384]{1,0:T(8,128)(2,1)S(1)}, bf16[768,384]{1,0:T(8,128)(2,1)S(1)}, u32[]{:S(2)}, u32[]{:S(2)}) collective-permute-start(bf16[768,384]{1,0:T(8,128)(2,1)S(1)} %copy-done.71), channel_id=1, source_target_pairs={{0,1},{1,0},{2,3},{3,2},{4,5},{5,4},{6,7},{7,6},{8,9},{9,8},{10,11... | collective-permute-start | bytes 1769480 | tf_op jit(solution)/shard_map/ppermute | solution.py:541
  53.0 36.6 %copy-start.37 = (bf16[256,768]{1,0:T(8,128)(2,1)S(1)}, bf16[256,768]{1,0:T(8,128)(2,1)}, u32[]{:S(2)}) copy-start(bf16[256,768]{1,0:T(8,128)(2,1)} %copy-done.36) | copy-start | bytes 1179652
  53.0 36.6 %copy-start.39 = (bf16[256,768]{1,0:T(8,128)(2,1)S(1)}, bf16[256,768]{1,0:T(8,128)(2,1)}, u32[]{:S(2)}) copy-start(bf16[256,768]{1,0:T(8,128)(2,1)} %copy-done.38) | copy-start | bytes 1179652
  53.0 36.6 %copy-start.41 = (bf16[256,768]{1,0:T(8,128)(2,1)S(1)}, bf16[256,768]{1,0:T(8,128)(2,1)}, u32[]{:S(2)}) copy-start(bf16[256,768]{1,0:T(8,128)(2,1)} %copy-done.40) | copy-start | bytes 1179652
  106.2 12.4 %copy-start.21 = (bf16[3072,768]{1,0:T(8,128)(2,1)}, bf16[3072,768]{1,0:T(8,128)(2,1)S(1)}, u32[]{:S(2)}) copy-start(bf16[3072,768]{1,0:T(8,128)(2,1)S(1)} %constant_dynamic-update-slice_fusion.10) | copy-start | bytes 14155780
  122.7 34.4 %slice-start.4 = ((s8[4718592]{0:T(1024)(128)(4,1)}), s8[524288]{0:T(1024)(128)(4,1)S(1)}, s32[]{:S(2)}) async-start(s8[4718592]{0:T(1024)(128)(4,1)} %bitcast.188), calls=%async_computation.4 | async-start | bytes 1048576
  126.4 30.7 %copy-start.4 = (f32[1024,768]{1,0:T(8,128)}, f32[1024,768]{1,0:T(8,128)S(1)}, u32[]{:S(2)}) copy-start(f32[1024,768]{1,0:T(8,128)S(1)} %get-tuple-element.55) | copy-start | bytes 9437188
  126.4 30.7 %slice-start.5 = ((s8[4718592]{0:T(1024)(128)(4,1)}), s8[4194304]{0:T(1024)(128)(4,1)S(1)}, s32[]{:S(2)}) async-start(s8[4718592]{0:T(1024)(128)(4,1)} %bitcast.188), calls=%async_computation.5 | async-start | bytes 8388608
  144.3 12.8 %copy-start.55 = (f32[768]{0:T(1024)S(1)}, f32[768]{0:T(1024)}, u32[]{:S(2)}) copy-start(f32[768]{0:T(1024)} %copy-done.54) | copy-start | bytes 9220
  144.4 12.8 %copy-start.74 = (bf16[1024,3072]{1,0:T(8,128)(2,1)S(1)}, bf16[1024,3072]{1,0:T(8,128)(2,1)}, u32[]{:S(2)}) copy-start(bf16[1024,3072]{1,0:T(8,128)(2,1)} %get-tuple-element.107) | copy-start | bytes 18874372
  179.3 56.3 %copy-start.48 = (bf16[768,768]{1,0:T(8,128)(2,1)S(1)}, bf16[768,768]{1,0:T(8,128)(2,1)}, u32[]{:S(2)}) copy-start(bf16[768,768]{1,0:T(8,128)(2,1)} %copy-done.47) | copy-start | bytes 3538948
  256.3 138.7 %copy-start.10 = (bf16[1024,768]{1,0:T(8,128)(2,1)S(1)}, bf16[1024,768]{1,0:T(8,128)(2,1)}, u32[]{:S(2)}) copy-start(bf16[1024,768]{1,0:T(8,128)(2,1)} %get-tuple-element.70) | copy-start | bytes 4718596
  256.3 141.0 %copy-start.26 = (bf16[1,512,768]{2,1,0:T(8,128)(2,1)S(1)}, bf16[1,512,768]{2,1,0:T(8,128)(2,1)}, u32[]{:S(2)}) copy-start(bf16[1,512,768]{2,1,0:T(8,128)(2,1)} %get-tuple-element.37) | copy-start | bytes 2359300
  395.9 37.9 %collective-permute-start.11 = (bf16[256,768]{1,0:T(8,128)(2,1)}, bf16[256,768]{1,0:T(8,128)(2,1)}, u32[]{:S(2)}, u32[]{:S(2)}) collective-permute-start(bf16[256,768]{1,0:T(8,128)(2,1)} %dynamic-slice_bitcast_fusion.5), channel_id=1, source_target_pairs={{0,1},{1,0},{2,3},{3,2},{4,5},{5,4},{6,7},{7,6},{8,9},{9,8},{10,11... | collective-permute-start | bytes 1179656 | tf_op jit(solution)/shard_map/ppermute | solution.py:541
  396.7 39.2 %collective-permute-start.12 = (bf16[256,768]{1,0:T(8,128)(2,1)}, bf16[256,768]{1,0:T(8,128)(2,1)}, u32[]{:S(2)}, u32[]{:S(2)}) collective-permute-start(bf16[256,768]{1,0:T(8,128)(2,1)} %dynamic-slice_bitcast_fusion.4), channel_id=1, source_target_pairs={{0,1},{1,0},{2,3},{3,2},{4,5},{5,4},{6,7},{7,6},{8,9},{9,8},{10,11... | collective-permute-start | bytes 1179656 | tf_op jit(solution)/shard_map/ppermute | solution.py:541
  401.9 36.1 %collective-permute-start.15 = (bf16[256,768]{1,0:T(8,128)(2,1)}, bf16[256,768]{1,0:T(8,128)(2,1)}, u32[]{:S(2)}, u32[]{:S(2)}) collective-permute-start(bf16[256,768]{1,0:T(8,128)(2,1)} %dynamic-slice_bitcast_fusion.1), channel_id=1, source_target_pairs={{0,1},{1,0},{2,3},{3,2},{4,5},{5,4},{6,7},{7,6},{8,9},{9,8},{10,11... | collective-permute-start | bytes 1179656 | tf_op jit(solution)/shard_map/ppermute | solution.py:541
  402.7 37.4 %collective-permute-start.16 = (bf16[256,768]{1,0:T(8,128)(2,1)}, bf16[256,768]{1,0:T(8,128)(2,1)}, u32[]{:S(2)}, u32[]{:S(2)}) collective-permute-start(bf16[256,768]{1,0:T(8,128)(2,1)} %dynamic-slice_bitcast_fusion), channel_id=1, source_target_pairs={{0,1},{1,0},{2,3},{3,2},{4,5},{5,4},{6,7},{7,6},{8,9},{9,8},{10,11... | collective-permute-start | bytes 1179656 | tf_op jit(solution)/shard_map/ppermute | solution.py:541
  (66 other events, 306.6 us)

commit v3 on v1

--- a/solution.py
+++ b/solution.py
@@ -1,3 +1,5 @@
+import functools
+
 import jax
 import jax.numpy as jnp
 import ml_dtypes
@@ -126,6 +128,11 @@
     )(lengths, rank_col, rank_row, live_row, seg_hot, proj_c, proj_q, keys, values, rel_keys, bias, embed)
 
 
+MESH = pl.DeviceIdType.MESH
+FOLDS = 4
+LAG = 2
+
+
 def shear_left(value_in):
     rows, wide = value_in.shape
     pack = 16
@@ -142,11 +149,159 @@
     return moved
 
 
-def attend_backward_body(
-    seg_hot, proj_c, proj_q, key_ref, value_ref, rel_ref, bias_ref, embed_ref, vec_c, vec_q,
-    grad_c, grad_q, prob_ref, gproj_c, gproj_q, gkey_ref, gvalue_ref, grel_ref, small_ref,
-    ext_scr, key_acc, value_acc, rel_acc,
-):
+def attend_backward_body(dp_size, layout, count, *refs):
+    (
+        seg_hot, proj_c, proj_q, key_ref, value_ref, rel_ref, bias_ref, embed_ref, vec_c, vec_q,
+        grad_c, grad_q, prob_ref, content_t, query_t, table_t, small_in, down_in, up_in, out_in,
+        gproj_c, gproj_q, gkey_ref, gvalue_ref, sum_out, small_out,
+        ext_scr, key_acc, value_acc, rel_acc, work, swapped, landed, extra, far_work,
+        small_work, small_far, small_land, load_sem, store_sem, swap_send, swap_recv,
+        fold_send, fold_recv, spread_send, spread_recv, more_send, more_recv, tiny_send, tiny_recv,
+    ) = refs
+    inputs = (down_in, up_in, out_in)
+    step_at = pl.program_id(0)
+    steps = pl.num_programs(0)
+    half_steps = 3
+    early = len(layout)
+    rows, cols = work.shape[1:]
+    place = lax.axis_index("dp")
+    core = lax.axis_index("mp")
+    strides = [1 + core, 2 - core, 4, 8]
+    more = [16 << step for step in range(8) if (16 << step) < dp_size]
+    bits = [(place // stride) % 2 for stride in strides]
+    partners = [place + (1 - 2 * bit) * stride for bit, stride in zip(bits, strides)]
+    more_partners = [place + (1 - 2 * ((place // stride) % 2)) * stride for stride in more]
+    lengths = [rows >> (fold + 1) for fold in range(FOLDS)]
+    starts, begin = [], 0
+    for bit, length in zip(bits, lengths):
+        begin = begin + bit * length
+        starts.append(begin)
+    land_at = [rows - 2 * length for length in lengths]
+    offsets = [number * LAG for number in range(2 * FOLDS + 1)]
+
+    def kept(fold):
+        return pl.ds(pl.multiple_of(starts[fold], 16), lengths[fold])
+
+    def given(fold):
+        return pl.ds(pl.multiple_of(starts[fold] + (1 - 2 * bits[fold]) * lengths[fold], 16), lengths[fold])
+
+    def remote(source, target, send, recv, device):
+        return pltpu.make_async_remote_copy(
+            src_ref=source, dst_ref=target, send_sem=send, recv_sem=recv,
+            device_id=device, device_id_type=MESH,
+        )
+
+    def fold_copy(fold, piece):
+        return remote(
+            work.at[piece, given(fold)],
+            landed.at[piece, pl.ds(land_at[fold], lengths[fold])],
+            fold_send.at[fold, piece], fold_recv.at[fold, piece], {"dp": partners[fold]},
+        )
+
+    def spread_copy(fold, piece):
+        return remote(
+            swapped.at[piece, kept(fold)],
+            swapped.at[piece, kept(fold)],
+            spread_send.at[fold, piece], spread_recv.at[fold, piece], {"dp": partners[fold]},
+        )
+
+    def more_copy(step, piece):
+        return remote(
+            work.at[piece, kept(FOLDS - 1)],
+            extra.at[step, piece],
+            more_send.at[step, piece], more_recv.at[step, piece], {"dp": more_partners[step]},
+        )
+
+    def whole_swap(piece):
+        return remote(
+            work.at[piece], swapped.at[piece], swap_send.at[piece], swap_recv.at[piece], {"mp": 1 - core}
+        )
+
+    def late_swap(late):
+        return remote(
+            far_work.at[late], swapped.at[early + late],
+            swap_send.at[early + late], swap_recv.at[early + late], {"mp": 1 - core},
+        )
+
+    def whole_load(piece):
+        return pltpu.make_async_copy(swapped.at[piece], work.at[piece], load_sem.at[piece])
+
+    def store(piece):
+        return pltpu.make_async_copy(swapped.at[piece], sum_out.at[piece], store_sem.at[piece])
+
+    def add_rows(piece, where, other):
+        mine = work[piece, where, :].astype(jnp.float32)
+        work[piece, where, :] = (mine + other.astype(jnp.float32)).astype(jnp.bfloat16)
+
+    tiny_devices = [{"mp": 1 - core}] + [{"dp": partner} for partner in partners + more_partners]
+
+    def tiny_copy(step):
+        return remote(
+            small_far if step == 0 else small_work.at[step],
+            small_land.at[step], tiny_send.at[step], tiny_recv.at[step], tiny_devices[step],
+        )
+
+    @pl.when(step_at == 0)
+    def _():
+        barrier = pltpu.get_barrier_semaphore()
+        for device in tiny_devices:
+            pl.semaphore_signal(barrier, inc=1, device_id=device, device_id_type=MESH)
+        pl.semaphore_wait(barrier, len(tiny_devices))
+        for piece in range(early):
+            for index, row, col, far_row, far_col, height, to_row in layout[piece]:
+                here = pl.ds(to_row, height)
+                remote(
+                    inputs[index].at[pl.ds(far_row, height), pl.ds(far_col, cols)],
+                    swapped.at[piece, here],
+                    swap_send.at[piece], swap_recv.at[piece], {"mp": 1 - core},
+                ).start()
+                pltpu.make_async_copy(
+                    inputs[index].at[pl.ds(row, height), pl.ds(col, cols)], work.at[piece, here], load_sem.at[piece]
+                ).start()
+        small_work[0] = small_in[0]
+        small_far[...] = small_in[1]
+
+    def stage(number, piece):
+        if number == 0:
+            @pl.when(piece < early)
+            def _():
+                whole_load(piece).wait()
+                whole_swap(piece).wait_recv()
+                add_rows(piece, pl.ds(0, rows), swapped[piece])
+
+            fold_copy(0, piece).start()
+        elif number <= FOLDS:
+            fold = number - 1
+            fold_copy(fold, piece).wait_recv()
+            add_rows(piece, kept(fold), landed[piece, pl.ds(land_at[fold], lengths[fold]), :])
+            if fold + 1 < FOLDS:
+                fold_copy(fold + 1, piece).start()
+                return
+            for step in range(len(more)):
+                more_copy(step, piece).start()
+                more_copy(step, piece).wait()
+                add_rows(piece, kept(fold), extra[step, piece])
+            swapped[piece, kept(fold), :] = work[piece, kept(fold), :]
+            spread_copy(fold, piece).start()
+        else:
+            fold = 2 * FOLDS - number
+            remote(
+                swapped.at[piece, kept(fold)], swapped.at[piece, given(fold)],
+                spread_send.at[fold, piece], spread_recv.at[fold, piece], {"dp": partners[fold]},
+            ).wait_recv()
+            if fold > 0:
+                spread_copy(fold - 1, piece).start()
+            else:
+                store(piece).start()
+
+    def advance(tick):
+        for number in reversed(range(2 * FOLDS + 1)):
+            piece = tick - offsets[number]
+
+            @pl.when((piece >= 0) & (piece < count))
+            def _():
+                stage(number, piece)
+
     seq_len = key_ref.shape[0]
     blocks = seq_len // ROWS
     wide = seq_len + ROWS
@@ -164,22 +319,22 @@
         grad_ref = (grad_c, grad_q)[stream]
         gproj_ref = (gproj_c, gproj_q)[stream]
         for block in range(blocks):
-            rows = pl.ds(block * ROWS, ROWS)
+            where = pl.ds(block * ROWS, ROWS)
             start = seq_len - (block + 1) * ROWS
-            proj = proj_ref[rows, :]
+            proj = proj_ref[where, :]
             query_ct = jnp.transpose(((proj + bias_ref[0:1, :]) * 0.125).astype(jnp.bfloat16))
             query_pt = jnp.transpose(((proj + bias_ref[1:2, :]) * 0.125).astype(jnp.bfloat16))
             query_s = proj + bias_ref[2:3, :]
-            hot = jnp.where(lane < 4, seg_hot[rows, :].astype(jnp.float32), 0.0)
-            grad = grad_ref[rows, :]
+            hot = jnp.where(lane < 4, seg_hot[where, :].astype(jnp.float32), 0.0)
+            grad = grad_ref[where, :]
             grad_t = jnp.transpose(grad)
-            inner = grad.astype(jnp.float32) * vec_ref[rows, :].astype(jnp.float32)
+            inner = grad.astype(jnp.float32) * vec_ref[where, :].astype(jnp.float32)
             window = (rel_ref[pl.ds(start, wide), :].astype(jnp.float32) * 0.125).astype(jnp.bfloat16)
             parts = []
             for head in range(2):
                 own = (lane >= DH) if head else first
                 low, high = head * DH, (head + 1) * DH
-                prob = prob_ref[stream, head, rows, :]
+                prob = prob_ref[stream, head, where, :]
                 grad_prob = nt(jnp.where(own, grad, jnp.zeros((), jnp.bfloat16)), value_ref[...])
                 row_inner = jnp.sum(jnp.where(own, inner, 0.0), axis=1, keepdims=True)
                 gscore = (prob.astype(jnp.float32) * (grad_prob - row_inner)).astype(jnp.bfloat16)
@@ -200,56 +355,238 @@
             g_same = jnp.where(first, parts[0][2], parts[1][2])
             g_other = jnp.where(first, parts[0][3], parts[1][3])
             g_segment = g_same * embed_ref[0:1, :] + g_other * embed_ref[1:2, :]
-            gproj_ref[rows, :] = (g_content + g_position + g_segment).astype(jnp.bfloat16)
+            gproj_ref[where, :] = (g_content + g_position + g_segment).astype(jnp.bfloat16)
             terms = (g_content, g_position, g_segment, g_same * query_s, g_other * query_s)
-            sums = [kept + jnp.sum(term, axis=0, keepdims=True) for kept, term in zip(sums, terms)]
+            sums = [kept_sum + jnp.sum(term, axis=0, keepdims=True) for kept_sum, term in zip(sums, terms)]
+        if stream == 0:
+            advance(2 * step_at)
     gkey_ref[...] = jnp.transpose(key_acc[...]).astype(jnp.bfloat16)
     gvalue_ref[...] = jnp.transpose(value_acc[...]).astype(jnp.bfloat16)
-    grel_ref[...] = rel_acc[...].astype(jnp.bfloat16)
-    small_ref[...] = jnp.concatenate(sums + [jnp.zeros((3, PAIR), jnp.float32)], axis=0)
-
-
-def attend_backward(seg_hot, proj_c, proj_q, keys, values, rel_keys, bias, embed, vec_c, vec_q, grad_c, grad_q, prob):
-    docs, seq_len, width = proj_c.shape
+    g_query = nn(content_t[...], gproj_c[...]) + nn(query_t[...], gproj_q[...])
+    g_key = nn(content_t[...], gkey_ref[...])
+    g_value = nn(content_t[...], gvalue_ref[...])
+    g_rel = nt(table_t[...], rel_acc[...].astype(jnp.bfloat16))
+    vectors = jnp.concatenate(sums, axis=0)
+
+    @pl.when(step_at < half_steps)
+    def _():
+        lanes = pl.ds(pl.multiple_of(step_at * PAIR, PAIR), PAIR)
+        far_work[step_at, :, 0:PAIR] = g_query.astype(jnp.bfloat16)
+        far_work[step_at, :, PAIR : 2 * PAIR] = g_key.astype(jnp.bfloat16)
+        far_work[step_at, :, 2 * PAIR :] = g_value.astype(jnp.bfloat16)
+        far_work[half_steps, :, lanes] = g_rel.astype(jnp.bfloat16)
+        small_far[0:5, lanes] = vectors
+        late_swap(step_at).start()
+
+        @pl.when(step_at == half_steps - 1)
+        def _():
+            late_swap(half_steps).start()
+            tiny_copy(0).start()
+
+    @pl.when(step_at >= half_steps)
+    def _():
+        late = step_at - half_steps
+        lanes = pl.ds(pl.multiple_of(late * PAIR, PAIR), PAIR)
+        late_swap(late).wait_recv()
+        for at, value in enumerate((g_query, g_key, g_value)):
+            cut = slice(at * PAIR, (at + 1) * PAIR)
+            value = value + swapped[early + late, :, cut].astype(jnp.float32)
+            work[early + late, :, cut] = value.astype(jnp.bfloat16)
+        work[early + half_steps, :, lanes] = g_rel.astype(jnp.bfloat16)
+        small_work[0, 0:5, lanes] = vectors
+
+        @pl.when(step_at == steps - 1)
+        def _():
+            late_swap(half_steps).wait_recv()
+            add_rows(early + half_steps, pl.ds(0, rows), swapped[early + half_steps])
+
+    advance(2 * step_at + 1)
+
+    @pl.when(step_at == steps - 1)
+    def _():
+        begin_tick = 2 * 2 * half_steps
+
+        def finish(tick, carry):
+            for step in range(len(tiny_devices)):
+                @pl.when(tick == begin_tick + 1 + step)
+                def _():
+                    tiny_copy(step).wait_recv()
+                    small_work[step + 1] = small_work[step] + small_land[step]
+                    if step + 1 < len(tiny_devices):
+                        tiny_copy(step + 1).start()
+
+            advance(tick)
+            return carry
+
+        lax.fori_loop(begin_tick, count + offsets[-1], finish, 0)
+        small_out[...] = small_work[len(tiny_devices)]
+        for step in range(len(tiny_devices)):
+            tiny_copy(step).wait_send()
+
+        def drain(piece, carry):
+            whole_swap(piece).wait_send()
+            for fold in range(FOLDS):
+                fold_copy(fold, piece).wait_send()
+                spread_copy(fold, piece).wait_send()
+            store(piece).wait()
+            return carry
+
+        lax.fori_loop(0, count, drain, 0)
+
+
+def piece_layout(cols, half_ff):
+    width = 2 * cols
+    pieces = []
+    for rblock in range(half_ff // width):
+        for cblock in range(2):
+            pieces.append([(0, rblock * width, cblock * cols, half_ff + rblock * width, cblock * cols, width, 0)])
+    for block in range(half_ff // cols):
+        pieces.append([(1, 0, block * cols, 0, half_ff + block * cols, width, 0)])
+    pieces.append([(2, 0, 0, cols, 0, cols, 0), (2, 0, cols, cols, cols, cols, cols)])
+    return pieces
+
+
+def attend_backward(
+    dp_size, layout, seg_hot, proj_c, proj_q, keys, values, rel_keys, bias, embed, vec_c, vec_q,
+    grad_c, grad_q, prob, content_t, query_t, table_t, small, g_down, g_up, g_out,
+):
+    seq_len, width = proj_c.shape
     pairs = width // PAIR
-    per_doc = lambda d, p: (d, 0, 0)
-    per_pair = lambda d, p: (d, 0, p)
-    shared = lambda d, p: (0, p)
-    tile = pl.BlockSpec((None, seq_len, PAIR), per_pair)
-    low = jax.ShapeDtypeStruct((docs, seq_len, width), jnp.bfloat16)
+    cols = width // 2
+    rows = width
+    count = len(layout) + 4
+    more = max(1, dp_size.bit_length() - 1 - FOLDS)
+    tiny = dp_size.bit_length()
+    low = jnp.bfloat16
+    dma = pltpu.SemaphoreType.DMA
+    whole = lambda g: (0, 0)
+    turn = lambda g: (g + pairs // 2) % pairs
+    per_pair = lambda g: (0, turn(g))
+    tile = pl.BlockSpec((seq_len, PAIR), per_pair)
+    once = pl.Buffered(1)
+    anywhere = pl.BlockSpec(memory_space=pl.ANY)
+    low_rows = jax.ShapeDtypeStruct((seq_len, width), low)
     return pl.pallas_call(
-        attend_backward_body,
+        functools.partial(attend_backward_body, dp_size, layout, count),
         out_shape=(
-            low, low, low, low,
-            jax.ShapeDtypeStruct((docs, width, 2 * seq_len), jnp.bfloat16),
-            jax.ShapeDtypeStruct((docs, 8, width), jnp.float32),
+            low_rows, low_rows, low_rows, low_rows,
+            jax.ShapeDtypeStruct((count, rows, cols), low),
+            jax.ShapeDtypeStruct(small.shape[1:], jnp.float32),
         ),
         grid_spec=pltpu.PrefetchScalarGridSpec(
             num_scalar_prefetch=0,
-            grid=(docs, pairs),
+            grid=(pairs,),
             in_specs=[
-                pl.BlockSpec((None, seq_len, PAIR), per_doc),
+                pl.BlockSpec((seq_len, PAIR), whole, pipeline_mode=once),
                 tile, tile, tile, tile,
-                pl.BlockSpec((2 * seq_len, PAIR), shared),
-                pl.BlockSpec((3, PAIR), shared),
-                pl.BlockSpec((2, PAIR), shared),
+                pl.BlockSpec((2 * seq_len, PAIR), per_pair),
+                pl.BlockSpec((3, PAIR), per_pair),
+                pl.BlockSpec((2, PAIR), per_pair),
                 tile, tile, tile, tile,
-                pl.BlockSpec((None, None, 2, 2, seq_len, seq_len), lambda d, p: (d, p, 0, 0, 0, 0)),
+                pl.BlockSpec((None, 2, 2, seq_len, seq_len), lambda g: (turn(g), 0, 0, 0, 0)),
+                pl.BlockSpec((width, seq_len), whole, pipeline_mode=once),
+                pl.BlockSpec((width, seq_len), whole, pipeline_mode=once),
+                pl.BlockSpec((width, 2 * seq_len), whole, pipeline_mode=once),
+                pl.BlockSpec(small.shape, lambda g: (0, 0, 0), pipeline_mode=once),
+                anywhere, anywhere, anywhere,
             ],
             out_specs=[
                 tile, tile, tile, tile,
-                pl.BlockSpec((None, PAIR, 2 * seq_len), lambda d, p: (d, p, 0)),
-                pl.BlockSpec((None, 8, PAIR), per_pair),
+                anywhere,
+                pl.BlockSpec(small.shape[1:], whole),
             ],
             scratch_shapes=[
-                pltpu.VMEM((seq_len, 2 * PAIR), jnp.bfloat16),
+                pltpu.VMEM((seq_len, 2 * PAIR), low),
                 pltpu.VMEM((PAIR, seq_len), jnp.float32),
                 pltpu.VMEM((PAIR, seq_len), jnp.float32),
                 pltpu.VMEM((PAIR, 2 * seq_len), jnp.float32),
+                pltpu.VMEM((count, rows, cols), low),
+                pltpu.VMEM((count, rows, cols), low),
+                pltpu.VMEM((count, rows, cols), low),
+                pltpu.VMEM((more, count, rows >> FOLDS, cols), low),
+                pltpu.VMEM((4, rows, cols), low),
+                pltpu.VMEM((tiny + 1,) + small.shape[1:], jnp.float32),
+                pltpu.VMEM(small.shape[1:], jnp.float32),
+                pltpu.VMEM((tiny,) + small.shape[1:], jnp.float32),
+                dma((count,)), dma((count,)), dma((count,)), dma((count,)),
+                dma((FOLDS, count)), dma((FOLDS, count)), dma((FOLDS, count)), dma((FOLDS, count)),
+                dma((more, count)), dma((more, count)), dma((tiny,)), dma((tiny,)),
             ],
         ),
+        compiler_params=pltpu.CompilerParams(
+            collective_id=0, has_side_effects=True, vmem_limit_bytes=60 << 20
+        ),
         name="attend_backward",
-    )(seg_hot, proj_c, proj_q, keys, values, rel_keys, bias, embed, vec_c, vec_q, grad_c, grad_q, prob)
+    )(
+        seg_hot, proj_c, proj_q, keys, values, rel_keys, bias, embed, vec_c, vec_q,
+        grad_c, grad_q, prob, content_t, query_t, table_t, small, g_down, g_up, g_out,
+    )
+
+
+def finish_body(counts, piece_ref, down_ref, up_ref, out_ref, query_ref, key_ref, value_ref, rel_ref):
+    down_count, up_count = counts
+    at = pl.program_id(0)
+    cols = piece_ref.shape[1]
+    value = piece_ref[...].astype(jnp.float32)
+    tail = down_count + up_count
+
+    @pl.when(at < down_count)
+    def _():
+        down_ref[...] = value
+
+    @pl.when((at >= down_count) & (at < tail))
+    def _():
+        up_ref[...] = value
+
+    @pl.when(at == tail)
+    def _():
+        out_ref[:, :cols] = value[:cols]
+        out_ref[:, cols:] = value[cols:]
+
+    for turn in range(3):
+        lanes = slice(turn * PAIR, (turn + 1) * PAIR)
+
+        @pl.when(at == tail + 1 + turn)
+        def _():
+            query_ref[:, lanes] = value[:, :PAIR]
+            key_ref[:, lanes] = value[:, PAIR : 2 * PAIR]
+            value_ref[:, lanes] = value[:, 2 * PAIR :]
+
+    @pl.when(at == tail + 4)
+    def _():
+        rel_ref[...] = value
+
+
+def finish(pieces, half_ff):
+    count, rows, cols = pieces.shape
+    down_count, up_count = 2 * (half_ff // rows), half_ff // cols
+    square = jax.ShapeDtypeStruct((rows, cols), jnp.float32)
+    whole = lambda p: (0, 0)
+    block = pl.BlockSpec((rows, cols), whole)
+
+    def down_at(p):
+        turn = jnp.minimum(p, down_count - 1)
+        return (turn // 2, turn % 2)
+
+    return pl.pallas_call(
+        functools.partial(finish_body, (down_count, up_count)),
+        out_shape=(
+            jax.ShapeDtypeStruct((half_ff, rows), jnp.float32),
+            jax.ShapeDtypeStruct((rows, half_ff), jnp.float32),
+            jax.ShapeDtypeStruct((cols, rows), jnp.float32),
+            square, square, square, square,
+        ),
+        grid=(count,),
+        in_specs=[pl.BlockSpec((None, rows, cols), lambda p: (p, 0, 0))],
+        out_specs=[
+            pl.BlockSpec((rows, cols), down_at),
+            pl.BlockSpec((rows, cols), lambda p: (0, jnp.clip(p - down_count, 0, up_count - 1))),
+            pl.BlockSpec((cols, rows), whole),
+            block, block, block, block,
+        ],
+        compiler_params=pltpu.CompilerParams(vmem_limit_bytes=40 << 20),
+        name="finish",
+    )(pieces)
 
 
 epsilon = 1e-06
@@ -282,6 +619,7 @@
 
 
 def on_device(
+    dp_size,
     content_in,
     query_in,
     doc_lengths,
@@ -400,62 +738,49 @@
     ff = up_weight.shape[1]
     cols = query_weight.shape[1]
 
-    def merge(left, right, axis):
-        if axis == 1:
-            split = right.shape[1] // 2
-            other = low_f(dot_left(left, right[:, split:]))
-            own = dot_left(left, right[:, :split])
-        else:
-            split = left.shape[1] // 2
-            other = low_f(dot_left(left[:, split:], right))
-            own = dot_left(left[:, :split], right)
-        return low_f(own + wide_f(swap(other)))
-
-    g_down = lax.psum(merge(act, grad_down, 0), "dp")
-    g_up = lax.psum(merge(first, grad_hidden, 1), "dp")
-    g_out = lax.psum(merge(vec, grad_mixed, 0), "dp")
-
-    gproj_c, gproj_q, gkeys, gvalues, grel, small = attend_backward(
-        seg_hot, proj_c, proj_q, keys, values, rel_keys, bias, embed, vec_c, vec_q,
-        grad_vec[None, :seq_len], grad_vec[None, seq_len:], prob,
-    )
-    gproj = jnp.concatenate([gproj_c[0], gproj_q[0]], axis=0)
-    g_query = lax.psum(merge(resid, gproj, 1), "dp")
-    g_key = lax.psum(merge(content, gkeys[0], 1), "dp")
-    g_value = lax.psum(merge(content, gvalues[0], 1), "dp")
-    g_rel = lax.psum(merge(table, jnp.transpose(grel[0]), 1), "dp")
+    g_down = low_f(dot_left(act, grad_down))
+    g_up = low_f(dot_left(first, grad_hidden))
+    g_out = low_f(dot_left(vec, grad_mixed))
+
+    up_rows = ff // cols
+    halves = jnp.concatenate([jnp.zeros((2, 5, cols), jnp.float32), g_up_bias.reshape(2, up_rows, cols)], axis=1)
+    same = jnp.stack([g_gain1, g_shift1, g_gain2, g_shift2, g_down_bias]).reshape(2 * 5, cols)
+    split_rows = 5 + up_rows
+    filler = jnp.zeros((2, (-split_rows - 10) % 8, cols), jnp.float32)
+    packed = jnp.concatenate([halves, jnp.stack([same, same]), filler], axis=1)
+    gproj_c, gproj_q, gkeys, gvalues, pieces, tiny = attend_backward(
+        dp_size, piece_layout(cols, ff), seg_hot[0], proj_c[0], proj_q[0], keys[0], values[0], rel_keys,
+        bias, embed, vec_c[0], vec_q[0], grad_vec[:seq_len], grad_vec[seq_len:], prob[0],
+        jnp.transpose(content), jnp.transpose(query), jnp.asarray(position_table(seq_len, width).T), packed,
+        g_down, g_up, g_out,
+    )
     content_grad = low_f(
-        nt(gproj_c[0], query_use) + nt(gkeys[0], key_use) + nt(gvalues[0], value_use) + grad_pre1[:seq_len]
-    )
-    query_grad = low_f(nt(gproj_q[0], query_use) + grad_pre1[seq_len:])
-
-    small = small[0]
-    pack_split = jnp.concatenate([small[:5].reshape(-1, 2, cols).transpose(1, 0, 2).reshape(2, -1), g_up_bias.reshape(2, ff)], axis=1)
-    pack_same = jnp.stack([g_gain1, g_shift1, g_gain2, g_shift2, g_down_bias]).reshape(-1)
-    got = swap(jnp.concatenate([pack_split[1], pack_same]))
-    tiny = lax.psum(jnp.concatenate([pack_split[0], pack_same]) + got, "dp")
-    at = 5 * cols
-    split_part = tiny[:at].reshape(5, cols)
-    same_part = tiny[at + ff :].reshape(5, width)
+        nt(gproj_c, query_use) + nt(gkeys, key_use) + nt(gvalues, value_use) + grad_pre1[:seq_len]
+    )
+    query_grad = low_f(nt(gproj_q, query_use) + grad_pre1[seq_len:])
+
+    down_sum, up_sum, out_sum, query_sum, key_sum, value_sum, rel_sum = finish(pieces, ff)
+    same_part = tiny[split_rows : split_rows + 10].reshape(5, width)
+    split_part = tiny[:5]
     return (
         return_doc(out_rows[:seq_len]),
         return_doc(out_rows[seq_len:]),
         return_doc(content_grad),
         return_doc(query_grad),
-        wide_f(g_query),
-        wide_f(g_key),
-        wide_f(g_value),
-        wide_f(g_out),
-        wide_f(g_rel),
+        query_sum,
+        key_sum,
+        value_sum,
+        out_sum,
+        rel_sum,
         split_part[0],
         split_part[1],
         split_part[2],
         split_part[3:5],
         same_part[0],
         same_part[1],
-        wide_f(g_up),
-        tiny[at : at + ff],
-        wide_f(g_down),
+        up_sum,
+        tiny[5:split_rows].reshape(ff),
+        down_sum,
         same_part[4],
         same_part[2],
         same_part[3],
@@ -491,7 +816,7 @@
         P("dp", "mp", None),
     )
     return jax.shard_map(
-        on_device,
+        functools.partial(on_device, mesh.shape["dp"]),
         mesh=mesh,
         in_specs=placed,
         out_specs=(

time: 531 us -> 405 us (0.76)
  waiting for transfers between devices: 140 us -> 0.12 us
  Pallas kernels: 91.8 us -> 198 us
  blocking collectives: 81.9 us -> 0 us
  local copies, waits for them, and re-layouts: 50.4 us -> 68.8 us
  between operations: 15.7 us -> 1.92 us
  other arithmetic: 41.5 us -> 29.5 us
    psum x1 -> x0, waiting for transfers between devices: 139 us -> none  [on_device(): g_query = lax.psum(merge(resid, gproj, 1), 'dp')]
    pallas_call x1 -> x2, Pallas kernels: 56.1 us -> 162 us  [the longest x1 153 us: attend_backward(): pl.pallas_call(functools.partial(attend_backward_body, dp_size, layout, c...]
    psum x1 -> x0, blocking collectives: 81.9 us -> none  [on_device(): tiny = lax.psum(jnp.concatenate([pack_split[0], pack_same]) + got, 'dp')]
    convert_element_type x12 -> x5, other arithmetic: 16.1 us -> 3.29 us  [on_device(): wide_f = lambda value: value.astype(jnp.float32)]
    dot_general x14 -> x3, matrix products: 32.4 us -> 19.9 us  [dot_left(): lax.dot_general(left_op, right_op, (((0,), (0,)), ((), ())), preferred_el...]
    dynamic_slice x0 -> x12, local copies, waits for them, and re-layouts: none -> 7.42 us  [the longest x8 3.74 us: gather_doc(): keep = lax.dynamic_index_in_dim(value, mine, 0, keepdims=False)]
    squeeze x4 -> x11, local copies, waits for them, and re-layouts: 3.4 us -> 10.2 us  [the longest x6 7.2 us: return_doc(): keep = lax.dynamic_index_in_dim(pair, mine, 0, keepdims=False)]
    reshape x3 -> x6, local copies, waits for them, and re-layouts: 3.41 us -> 9.61 us  [the longest x4 8.28 us: return_doc(): pair = value.reshape(2, half, width)]
  transfers between devices with their start and end apart: 26 -> 17, of which waited for: 2 -> 1; matrix products, arithmetic and copies ran while one was open for 20% -> 25% of each run, Pallas kernels for 7% -> 50%
where the time goes in v3:
time: 405 us; the launch traced here: 397 us
  Pallas kernels  198 us (49%)
  matrix products  93.5 us (23%)
  local copies, waits for them, and re-layouts  68.8 us (17%)
  other arithmetic  29.5 us (7%)
  starting transfers between devices  4.87 us (1%)
    pallas_call x1, Pallas kernels, attend_backward(): pl.pallas_call(functools.partial(attend_backward_body, dp_size, layout, c...  153 us
    dot_general x7, matrix products, nt(): lax.dot_general(left_op, right_op, (((1,), (1,)), ((), ())), preferred_el...  39.9 us
    pallas_call x1, Pallas kernels, attend_forward(): pl.pallas_call(attend_forward_body, out_shape=(jax.ShapeDtypeStruct((docs...  35.7 us
    dot_general x8, matrix products, nn(): return jnp.dot(left_op, right_op, preferred_element_type=jnp.float32)  33.7 us
    dot_general x3, matrix products, dot_left(): lax.dot_general(left_op, right_op, (((0,), (0,)), ((), ())), preferred_el...  19.9 us
    unnamed x134, local copies, waits for them, and re-layouts  18.2 us
    pallas_call x1, Pallas kernels, finish(): pl.pallas_call(functools.partial(finish_body, (down_count, up_count)), ou...  9.25 us
    reshape x4, local copies, waits for them, and re-layouts, return_doc(): pair = value.reshape(2, half, width)  8.28 us
  transfers between devices with their start and end apart: 17, of which 1 were waited for; matrix products, arithmetic and copies ran while one was open for 25% of the time, Pallas kernels for 50%

profile of v3, /device:TPU:0, one launch (start us, length us, event | category | flops | bytes accessed | tf_op | source)
XLA Modules:
  0.0 396.8 jit_solution(15540305435936608526)
XLA Ops:
  5.6 3.2 constant_dynamic-update-slice_fusion.11
  13.0 2.0 constant_dynamic-update-slice_fusion.7
  39.5 1.9 fusion.32.refs_1_
  43.2 2.0 fusion.20.refs_2_
  46.9 2.6 fusion.13.rel_ref.refs_5_
  49.5 35.7 %attend_forward.1 = (bf16[1,512,768]{2,1,0:T(8,128)(2,1)}, bf16[1,512,768]{2,1,0:T(8,128)(2,1)}, bf16[1,6,2,2,512,512]{5,4,3,2,1,0:T(8,128)(2,1)}) custom-call(s32[1]{0:T(128)} %dynamic_slice.63.len_ref, s32[1,512,1]{2,1,0:T(8,128)} %copy.73.rank_col, s32[1,1,512]{2,1,0:T(1,128)} %get-tuple-element.150.rank_row, s32[1,1,512]{2,1,0:T(1,128)} %fusion.24.live_row, ...), custom_call_target="tpu_custom_call" | custom-call | tf_op jit(solution)/shard_map/attend_forward/pallas_call | solution.py:98
  85.2 1.9 constant_dynamic-update-slice_fusion.6
  87.2 3.5 fusion.39
  91.1 2.1 constant_dynamic-update-slice_fusion.8
  93.2 8.6 %fusion.41 = f32[1024,3072]{1,0:T(8,128)} fusion(bf16[768,3072]{1,0:T(8,128)(2,1)S(1)} %constant_dynamic-update-slice_fusion.8, f32[1024,768]{0,1:T(8,128)S(1)} %get-tuple-element.153, f32[768]{0:T(1024)S(1)} %convert_element_type.93, f32[768]{0:T(1024)S(1)} %convert_element_type.92, f32[1024]{0:T(1024)S(1)} %fusion.22, f32[1024]{0:T(1024)S(1)} %broadcast_multiply_fusion.1), kind=kOutput, calls=%fused_computation.148 | convolution fusion | flops 4835770368 | bytes 20461568 | tf_op jit(solution)/shard_map/dot_general | solution.py:25
  103.7 11.8 %fusion.40 = (f32[1024]{0:T(1024)S(1)}, f32[1024,768]{0,1:T(8,128)S(1)}) fusion(f32[768]{0:T(1024)S(1)} %copy-done.40, bf16[3072,768]{1,0:T(8,128)(2,1)S(1)} %constant_dynamic-update-slice_fusion.10, f32[1024,3072]{1,0:T(8,128)} %fusion.41, f32[3072]{0:T(1024)S(1)} %bitcast.122, f32[768]{0:T(1024)S(1)} %convert_element_type.93, ...), kind=kOutput, calls=%fused_computation.147 | convolution fusion | flops 4870372352 | bytes 23626752 | tf_op jit(solution)/shard_map/dot_general | solution.py:25
  116.0 2.2 fusion.10
  118.2 2.9 fusion.35
  121.1 20.0 %convert_reduce_fusion = (f32[3072]{0:T(1024)}, bf16[1024,3072]{1,0:T(8,128)(2,1)}) fusion(f32[1024,3072]{1,0:T(8,128)} %fusion.41, f32[3072]{0:T(1024)S(1)} %bitcast.123, bf16[3072,768]{1,0:T(8,128)(2,1)} %copy-done.15, f32[1024,768]{0,1:T(8,128)} %get-tuple-element.106, f32[1024]{0:T(1024)S(1)} %negate_multiply_fusion.1), kind=kOutput, calls=%fused_computation.9 | convolution fusion | flops 4905759744 | bytes 26767360 | tf_op jit(solution)/shard_map/dot_general | solution.py:19
  141.1 2.3 add_reduce_fusion
  143.9 10.3 %convolution_convert_fusion.1.refs_17_ = bf16[3072,768]{1,0:T(8,128)(2,1)} fusion(f32[1024,768]{0,1:T(8,128)S(1)} %copy-done.3, f32[1024]{0:T(1024)S(1)} %negate_multiply_fusion.1, f32[1024,3072]{1,0:T(8,128)S(1)} %bitcast.96, f32[3072]{0:T(1024)S(1)} %bitcast.124), kind=kOutput, calls=%fused_computation.12 | convolution fusion | flops 4867227648 | bytes 20463616 | tf_op jit(solution)/shard_map/dot_general | solution.py:616
  154.3 9.1 %fusion.34 = (f32[768]{0:T(1024)}, f32[1024]{0:T(1024)S(1)}, f32[1024,768]{0,1:T(8,128)S(1)}) fusion(f32[768]{0:T(1024)S(1)} %convert_element_type.92, f32[1024,768]{0,1:T(8,128)S(1)} %get-tuple-element.153, f32[1024]{0:T(1024)S(1)} %broadcast_multiply_fusion.1, f32[1024,768]{0,1:T(8,128)S(1)} %copy-done.3, f32[1024]{0:T(1024)S(1)} %negate_multiply_fusion.1, ...), kind=kOutput, calls=%fused_computation.141 | convolution fusion | flops 4837341184 | bytes 20465664 | tf_op jit(solution)/shard_map/dot_general | solution.py:19
  163.3 7.1 %convolution_convert_fusion.refs_18_ = bf16[768,3072]{1,0:T(8,128)(2,1)} fusion(bf16[1024,3072]{1,0:T(8,128)(2,1)S(1)} %copy-done.52, f32[1024,768]{0,1:T(8,128)S(1)} %get-tuple-element.153, f32[768]{0:T(1024)S(1)} %convert_element_type.93, f32[768]{0:T(1024)S(1)} %convert_element_type.92, f32[1024]{0:T(1024)S(1)} %fusion.22, ...), kind=kOutput, calls=%fused_computation.11 | convolution fusion | flops 4838129664 | bytes 14170112 | tf_op jit(solution)/shard_map/dot_general | solution.py:616
  173.0 2.6 convolution_convert_fusion.3
  175.6 2.5 convolution_convert_fusion.4.refs_19_
  179.4 2.3 copy.118
  181.7 2.3 copy.117
  184.0 2.4 dynamic-slice_bitcast_fusion.5
  186.4 2.0 copy.79
  190.6 1.9 copy.83
  192.9 2.6 fusion.36
  201.6 153.1 %attend_backward.1 = (bf16[512,768]{1,0:T(8,128)(2,1)}, bf16[512,768]{1,0:T(8,128)(2,1)}, bf16[512,768]{1,0:T(8,128)(2,1)}, bf16[512,768]{1,0:T(8,128)(2,1)}, bf...) custom-call(bf16[512,128]{1,0:T(8,128)(2,1)} %and_convert_fusion.refs_0_, f32[512,768]{1,0:T(8,128)} %fusion.32.refs_1_, ...), custom_call_target="tpu_custom_call" | custom-call | tf_op jit(solution)/shard_map/attend_backward/pallas_call | solution.py:469
  354.7 3.2 fusion.11
  357.9 2.3 copy.120
  360.2 2.5 fusion.42
  369.9 3.2 copy-done.2
  373.1 9.2 %finish.1 = (f32[1536,768]{1,0:T(8,128)}, f32[768,1536]{1,0:T(8,128)}, f32[384,768]{1,0:T(8,128)}, f32[768,384]{1,0:T(8,128)}, f32[768,384]{1,0:T(8,128)}, /*index=5*/f32[768,384]{1,0:T(8,128)}, f32[768,384]{1,0:T(8,128)}) custom-call(bf16[13,768,384]{2,1,0:T(8,128)(2,1)S(1)} %copy-done.2), custom_call_target="tpu_custom_call" | custom-call | tf_op jit(solution)/shard_map/finish/pallas_call | solution.py:571
  (265 shorter events, 73.6 us)
Async XLA Ops:
  0.7 10.7 %copy-start = (s32[2,512]{1,0:T(2,128)S(1)}, s32[2,512]{1,0:T(2,128)}, u32[]{:S(2)}) copy-start(s32[2,512]{1,0:T(2,128)} %param.31) | copy-start | bytes 12292
  0.7 101.2 %collective-permute-start.10 = (bf16[1536,768]{1,0:T(8,128)(2,1)}, bf16[1536,768]{1,0:T(8,128)(2,1)}, u32[]{:S(2)}, u32[]{:S(2)}) collective-permute-start(bf16[1536,768]{1,0:T(8,128)(2,1)} %param.46), channel_id=1, source_target_pairs={{0,1},{1,0},{2,3},{3,2},{4,5},{5,4},{6,7},{7,6},{8,9},{9,8},{10,11... | collective-permute-start | bytes 7077896 | tf_op jit(solution)/shard_map/ppermute | solution.py:656
  1.2 89.8 %collective-permute-start.8 = (bf16[768,1536]{1,0:T(8,128)(2,1)}, bf16[768,1536]{1,0:T(8,128)(2,1)}, u32[]{:S(2)}, u32[]{:S(2)}) collective-permute-start(bf16[768,1536]{1,0:T(8,128)(2,1)} %param.44), channel_id=1, source_target_pairs={{0,1},{1,0},{2,3},{3,2},{4,5},{5,4},{6,7},{7,6},{8,9},{9,8},{10,11... | collective-permute-start | bytes 7077896 | tf_op jit(solution)/shard_map/ppermute | solution.py:656
  3.4 29.6 %collective-permute-start = (bf16[256,768]{0,1:T(8,128)(2,1)}, bf16[256,768]{0,1:T(8,128)(2,1)}, u32[]{:S(2)}, u32[]{:S(2)}) collective-permute-start(bf16[256,768]{0,1:T(8,128)(2,1)} %bitcast.5), channel_id=1, source_target_pairs={{0,1},{1,0},{2,3},{3,2},{4,5},{5,4},{6,7},{7,6},{8,9},{9,8},{10,11... | collective-permute-start | bytes 1179656 | tf_op jit(solution)/shard_map/ppermute | solution.py:656
  3.8 33.7 %collective-permute-start.1 = (bf16[768,384]{1,0:T(8,128)(2,1)}, bf16[768,384]{1,0:T(8,128)(2,1)}, u32[]{:S(2)}, u32[]{:S(2)}) collective-permute-start(bf16[768,384]{1,0:T(8,128)(2,1)} %param.33), channel_id=1, source_target_pairs={{0,1},{1,0},{2,3},{3,2},{4,5},{5,4},{6,7},{7,6},{8,9},{9,8},{10,11... | collective-permute-start | bytes 1769480 | tf_op jit(solution)/shard_map/ppermute | solution.py:656
  5.2 23.4 %collective-permute-start.9 = (f32[1,1536]{1,0:T(1,128)}, f32[1,1536]{1,0:T(1,128)}, u32[]{:S(2)}, u32[]{:S(2)}) collective-permute-start(f32[1,1536]{1,0:T(1,128)} %reshape.274), channel_id=1, source_target_pairs={{0,1},{1,0},{2,3},{3,2},{4,5},{5,4},{6,7},{7,6},{8,9},{9,8},{10,11... | collective-permute-start | bytes 18440 | tf_op jit(solution)/shard_map/ppermute | solution.py:656
  28.6 1.4 collective-permute-start.6
  30.0 5.3 %collective-permute-start.2 = (bf16[256,768]{0,1:T(8,128)(2,1)}, bf16[256,768]{0,1:T(8,128)(2,1)S(1)}, u32[]{:S(2)}, u32[]{:S(2)}) collective-permute-start(bf16[256,768]{0,1:T(8,128)(2,1)} %bitcast.119), channel_id=1, source_target_pairs={{0,1},{1,0},{2,3},{3,2},{4,5},{5,4},{6,7},{7,6},{8,9},{9,8},{10,11... | collective-permute-start | bytes 1179656 | tf_op jit(solution)/shard_map/ppermute | solution.py:656
  33.0 3.7 collective-permute-start.14
  34.2 11.0 %copy-start.9 = (bf16[256,768]{0,1:T(8,128)(2,1)}, bf16[256,768]{0,1:T(8,128)(2,1)S(1)}, u32[]{:S(2)}) copy-start(bf16[256,768]{0,1:T(8,128)(2,1)S(1)} %get-tuple-element.137) | copy-start | bytes 1179652
  35.2 1.8 collective-permute-start.13
  36.8 2.1 collective-permute-start.3
  37.0 48.2 %collective-permute-start.7 = (bf16[384,768]{1,0:T(8,128)(2,1)}, bf16[384,768]{1,0:T(8,128)(2,1)}, u32[]{:S(2)}, u32[]{:S(2)}) collective-permute-start(bf16[384,768]{1,0:T(8,128)(2,1)} %param.36), channel_id=1, source_target_pairs={{0,1},{1,0},{2,3},{3,2},{4,5},{5,4},{6,7},{7,6},{8,9},{9,8},{10,11... | collective-permute-start | bytes 1769480 | tf_op jit(solution)/shard_map/ppermute | solution.py:656
  37.5 5.6 %collective-permute-start.4 = (bf16[768,384]{1,0:T(8,128)(2,1)S(1)}, bf16[768,384]{1,0:T(8,128)(2,1)S(1)}, u32[]{:S(2)}, u32[]{:S(2)}) collective-permute-start(bf16[768,384]{1,0:T(8,128)(2,1)S(1)} %copy-done.26), channel_id=1, source_target_pairs={{0,1},{1,0},{2,3},{3,2},{4,5},{5,4},{6,7},{7,6},{8,9},{9,8},{10,11... | collective-permute-start | bytes 1769480 | tf_op jit(solution)/shard_map/ppermute | solution.py:656
  38.9 8.0 %collective-permute-start.5 = (bf16[768,384]{1,0:T(8,128)(2,1)S(1)}, bf16[768,384]{1,0:T(8,128)(2,1)S(1)}, u32[]{:S(2)}, u32[]{:S(2)}) collective-permute-start(bf16[768,384]{1,0:T(8,128)(2,1)S(1)} %copy-done.50), channel_id=1, source_target_pairs={{0,1},{1,0},{2,3},{3,2},{4,5},{5,4},{6,7},{7,6},{8,9},{9,8},{10,11... | collective-permute-start | bytes 1769480 | tf_op jit(solution)/shard_map/ppermute | solution.py:656
  49.5 37.7 %copy-start.10 = (bf16[256,768]{0,1:T(8,128)(2,1)S(1)}, bf16[256,768]{0,1:T(8,128)(2,1)}, u32[]{:S(2)}) copy-start(bf16[256,768]{0,1:T(8,128)(2,1)} %copy-done.9) | copy-start | bytes 1179652
  49.5 37.7 %copy-start.12 = (bf16[256,768]{0,1:T(8,128)(2,1)S(1)}, bf16[256,768]{0,1:T(8,128)(2,1)}, u32[]{:S(2)}) copy-start(bf16[256,768]{0,1:T(8,128)(2,1)} %copy-done.11) | copy-start | bytes 1179652
  49.5 37.7 %copy-start.14 = (bf16[256,768]{0,1:T(8,128)(2,1)S(1)}, bf16[256,768]{0,1:T(8,128)(2,1)}, u32[]{:S(2)}) copy-start(bf16[256,768]{0,1:T(8,128)(2,1)} %copy-done.13) | copy-start | bytes 1179652
  91.1 10.8 %slice-start.7 = ((s8[4718592]{0:T(1024)(128)(4,1)}), s8[4194304]{0:T(1024)(128)(4,1)S(1)}, s32[]{:S(2)}) async-start(s8[4718592]{0:T(1024)(128)(4,1)} %bitcast.109), calls=%async_computation.7 | async-start | bytes 8388608
  103.7 11.8 %copy-start.15 = (bf16[3072,768]{1,0:T(8,128)(2,1)}, bf16[3072,768]{1,0:T(8,128)(2,1)S(1)}, u32[]{:S(2)}) copy-start(bf16[3072,768]{1,0:T(8,128)(2,1)S(1)} %constant_dynamic-update-slice_fusion.10) | copy-start | bytes 14155780
  118.2 25.2 %slice-start = ((s8[12582912]{0:T(1024)(128)(4,1)}), s8[4194304]{0:T(1024)(128)(4,1)S(1)}, s32[]{:S(2)}) async-start(s8[12582912]{0:T(1024)(128)(4,1)} %bitcast.95), calls=%async_computation | async-start | bytes 8388608
  121.1 22.3 %slice-start.1 = ((s8[12582912]{0:T(1024)(128)(4,1)}), s8[4194304]{0:T(1024)(128)(4,1)S(1)}, s32[]{:S(2)}) async-start(s8[12582912]{0:T(1024)(128)(4,1)} %bitcast.95), calls=%async_computation.1 | async-start | bytes 8388608
  121.1 22.3 %slice-start.2 = ((s8[12582912]{0:T(1024)(128)(4,1)}), s8[4194304]{0:T(1024)(128)(4,1)S(1)}, s32[]{:S(2)}) async-start(s8[12582912]{0:T(1024)(128)(4,1)} %bitcast.95), calls=%async_computation.2 | async-start | bytes 8388608
  141.1 13.2 %slice-start.5 = ((s8[4718592]{0:T(1024)(128)(4,1)}), s8[4194304]{0:T(1024)(128)(4,1)S(1)}, s32[]{:S(2)}) async-start(s8[4718592]{0:T(1024)(128)(4,1)} %bitcast.99), calls=%async_computation.5 | async-start | bytes 8388608
  143.9 10.3 %slice-start.6 = ((s8[4718592]{0:T(1024)(128)(4,1)}), s8[524288]{0:T(1024)(128)(4,1)S(1)}, s32[]{:S(2)}) async-start(s8[4718592]{0:T(1024)(128)(4,1)} %bitcast.99), calls=%async_computation.6 | async-start | bytes 1048576
  186.4 9.7 %copy-start.36 = (f32[768]{0:T(1024)S(1)}, f32[768]{0:T(1024)}, u32[]{:S(2)}) copy-start(f32[768]{0:T(1024)} %get-tuple-element.97) | copy-start | bytes 9220
  186.4 10.3 %copy-start.35 = (f32[768]{0:T(1024)S(1)}, f32[768]{0:T(1024)}, u32[]{:S(2)}) copy-start(f32[768]{0:T(1024)} %get-tuple-element.101) | copy-start | bytes 9220
  189.3 197.8 %collective-permute-start.11 = (bf16[256,768]{0,1:T(8,128)(2,1)}, bf16[256,768]{0,1:T(8,128)(2,1)}, u32[]{:S(2)}, u32[]{:S(2)}) collective-permute-start(bf16[256,768]{0,1:T(8,128)(2,1)} %copy.78), channel_id=1, source_target_pairs={{0,1},{1,0},{2,3},{3,2},{4,5},{5,4},{6,7},{7,6},{8,9},{9,8},{10,11... | collective-permute-start | bytes 1179656 | tf_op jit(solution)/shard_map/ppermute | solution.py:656
  192.6 196.9 %collective-permute-start.12 = (bf16[256,768]{0,1:T(8,128)(2,1)}, bf16[256,768]{0,1:T(8,128)(2,1)}, u32[]{:S(2)}, u32[]{:S(2)}) collective-permute-start(bf16[256,768]{0,1:T(8,128)(2,1)} %copy.83), channel_id=1, source_target_pairs={{0,1},{1,0},{2,3},{3,2},{4,5},{5,4},{6,7},{7,6},{8,9},{9,8},{10,11... | collective-permute-start | bytes 1179656 | tf_op jit(solution)/shard_map/ppermute | solution.py:656
  368.9 22.8 %collective-permute-start.15 = (bf16[256,768]{0,1:T(8,128)(2,1)S(1)}, bf16[256,768]{0,1:T(8,128)(2,1)}, u32[]{:S(2)}, u32[]{:S(2)}) collective-permute-start(bf16[256,768]{0,1:T(8,128)(2,1)S(1)} %copy.96), channel_id=1, source_target_pairs={{0,1},{1,0},{2,3},{3,2},{4,5},{5,4},{6,7},{7,6},{8,9},{9,8},{10,11... | collective-permute-start | bytes 1179656 | tf_op jit(solution)/shard_map/ppermute | solution.py:656
  369.3 24.7 %collective-permute-start.16 = (bf16[256,768]{0,1:T(8,128)(2,1)S(1)}, bf16[256,768]{0,1:T(8,128)(2,1)}, u32[]{:S(2)}, u32[]{:S(2)}) collective-permute-start(bf16[256,768]{0,1:T(8,128)(2,1)S(1)} %copy.102), channel_id=1, source_target_pairs={{0,1},{1,0},{2,3},{3,2},{4,5},{5,4},{6,7},{7,6},{8,9},{9,8},{10,11... | collective-permute-start | bytes 1179656 | tf_op jit(solution)/shard_map/ppermute | solution.py:656
  373.1 14.1 %copy-start.8 = (bf16[256,768]{0,1:T(8,128)(2,1)S(1)}, bf16[256,768]{0,1:T(8,128)(2,1)}, u32[]{:S(2)}) copy-start(bf16[256,768]{0,1:T(8,128)(2,1)} %copy.79) | copy-start | bytes 1179652
  (47 other events, 207.5 us)

commit v4 on v3

v4 whole, which is shorter than its diff:
```python
import functools

import jax
import jax.numpy as jnp
import ml_dtypes
import numpy as np
from jax import lax
from jax.experimental import pallas as pl
from jax.experimental.pallas import tpu as pltpu
from jax.sharding import PartitionSpec as P

epsilon = 1e-06
DH = 64
PAIR = 2 * DH
ROWS = 256
NEG = -1e30


def nt(left_op, right_op):
    return lax.dot_general(
        left_op, right_op, (((1,), (1,)), ((), ())), preferred_element_type=jnp.float32
    )


def nn(left_op, right_op):
    return jnp.dot(left_op, right_op, preferred_element_type=jnp.float32)


def lane_ids(rows):
    return lax.broadcasted_iota(jnp.int32, (rows, PAIR), 1)


def attend_forward_body(
    len_ref, rank_col, rank_row, live_row, seg_hot, proj_c, proj_q, key_ref, value_ref, rel_ref,
    bias_ref, embed_ref, vec_c, vec_q, prob_ref, mask_scr, ext_scr,
):
    seq_len = key_ref.shape[0]
    blocks = seq_len // ROWS
    wide = seq_len + ROWS

    @pl.when(pl.program_id(1) == 0)
    def _():
        length = len_ref[pl.program_id(0)]
        for block in range(blocks):
            rows = pl.ds(block * ROWS, ROWS)
            place_j = lax.broadcasted_iota(jnp.int32, (ROWS, seq_len), 1)
            place_i = lax.broadcasted_iota(jnp.int32, (ROWS, seq_len), 0) + block * ROWS
            visible = (place_j < length) & (
                (live_row[...] == 0) | (rank_row[...] < rank_col[rows, :])
            )
            diagonal = place_i == place_j
            mask_scr[0, rows, :] = jnp.where(visible | diagonal, 0.0, NEG)
            mask_scr[1, rows, :] = jnp.where(visible & jnp.logical_not(diagonal), 0.0, NEG)

    ext_scr[:, :PAIR] = key_ref[...]
    ext_scr[:, PAIR:] = seg_hot[...]
    lane = lane_ids(ROWS)
    diff = embed_ref[0:1, :] - embed_ref[1:2, :]
    for stream in range(2):
        proj_ref = (proj_c, proj_q)[stream]
        vec_ref = (vec_c, vec_q)[stream]
        for block in range(blocks):
            rows = pl.ds(block * ROWS, ROWS)
            proj = proj_ref[rows, :]
            query_c = ((proj + bias_ref[0:1, :]) * 0.125).astype(jnp.bfloat16)
            query_p = ((proj + bias_ref[1:2, :]) * 0.125).astype(jnp.bfloat16)
            seg_gap = (proj + bias_ref[2:3, :]) * (diff * 0.125)
            hot = seg_hot[rows, :].astype(jnp.float32)
            window = rel_ref[pl.ds(seq_len - (block + 1) * ROWS, wide), :]
            vec_pair = None
            for head in range(2):
                own = (lane >= DH) if head else (lane < DH)
                zero = jnp.zeros((), jnp.bfloat16)
                gap = jnp.sum(jnp.where(own, seg_gap, 0.0), axis=1, keepdims=True)
                gap_high = gap.astype(jnp.bfloat16).astype(jnp.float32)
                seg_part = (jnp.where(lane < 4, gap_high, gap - gap_high) * hot).astype(jnp.bfloat16)
                left = jnp.concatenate([jnp.where(own, query_c, zero), seg_part], axis=1)
                scores = nt(left, ext_scr[...])
                table = nt(jnp.where(own, query_p, zero), window)
                table = pltpu.roll(table, 1, 1, stride=1, stride_axis=0)
                scores = scores + table[:, ROWS:] + mask_scr[stream, rows, :]
                top = jnp.max(scores, axis=1, keepdims=True)
                terms = jnp.exp(scores - top)
                total = jnp.sum(terms, axis=1, keepdims=True)
                prob = (terms * (1.0 / total)).astype(jnp.bfloat16)
                prob_ref[stream, head, rows, :] = prob
                part = nn(prob, value_ref[...])
                vec_pair = part if head == 0 else jnp.where(own, part, vec_pair)
            vec_ref[rows, :] = vec_pair.astype(jnp.bfloat16)


def attend_forward(lengths, rank_col, rank_row, live_row, seg_hot, proj_c, proj_q, keys, values, rel_keys, bias, embed):
    docs, seq_len, width = proj_c.shape
    pairs = width // PAIR
    per_doc = lambda d, p, *_: (d, 0, 0)
    per_pair = lambda d, p, *_: (d, 0, p)
    shared = lambda d, p, *_: (0, p)
    tile = pl.BlockSpec((None, seq_len, PAIR), per_pair)
    return pl.pallas_call(
        attend_forward_body,
        out_shape=(
            jax.ShapeDtypeStruct((docs, seq_len, width), jnp.bfloat16),
            jax.ShapeDtypeStruct((docs, seq_len, width), jnp.bfloat16),
            jax.ShapeDtypeStruct((docs, pairs, 2, 2, seq_len, seq_len), jnp.bfloat16),
        ),
        grid_spec=pltpu.PrefetchScalarGridSpec(
            num_scalar_prefetch=1,
            grid=(docs, pairs),
            in_specs=[
                pl.BlockSpec((None, seq_len, 1), per_doc),
                pl.BlockSpec((None, 1, seq_len), per_doc),
                pl.BlockSpec((None, 1, seq_len), per_doc),
                pl.BlockSpec((None, seq_len, PAIR), per_doc),
                tile, tile, tile, tile,
                pl.BlockSpec((2 * seq_len, PAIR), shared),
                pl.BlockSpec((3, PAIR), shared),
                pl.BlockSpec((2, PAIR), shared),
            ],
            out_specs=[
                tile, tile,
                pl.BlockSpec((None, None, 2, 2, seq_len, seq_len), lambda d, p, *_: (d, p, 0, 0, 0, 0)),
            ],
            scratch_shapes=[
                pltpu.VMEM((2, seq_len, seq_len), jnp.float32),
                pltpu.VMEM((seq_len, 2 * PAIR), jnp.bfloat16),
            ],
        ),
        name="attend_forward",
    )(lengths, rank_col, rank_row, live_row, seg_hot, proj_c, proj_q, keys, values, rel_keys, bias, embed)


GELU_A = 0.7978845608028654
GELU_B = 0.044715


def norm_parts(value_in):
    center = value_in - jnp.mean(value_in, axis=1, keepdims=True)
    scale = lax.rsqrt(jnp.mean(center * center, axis=1, keepdims=True) + epsilon)
    return center * scale, scale


def norm_pull(normal, scale, grad):
    return scale * (
        grad
        - jnp.mean(grad, axis=1, keepdims=True)
        - normal * jnp.mean(grad * normal, axis=1, keepdims=True)
    )


def feed_forward_body(
    vec_c, vec_q, content, query, cot_c, cot_q, out_ref, up_ref, down_ref, up_bias, norms,
    first_t, normal_ref, scale_ref, act_ref, slope_ref, grad_ref, low_ref, low_t, rows_ref, sums_ref,
    first_scr, total_scr,
):
    step = pl.program_id(0)
    half_rows = vec_c.shape[0]
    chunks = [(s, at) for s in range(2) for at in range(0, half_rows, ROWS)]

    @pl.when(step == 0)
    def _():
        for stream, at in chunks:
            here = pl.ds(at, ROWS)
            there = slice(stream * half_rows + at, stream * half_rows + at + ROWS)
            mixed = nn((vec_c, vec_q)[stream][here, :], out_ref[...])
            mixed = mixed + (content, query)[stream][here, :].astype(jnp.float32)
            normal, scale = norm_parts(mixed)
            first = (normal * norms[0:1, :] + norms[1:2, :]).astype(jnp.bfloat16)
            first_scr[there, :] = first
            first_t[:, there] = jnp.transpose(first)
            normal_ref[there, :] = normal.astype(jnp.bfloat16)
            scale_ref[there, :] = scale
            total_scr[there, :] = first.astype(jnp.float32) + norms[4:5, :]

    for stream, at in chunks:
        there = slice(stream * half_rows + at, stream * half_rows + at + ROWS)
        value = nn(first_scr[there, :], up_ref[...]) + up_bias[...]
        square = value * value
        half = 0.5 + 0.5 * jnp.tanh(value * (GELU_A + (GELU_A * GELU_B) * square))
        wide = value * half
        act = wide.astype(jnp.bfloat16)
        slope = half + (wide * (1.0 - half)) * ((2.0 * GELU_A) + (6.0 * GELU_A * GELU_B) * square)
        act_ref[there, :] = act
        slope_ref[there, :] = slope.astype(jnp.bfloat16)
        total_scr[there, :] += nn(act, down_ref[...])

    @pl.when(step == pl.num_programs(0) - 1)
    def _():
        sums = [jnp.zeros((1, content.shape[1]), jnp.float32) for _ in range(3)]
        for stream, at in chunks:
            here = pl.ds(at, ROWS)
            there = slice(stream * half_rows + at, stream * half_rows + at + ROWS)
            normal, scale = norm_parts(total_scr[there, :])
            rows_ref[there, :] = (normal * norms[2:3, :] + norms[3:4, :]).astype(jnp.bfloat16)
            cot = (cot_c, cot_q)[stream][here, :].astype(jnp.float32)
            grad = norm_pull(normal, scale, cot * norms[2:3, :])
            grad_ref[there, :] = grad
            low = grad.astype(jnp.bfloat16)
            low_ref[there, :] = low
            low_t[:, there] = jnp.transpose(low)
            for at_sum, term in enumerate((cot * normal, cot, grad)):
                sums[at_sum] = sums[at_sum] + jnp.sum(term, axis=0, keepdims=True)
        sums_ref[...] = jnp.concatenate(sums + [jnp.zeros((5, content.shape[1]), jnp.float32)], axis=0)


def feed_forward(vec_c, vec_q, content, query, cot_c, cot_q, out_use, up_use, down_use, up_bias, norms):
    seq_len, width = content.shape
    hidden = up_use.shape[1]
    cols = width // 2
    rows = 2 * seq_len
    low = jnp.bfloat16
    once = pl.Buffered(1)
    whole = lambda f: (0, 0)
    side = lambda f: (0, f)
    keep = lambda shape: pl.BlockSpec(shape, whole, pipeline_mode=once)
    stream = keep((seq_len, width))
    return pl.pallas_call(
        feed_forward_body,
        out_shape=(
            jax.ShapeDtypeStruct((width, rows), low),
            jax.ShapeDtypeStruct((rows, width), low),
            jax.ShapeDtypeStruct((rows, 1), jnp.float32),
            jax.ShapeDtypeStruct((rows, hidden), low),
            jax.ShapeDtypeStruct((rows, hidden), low),
            jax.ShapeDtypeStruct((rows, width), jnp.float32),
            jax.ShapeDtypeStruct((rows, width), low),
            jax.ShapeDtypeStruct((width, rows), low),
            jax.ShapeDtypeStruct((rows, width), low),
            jax.ShapeDtypeStruct((8, width), jnp.float32),
        ),
        grid=(hidden // cols,),
        in_specs=[
            stream, stream, stream, stream, stream, stream,
            keep((width, width)),
            pl.BlockSpec((width, cols), side),
            pl.BlockSpec((cols, width), lambda f: (f, 0)),
            pl.BlockSpec((1, cols), side),
            keep((8, width)),
        ],
        out_specs=[
            pl.BlockSpec((width, rows), whole),
            pl.BlockSpec((rows, width), whole),
            pl.BlockSpec((rows, 1), whole),
            pl.BlockSpec((rows, cols), side),
            pl.BlockSpec((rows, cols), side),
            pl.BlockSpec((rows, width), whole),
            pl.BlockSpec((rows, width), whole),
            pl.BlockSpec((width, rows), whole),
            pl.BlockSpec((rows, width), whole),
            pl.BlockSpec((8, width), whole),
        ],
        scratch_shapes=[
            pltpu.VMEM((rows, width), low),
            pltpu.VMEM((rows, width), jnp.float32),
        ],
        compiler_params=pltpu.CompilerParams(vmem_limit_bytes=60 << 20),
        name="feed_forward",
    )(vec_c, vec_q, content, query, cot_c, cot_q, out_use, up_use, down_use, up_bias, norms)


MESH = pl.DeviceIdType.MESH
FOLDS = 4
LAG = 2
EARLY = 9
COUNT = 13


def shear_left(value_in):
    rows, wide = value_in.shape
    pack = 16
    groups = []
    for group in range(rows // pack):
        piece = value_in[group * pack : (group + 1) * pack]
        groups.append(pltpu.roll(piece, wide - 1 - group * pack, 1))
    moved = jnp.concatenate(groups, axis=0)
    place = lax.broadcasted_iota(jnp.int32, (rows, wide), 0)
    step = 1
    while step < pack:
        moved = jnp.where((place & step) != 0, pltpu.roll(moved, wide - step, 1), moved)
        step = step * 2
    return moved


def backward_body(dp_size, *refs):
    (
        seg_hot, proj_c, proj_q, key_ref, value_ref, rel_ref, bias_ref, embed_ref, prob_ref,
        query_w, key_w, value_w, vec_c, vec_q, content_t, query_t, table_t, out_w,
        act_ref, slope_ref, up_ref, down_ref, low_ref, low_t, first_t, normal_ref, scale_ref,
        norms, sums_in, grad_in, rows_in,
        sum_out, small_out, keep_out, rows_came, grad_came,
        vt_scr, key_acc, value_acc, rel_acc, total, vec_grad, hid_scr,
        work, swapped, landed, extra, small_work, small_far, small_land,
        store_sem, swap_send, swap_recv, fold_send, fold_recv, spread_send, spread_recv,
        more_send, more_recv, tiny_send, tiny_recv, grad_sem, keep_sem, back_send, back_recv,
    ) = refs
    gproj_c = hid_scr.at[: key_ref.shape[0], :]
    gproj_q = hid_scr.at[key_ref.shape[0] :, :PAIR]
    ext_scr = hid_scr.at[key_ref.shape[0] :, PAIR:]
    grid_at = pl.program_id(0)
    feeds = 8
    pairs = 6
    half_pairs = pairs // 2
    last = pl.num_programs(0) - 1
    rows, cols = work.shape[1:]
    seq_len = key_ref.shape[0]
    place = lax.axis_index("dp")
    core = lax.axis_index("mp")
    strides = [1 + core, 2 - core, 4, 8]
    more = [16 << step for step in range(8) if (16 << step) < dp_size]
    bits = [(place // stride) % 2 for stride in strides]
    partners = [place + (1 - 2 * bit) * stride for bit, stride in zip(bits, strides)]
    more_partners = [place + (1 - 2 * ((place // stride) % 2)) * stride for stride in more]
    lengths = [rows >> (fold + 1) for fold in range(FOLDS)]
    starts, begin = [], 0
    for bit, length in zip(bits, lengths):
        begin = begin + bit * length
        starts.append(begin)
    land_at = [rows - 2 * length for length in lengths]
    offsets = [number * LAG for number in range(2 * FOLDS + 1)]
    final_slot = 20

    def kept(fold):
        return pl.ds(pl.multiple_of(starts[fold], 16), lengths[fold])

    def given(fold):
        return pl.ds(pl.multiple_of(starts[fold] + (1 - 2 * bits[fold]) * lengths[fold], 16), lengths[fold])

    def remote(source, target, send, recv, device):
        return pltpu.make_async_remote_copy(
            src_ref=source, dst_ref=target, send_sem=send, recv_sem=recv,
            device_id=device, device_id_type=MESH,
        )

    def swap_copy(piece):
        return remote(
            work.at[piece], swapped.at[piece], swap_send.at[piece], swap_recv.at[piece], {"mp": 1 - core}
        )

    def fold_copy(fold, piece):
        return remote(
            work.at[piece, given(fold)],
            landed.at[piece, pl.ds(land_at[fold], lengths[fold])],
            fold_send.at[fold, piece], fold_recv.at[fold, piece], {"dp": partners[fold]},
        )

    def spread_copy(fold, piece):
        return remote(
            swapped.at[piece, kept(fold)],
            swapped.at[piece, kept(fold)],
            spread_send.at[fold, piece], spread_recv.at[fold, piece], {"dp": partners[fold]},
        )

    def extra_ref(step, piece):
        if step == 0:
            return landed.at[piece, pl.ds(rows - lengths[-1], lengths[-1])]
        return extra.at[step - 1, piece]

    def more_copy(step, piece):
        return remote(
            work.at[piece, kept(FOLDS - 1)],
            extra_ref(step, piece),
            more_send.at[step, piece], more_recv.at[step, piece], {"dp": more_partners[step]},
        )

    def store(piece):
        return pltpu.make_async_copy(swapped.at[piece], sum_out.at[piece], store_sem.at[piece])

    def add_rows(piece, where, other):
        mine = work[piece, where, :].astype(jnp.float32)
        work[piece, where, :] = (mine + other.astype(jnp.float32)).astype(jnp.bfloat16)

    tiny_devices = [{"mp": 1 - core}] + [{"dp": partner} for partner in partners + more_partners]

    def tiny_copy(step):
        return remote(
            small_far if step == 0 else small_work.at[step],
            small_land.at[step], tiny_send.at[step], tiny_recv.at[step], tiny_devices[step],
        )

    far_rows = (1 - core) * ROWS

    def rows_copy(stream):
        return remote(
            rows_in.at[pl.ds(pl.multiple_of(stream * seq_len + far_rows, ROWS), ROWS)], rows_came.at[stream],
            back_send.at[stream], back_recv.at[stream], {"mp": 1 - core},
        )

    def grad_copy(stream):
        return remote(
            vec_grad.at[pl.ds(pl.multiple_of(stream * seq_len + far_rows, ROWS), ROWS)], grad_came.at[stream],
            back_send.at[2 + stream], back_recv.at[2 + stream], {"mp": 1 - core},
        )

    def keep_copy(stream):
        return pltpu.make_async_copy(
            vec_grad.at[pl.ds(pl.multiple_of(stream * seq_len + core * ROWS, ROWS), ROWS)],
            keep_out.at[stream], keep_sem.at[stream],
        )

    grad_load = pltpu.make_async_copy(grad_in, total, grad_sem)

    def stage(number, piece):
        if number == 0:
            fold_copy(0, piece).start()
        elif number <= FOLDS:
            fold = number - 1
            fold_copy(fold, piece).wait_recv()
            add_rows(piece, kept(fold), landed[piece, pl.ds(land_at[fold], lengths[fold]), :])
            if fold + 1 < FOLDS:
                fold_copy(fold + 1, piece).start()
                return
            for step in range(len(more)):
                more_copy(step, piece).start()
                more_copy(step, piece).wait()
                add_rows(piece, kept(fold), extra_ref(step, piece)[...])
            swapped[piece, kept(fold), :] = work[piece, kept(fold), :]
            spread_copy(fold, piece).start()
        else:
            fold = 2 * FOLDS - number
            remote(
                swapped.at[piece, kept(fold)], swapped.at[piece, given(fold)],
                spread_send.at[fold, piece], spread_recv.at[fold, piece], {"dp": partners[fold]},
            ).wait_recv()
            if fold > 0:
                spread_copy(fold - 1, piece).start()
            else:
                store(piece).start()

    def advance(tick):
        for number in reversed(range(2 * FOLDS + 1)):
            slot = tick - offsets[number]
            piece = jnp.where(slot < EARLY, slot, EARLY + (slot - 14) // 2)

            @pl.when(
                (slot >= 0)
                & ((slot < EARLY) | (slot == 15) | (slot == 17) | (slot == 19) | (slot == final_slot))
            )
            def _():
                stage(number, piece)

    def settle(piece):
        swap_copy(piece).wait_recv()
        add_rows(piece, pl.ds(0, rows), swapped[piece])

    @pl.when(grid_at == 0)
    def _():
        barrier = pltpu.get_barrier_semaphore()
        for device in tiny_devices:
            pl.semaphore_signal(barrier, inc=1, device_id=device, device_id_type=MESH)
        pl.semaphore_wait(barrier, len(tiny_devices))
        grad_load.start()
        rows_copy(0).start()
        rows_copy(1).start()
        small_work[0] = jnp.zeros_like(small_work[0])
        small_far[...] = jnp.zeros_like(small_far)
        for at in range(3):
            for side in range(2):
                line = sums_in[at : at + 1, side * cols : (side + 1) * cols]
                spot = slice(13 + 2 * at + side, 14 + 2 * at + side)
                small_work[0, spot, :] = line
                small_far[spot, :] = line
        grad_load.wait()

    @pl.when(grid_at < feeds)
    def _():
        chunk = grid_at // 2
        near = grid_at % 2 == 1
        bias_sum = jnp.zeros((1, cols), jnp.float32)
        for at in range(0, total.shape[0], ROWS):
            here = slice(at, at + ROWS)
            grad_act = nt(low_ref[here, :], down_ref[...])
            hid = (grad_act * slope_ref[here, :].astype(jnp.float32)).astype(jnp.bfloat16)
            hid_scr[here, :] = hid
            bias_sum = bias_sum + jnp.sum(hid.astype(jnp.float32), axis=0, keepdims=True)
            total[here, :] += nt(hid, up_ref[...])

        @pl.when(near)
        def _():
            swap_copy(2 * chunk).wait_send()
            swap_copy(2 * chunk + 1).wait_send()

        for at in range(0, rows, ROWS):
            here = slice(at, at + ROWS)
            work[2 * chunk, here, :] = nn(low_t[here, :], act_ref[...]).astype(jnp.bfloat16)
            work[2 * chunk + 1, here, :] = nn(first_t[here, :], hid_scr[...]).astype(jnp.bfloat16)

        @pl.when(near)
        def _():
            small_work[0, pl.ds(5 + chunk, 1), :] = bias_sum
            settle(2 * chunk)
            settle(2 * chunk + 1)

        @pl.when(jnp.logical_not(near))
        def _():
            small_far[pl.ds(5 + chunk, 1), :] = bias_sum
            swap_copy(2 * chunk).start()
            swap_copy(2 * chunk + 1).start()

    @pl.when(grid_at == feeds)
    def _():
        sums = [jnp.zeros((1, 2 * cols), jnp.float32) for _ in range(2)]
        out_piece = EARLY - 1
        near_sum = jnp.zeros((rows, cols), jnp.float32)
        far_sum = jnp.zeros((rows, cols), jnp.float32)
        for at in range(0, total.shape[0], ROWS):
            here = slice(at, at + ROWS)
            normal = normal_ref[here, :].astype(jnp.float32)
            grad = total[here, :]
            sums[0] = sums[0] + jnp.sum(grad * normal, axis=0, keepdims=True)
            sums[1] = sums[1] + jnp.sum(grad, axis=0, keepdims=True)
            grad = norm_pull(normal, scale_ref[here, :], grad * norms[0:1, :])
            total[here, :] = grad
            low = grad.astype(jnp.bfloat16)
            hid_scr[here, :] = low[:, :cols]
            vec_grad[here, :] = low
        for at in range(0, total.shape[0], ROWS):
            here = slice(at, at + ROWS)
            low = vec_grad[here, :]
            low_turn = jnp.transpose(low)
            vec = (vec_c, vec_q)[at // seq_len][at % seq_len : at % seq_len + ROWS, :]
            far_sum = far_sum + nn(low_turn, vec[:, cols:])
            near_sum = near_sum + nn(low_turn, vec[:, :cols])
            vec_grad[here, :] = nt(low, out_w[...]).astype(jnp.bfloat16)
        work[out_piece] = far_sum.astype(jnp.bfloat16)
        swap_copy(out_piece).start()
        for at in range(2):
            for side in range(2):
                line = sums[at][:, side * cols : (side + 1) * cols]
                spot = slice(9 + 2 * at + side, 10 + 2 * at + side)
                small_work[0, spot, :] = line
                small_far[spot, :] = line
        swap_copy(out_piece).wait()
        work[out_piece] = (near_sum + swapped[out_piece].astype(jnp.float32)).astype(jnp.bfloat16)

    @pl.when(grid_at > feeds)
    def _():
        turn = grid_at - feeds - 1
        pair = (turn + half_pairs) % pairs
        pair_lanes = pl.ds(pl.multiple_of(pair * PAIR, PAIR), PAIR)
        blocks = seq_len // ROWS
        wide = seq_len + ROWS
        ext_scr[:, :PAIR] = (key_ref[...].astype(jnp.float32) * 0.125).astype(jnp.bfloat16)
        ext_scr[:, PAIR:] = (seg_hot[...].astype(jnp.float32) * 0.125).astype(jnp.bfloat16)
        vt_scr[...] = jnp.transpose(value_ref[...])
        key_acc[...] = jnp.zeros_like(key_acc)
        value_acc[...] = jnp.zeros_like(value_acc)
        rel_acc[...] = jnp.zeros_like(rel_acc)
        lane = lane_ids(ROWS)
        first = lane < DH
        sums = [jnp.zeros((1, PAIR), jnp.float32) for _ in range(5)]
        for stream in range(2):
            proj_ref = (proj_c, proj_q)[stream]
            vec_ref = (vec_c, vec_q)[stream]
            gproj_ref = (gproj_c, gproj_q)[stream]
            for block in range(blocks):
                where = pl.ds(block * ROWS, ROWS)
                start = seq_len - (block + 1) * ROWS
                proj = proj_ref[where, :]
                query_ct = jnp.transpose(((proj + bias_ref[0:1, :]) * 0.125).astype(jnp.bfloat16))
                query_pt = jnp.transpose(((proj + bias_ref[1:2, :]) * 0.125).astype(jnp.bfloat16))
                query_s = proj + bias_ref[2:3, :]
                hot = jnp.where(lane < 4, seg_hot[where, :].astype(jnp.float32), 0.0)
                grad = vec_grad[pl.ds(stream * seq_len + block * ROWS, ROWS), pair_lanes]
                grad_t = jnp.transpose(grad)
                inner = grad.astype(jnp.float32) * vec_ref[where, pair_lanes].astype(jnp.float32)
                window = (rel_ref[pl.ds(start, wide), :].astype(jnp.float32) * 0.125).astype(jnp.bfloat16)
                parts = []
                for head in range(2):
                    own = (lane >= DH) if head else first
                    low, high = head * DH, (head + 1) * DH
                    prob = prob_ref[stream, head, where, :]
                    grad_prob = nn(jnp.where(own, grad, jnp.zeros((), jnp.bfloat16)), vt_scr[...])
                    row_inner = jnp.sum(jnp.where(own, inner, 0.0), axis=1, keepdims=True)
                    gscore = (prob.astype(jnp.float32) * (grad_prob - row_inner)).astype(jnp.bfloat16)
                    value_acc[low:high, :] += nn(grad_t[low:high, :], prob)
                    key_acc[low:high, :] += nn(query_ct[low:high, :], gscore)
                    both = nn(gscore, ext_scr[...])
                    table = jnp.concatenate([jnp.zeros((ROWS, ROWS), jnp.bfloat16), gscore], axis=1)
                    table = shear_left(table)
                    gpos = nn(table, window)
                    rel_acc[low:high, start : start + wide] += nn(query_pt[low:high, :], table)
                    tail = both[:, PAIR:]
                    tail = jnp.where(lane < 4, tail, 0.0)
                    g_same = jnp.sum(tail * hot, axis=1, keepdims=True)
                    g_other = jnp.sum(tail, axis=1, keepdims=True) - g_same
                    parts.append((both[:, :PAIR], gpos, g_same, g_other))
                g_content = jnp.where(first, parts[0][0], parts[1][0])
                g_position = jnp.where(first, parts[0][1], parts[1][1])
                g_same = jnp.where(first, parts[0][2], parts[1][2])
                g_other = jnp.where(first, parts[0][3], parts[1][3])
                g_segment = g_same * embed_ref[0:1, :] + g_other * embed_ref[1:2, :]
                gproj_ref[where, :PAIR] = (g_content + g_position + g_segment).astype(jnp.bfloat16)
                terms = (g_content, g_position, g_segment, g_same * query_s, g_other * query_s)
                sums = [old + jnp.sum(term, axis=0, keepdims=True) for old, term in zip(sums, terms)]
            if stream == 0:
                advance(2 * grid_at - 10)
        gproj_c[:, PAIR : 2 * PAIR] = jnp.transpose(key_acc[...]).astype(jnp.bfloat16)
        gproj_c[:, 2 * PAIR :] = jnp.transpose(value_acc[...]).astype(jnp.bfloat16)
        triple = nn(content_t[...], gproj_c[...])
        g_query = triple[:, :PAIR] + nn(query_t[...], gproj_q[...])
        g_rel = nt(table_t[...], rel_acc[...].astype(jnp.bfloat16))
        vectors = jnp.concatenate(sums, axis=0)
        weights = jnp.concatenate([query_w[...], key_w[...], value_w[...]], axis=1)
        total[:seq_len, :] += nt(gproj_c[...], weights)
        total[seq_len:, :] += nt(gproj_q[...], query_w[...])
        late = turn % half_pairs
        piece = EARLY + late
        rel_piece = EARLY + half_pairs
        lanes = pl.ds(pl.multiple_of(late * PAIR, PAIR), PAIR)

        @pl.when(turn >= half_pairs)
        def _():
            swap_copy(piece).wait_send()

            @pl.when(turn == half_pairs)
            def _():
                swap_copy(rel_piece).wait_send()

        work[piece, :, :PAIR] = g_query.astype(jnp.bfloat16)
        work[piece, :, PAIR:] = triple[:, PAIR:].astype(jnp.bfloat16)
        work[rel_piece, :, lanes] = g_rel.astype(jnp.bfloat16)

        @pl.when(turn < half_pairs)
        def _():
            small_far[0:5, lanes] = vectors
            swap_copy(piece).start()

            @pl.when(turn == half_pairs - 1)
            def _():
                swap_copy(rel_piece).start()
                tiny_copy(0).start()

        @pl.when(turn >= half_pairs)
        def _():
            small_work[0, 0:5, lanes] = vectors
            settle(piece)

            @pl.when(turn == pairs - 1)
            def _():
                settle(rel_piece)

    advance(grid_at - 1 + (grid_at // (feeds + 1)) * (grid_at - feeds))

    @pl.when(grid_at == last)
    def _():
        for at in range(0, total.shape[0], ROWS):
            vec_grad[at : at + ROWS, :] = total[at : at + ROWS, :].astype(jnp.bfloat16)
        begin_tick = final_slot

        def finish_tick(tick, carry):
            for step in range(len(tiny_devices)):
                @pl.when(tick == begin_tick + 1 + step)
                def _():
                    tiny_copy(step).wait_recv()
                    small_work[step + 1] = small_work[step] + small_land[step]
                    if step + 1 < len(tiny_devices):
                        tiny_copy(step + 1).start()

            advance(tick)

            @pl.when(tick == begin_tick)
            def _():
                grad_copy(0).start()
                grad_copy(1).start()
                keep_copy(0).start()
                keep_copy(1).start()

            return carry

        lax.fori_loop(begin_tick, final_slot + 1 + offsets[-1], finish_tick, 0)
        small_out[...] = small_work[len(tiny_devices)]
        for step in range(len(tiny_devices)):
            tiny_copy(step).wait_send()
        for stream in range(2):
            rows_copy(stream).wait()
            grad_copy(stream).wait()
            keep_copy(stream).wait()

        def drain(piece, carry):
            for fold in range(FOLDS):
                fold_copy(fold, piece).wait_send()
                spread_copy(fold, piece).wait_send()
            store(piece).wait()
            return carry

        lax.fori_loop(0, COUNT, drain, 0)


def backward(
    dp_size, seg_hot, proj_c, proj_q, keys, values, rel_keys, bias, embed, prob, query_w, key_w, value_w,
    vec_c, vec_q, content_t, query_t, table_t, out_w, act, slope, up_w, down_w, low_rows, low_t, first_t,
    normal, scale, norms, sums, grad, rows_in,
):
    seq_len, width = proj_c.shape
    pairs = width // PAIR
    cols = width // 2
    feeds = up_w.shape[1] // cols
    rows = 2 * seq_len
    small_rows = 24
    more = max(1, dp_size.bit_length() - 1 - FOLDS)
    tiny = dp_size.bit_length()
    low = jnp.bfloat16
    dma = pltpu.SemaphoreType.DMA
    once = pl.Buffered(1)
    anywhere = pl.BlockSpec(memory_space=pl.ANY)
    whole = lambda g: (0, 0)
    turn = lambda g: (jnp.maximum(g - feeds - 1, 0) + pairs // 2) % pairs
    per_pair = lambda g: (0, turn(g))
    tile = pl.BlockSpec((seq_len, PAIR), per_pair)
    weight = pl.BlockSpec((width, PAIR), per_pair)

    def chunk(g):
        at = jnp.minimum(g, feeds - 1)
        return (1 - at % 2) * (feeds // 2) + at // 2

    side = lambda g: (0, chunk(g))
    keep = lambda shape: pl.BlockSpec(shape, whole, pipeline_mode=once)
    return pl.pallas_call(
        functools.partial(backward_body, dp_size),
        out_shape=(
            jax.ShapeDtypeStruct((COUNT, width, cols), low),
            jax.ShapeDtypeStruct((small_rows, cols), jnp.float32),
            jax.ShapeDtypeStruct((2, ROWS, width), low),
            jax.ShapeDtypeStruct((2, ROWS, width), low),
            jax.ShapeDtypeStruct((2, ROWS, width), low),
        ),
        grid_spec=pltpu.PrefetchScalarGridSpec(
            num_scalar_prefetch=0,
            grid=(feeds + 1 + pairs,),
            in_specs=[
                keep((seq_len, PAIR)),
                tile, tile, tile, tile,
                pl.BlockSpec((2 * seq_len, PAIR), per_pair),
                pl.BlockSpec((3, PAIR), per_pair),
                pl.BlockSpec((2, PAIR), per_pair),
                pl.BlockSpec((None, 2, 2, seq_len, seq_len), lambda g: (turn(g), 0, 0, 0, 0)),
                weight, weight, weight,
                keep((seq_len, width)), keep((seq_len, width)),
                keep((width, seq_len)), keep((width, seq_len)), keep((width, 2 * seq_len)),
                keep((width, width)),
                pl.BlockSpec((rows, cols), side), pl.BlockSpec((rows, cols), side),
                pl.BlockSpec((width, cols), side), pl.BlockSpec((cols, width), lambda g: (chunk(g), 0)),
                keep((rows, width)), keep((width, rows)), keep((width, rows)), keep((rows, width)),
                keep((rows, 1)), keep((8, width)), keep((8, width)),
                anywhere, anywhere,
            ],
            out_specs=[
                anywhere,
                pl.BlockSpec((small_rows, cols), whole),
                anywhere, anywhere, anywhere,
            ],
            scratch_shapes=[
                pltpu.VMEM((PAIR, seq_len), low),
                pltpu.VMEM((PAIR, seq_len), jnp.float32),
                pltpu.VMEM((PAIR, seq_len), jnp.float32),
                pltpu.VMEM((PAIR, 2 * seq_len), jnp.float32),
                pltpu.VMEM((rows, width), jnp.float32),
                pltpu.VMEM((rows, width), low),
                pltpu.VMEM((rows, cols), low),
                pltpu.VMEM((COUNT, width, cols), low),
                pltpu.VMEM((COUNT, width, cols), low),
                pltpu.VMEM((COUNT, width, cols), low),
                pltpu.VMEM((max(1, more - 1), COUNT if dp_size > 32 else 1, width >> FOLDS, cols), low),
                pltpu.VMEM((tiny + 1, small_rows, cols), jnp.float32),
                pltpu.VMEM((small_rows, cols), jnp.float32),
                pltpu.VMEM((tiny, small_rows, cols), jnp.float32),
                dma((COUNT,)), dma((COUNT,)), dma((COUNT,)),
                dma((FOLDS, COUNT)), dma((FOLDS, COUNT)), dma((FOLDS, COUNT)), dma((FOLDS, COUNT)),
                dma((more, COUNT)), dma((more, COUNT)), dma((tiny,)), dma((tiny,)),
                dma, dma((2,)), dma((4,)), dma((4,)),
            ],
        ),
        compiler_params=pltpu.CompilerParams(
            collective_id=0, has_side_effects=True, vmem_limit_bytes=67043328
        ),
        name="backward",
    )(
        seg_hot, proj_c, proj_q, keys, values, rel_keys, bias, embed, prob, query_w, key_w, value_w,
        vec_c, vec_q, content_t, query_t, table_t, out_w, act, slope, up_w, down_w, low_rows, low_t, first_t,
        normal, scale, norms, sums, grad, rows_in,
    )


def finish_body(
    piece_ref, rows_ref, rows_came, keep_ref, grad_came,
    content_out, query_out, content_grad, query_grad, down_ref, up_ref, out_ref, query_ref, key_ref, value_ref, rel_ref,
):
    at = pl.program_id(0)
    core = lax.axis_index("mp")
    cols = piece_ref.shape[1]
    feeds = 8

    @pl.when((at < feeds) & (at % 2 == 0))
    def _():
        down_ref[...] = jnp.transpose(piece_ref[...].astype(jnp.float32))

    @pl.when((at < feeds) & (at % 2 == 1))
    def _():
        up_ref[...] = piece_ref[...].astype(jnp.float32)

    @pl.when(at == feeds)
    def _():
        out_ref[...] = jnp.transpose(piece_ref[...].astype(jnp.float32))

    for turn in range(3):
        lanes = slice(turn * PAIR, (turn + 1) * PAIR)

        @pl.when(at == EARLY + turn)
        def _():
            query_ref[:, lanes] = piece_ref[:, :PAIR].astype(jnp.float32)
            key_ref[:, lanes] = piece_ref[:, PAIR : 2 * PAIR].astype(jnp.float32)
            value_ref[:, lanes] = piece_ref[:, 2 * PAIR :].astype(jnp.float32)

    @pl.when(at == EARLY + 3)
    def _():
        rel_ref[...] = piece_ref[...].astype(jnp.float32)

    @pl.when(at == 0)
    def _():
        content_out[core] = rows_ref[core]
        content_out[1 - core] = rows_came[0]
        query_out[core] = rows_ref[2 + core]
        query_out[1 - core] = rows_came[1]
        content_grad[core] = keep_ref[0]
        content_grad[1 - core] = grad_came[0]
        query_grad[core] = keep_ref[1]
        query_grad[1 - core] = grad_came[1]


def finish(pieces, rows_out, rows_came, keep_rows, grad_came, half_ff):
    count, rows, cols = pieces.shape
    feeds = 2 * (half_ff // cols)
    square = jax.ShapeDtypeStruct((rows, cols), jnp.float32)
    pair = jax.ShapeDtypeStruct(rows_came.shape, jnp.bfloat16)
    whole = lambda p: (0, 0)
    block = pl.BlockSpec((rows, cols), whole)
    lead = lambda p: (0, 0, 0)
    once = pl.Buffered(1)
    token = pl.BlockSpec(rows_came.shape, lead)
    token_in = pl.BlockSpec(rows_came.shape, lead, pipeline_mode=once)
    at_chunk = lambda p: jnp.minimum(p // 2, feeds // 2 - 1)
    return pl.pallas_call(
        finish_body,
        out_shape=(
            pair, pair, pair, pair,
            jax.ShapeDtypeStruct((half_ff, rows), jnp.float32),
            jax.ShapeDtypeStruct((rows, half_ff), jnp.float32),
            jax.ShapeDtypeStruct((cols, rows), jnp.float32),
            square, square, square, square,
        ),
        grid=(count,),
        in_specs=[
            pl.BlockSpec((None, rows, cols), lambda p: (p, 0, 0)),
            pl.BlockSpec(rows_out.shape, lead, pipeline_mode=once),
            token_in, token_in, token_in,
        ],
        out_specs=[
            token, token, token, token,
            pl.BlockSpec((cols, rows), lambda p: (at_chunk(p), 0)),
            pl.BlockSpec((rows, cols), lambda p: (0, at_chunk(p))),
            pl.BlockSpec((cols, rows), whole),
            block, block, block, block,
        ],
        compiler_params=pltpu.CompilerParams(vmem_limit_bytes=48 << 20),
        name="finish",
    )(pieces, rows_out, rows_came, keep_rows, grad_came)


def position_table(seq_len, width):
    distance = seq_len - 1.0 - np.arange(2 * seq_len - 1, dtype=np.float32)
    freq_exp = np.arange(0, width, 2).astype(np.float32) / np.float32(width)
    inverse = np.float32(1.0) / np.float32(10000.0) ** freq_exp
    angle = (distance[:, None] * inverse[None, :]).astype(np.float32)
    table = np.concatenate([np.sin(angle), np.cos(angle)], axis=1)
    table = np.concatenate([table, np.zeros((1, width), np.float32)], axis=0)
    return table.astype(ml_dtypes.bfloat16)


def on_device(
    dp_size,
    content_in,
    query_in,
    doc_lengths,
    order_ranks,
    segment_ids,
    target_flags,
    query_weight,
    key_weight,
    value_weight,
    out_weight,
    rel_weight,
    content_bias,
    position_bias,
    segment_bias,
    segment_embed,
    first_gain,
    first_shift,
    up_weight,
    up_bias,
    down_weight,
    down_bias,
    second_gain,
    second_shift,
    content_cot,
    query_cot,
):
    docs_dev, half, width = content_in.shape
    seq_len = order_ranks.shape[1]
    mine = lax.axis_index("mp")
    wide_f = lambda value: value.astype(jnp.float32)
    low_f = lambda value: value.astype(jnp.bfloat16)

    def swap(value):
        return lax.ppermute(value, "mp", [(0, 1), (1, 0)])

    def gather_doc(value):
        keep = lax.dynamic_index_in_dim(value, mine, 0, keepdims=False)
        came = swap(lax.dynamic_index_in_dim(value, 1 - mine, 0, keepdims=False))
        head = jnp.where(mine == 0, keep, came)
        tail = jnp.where(mine == 0, came, keep)
        return jnp.concatenate([head, tail], axis=0)

    def both(value, axis):
        return jnp.concatenate([value, swap(value)], axis=axis)

    content = gather_doc(content_in)
    query = gather_doc(query_in)
    query_use = both(query_weight, 1)
    key_use = both(key_weight, 1)
    value_use = both(value_weight, 1)
    rel_use = both(rel_weight, 1)
    vectors = both(
        jnp.concatenate(
            [
                wide_f(content_bias)[None],
                wide_f(position_bias)[None],
                wide_f(segment_bias)[None],
                wide_f(segment_embed),
            ],
            axis=0,
        ),
        1,
    )
    bias, embed = vectors[:3], vectors[3:]
    out_use = both(out_weight, 0)
    up_use = both(up_weight, 1)
    down_use = both(down_weight, 0)
    up_bias_use = both(wide_f(up_bias)[None], 1)
    cot_c = gather_doc(content_cot)
    cot_q = gather_doc(query_cot)

    lengths = lax.dynamic_slice_in_dim(doc_lengths, mine, 1, 0)
    ranks = lax.dynamic_slice_in_dim(order_ranks, mine, 1, 0)
    segments = lax.dynamic_slice_in_dim(segment_ids, mine, 1, 0)
    targets = lax.dynamic_slice_in_dim(target_flags, mine, 1, 0)
    live = targets * (jnp.arange(seq_len) >= 2).astype(jnp.int32)[None]
    lanes = jnp.arange(PAIR)
    seg_hot = low_f((segments[:, :, None] == lanes % 4) & (lanes < 8))
    table = jnp.asarray(position_table(seq_len, width))
    rel_keys = low_f(nn(table, rel_use))
    proj_c = nn(content, query_use)[None]
    proj_q = nn(query, query_use)[None]
    keys = low_f(nn(content, key_use))[None]
    values = low_f(nn(content, value_use))[None]
    vec_c, vec_q, prob = attend_forward(
        lengths, ranks[:, :, None], ranks[:, None, :], live[:, None, :], seg_hot,
        proj_c, proj_q, keys, values, rel_keys, bias, embed,
    )
    norms = jnp.stack(
        [first_gain, first_shift, second_gain, second_shift, down_bias, down_bias, down_bias, down_bias]
    ).astype(jnp.float32)
    first_t, normal, scale, act, slope, grad, low_rows, low_t, rows_out, sums = feed_forward(
        vec_c[0], vec_q[0], content, query, cot_c, cot_q, out_use, up_use, down_use, up_bias_use, norms
    )
    pieces, tiny, keep_rows, rows_came, grad_came = backward(
        dp_size, seg_hot[0], proj_c[0], proj_q[0], keys[0], values[0], rel_keys, bias, embed, prob[0],
        query_use, key_use, value_use, vec_c[0], vec_q[0], jnp.transpose(content), jnp.transpose(query),
        jnp.asarray(position_table(seq_len, width).T), out_use, act, slope, up_use, down_use,
        low_rows, low_t, first_t, normal, scale, norms, sums, grad, rows_out,
    )
    ff = up_weight.shape[1]
    cols = query_weight.shape[1]
    (
        content_out, query_out, content_grad, query_grad,
        down_sum, up_sum, out_sum, query_sum, key_sum, value_sum, rel_sum,
    ) = finish(pieces, rows_out.reshape(4, half, width), rows_came, keep_rows, grad_came, ff)
    split_rows = 5 + ff // cols
    same_part = tiny[split_rows : split_rows + 10].reshape(5, width)
    split_part = tiny[:5]
    return (
        content_out,
        query_out,
        content_grad,
        query_grad,
        query_sum,
        key_sum,
        value_sum,
        out_sum,
        rel_sum,
        split_part[0],
        split_part[1],
        split_part[2],
        split_part[3:5],
        same_part[0],
        same_part[1],
        up_sum,
        tiny[5:split_rows].reshape(ff),
        down_sum,
        same_part[4],
        same_part[2],
        same_part[3],
    )


def solution(mesh):
    placed = (
        P("dp", "mp", None),
        P("dp", "mp", None),
        P("dp"),
        P("dp", None),
        P("dp", None),
        P("dp", None),
        P(None, "mp"),
        P(None, "mp"),
        P(None, "mp"),
        P("mp", None),
        P(None, "mp"),
        P("mp"),
        P("mp"),
        P("mp"),
        P(None, "mp"),
        P(),
        P(),
        P(None, "mp"),
        P("mp"),
        P("mp", None),
        P(),
        P(),
        P(),
        P("dp", "mp", None),
        P("dp", "mp", None),
    )
    return jax.shard_map(
        functools.partial(on_device, mesh.shape["dp"]),
        mesh=mesh,
        in_specs=placed,
        out_specs=(
            P("dp", "mp", None),
            P("dp", "mp", None),
            P("dp", "mp", None),
            P("dp", "mp", None),
            P(None, "mp"),
            P(None, "mp"),
            P(None, "mp"),
            P("mp", None),
            P(None, "mp"),
            P("mp"),
            P("mp"),
            P("mp"),
            P(None, "mp"),
            P(),
            P(),
            P(None, "mp"),
            P("mp"),
            P("mp", None),
            P(),
            P(),
            P(),
        ),
        check_vma=False,
    )
```

time: 405 us -> 374 us (0.923); the launches traced: 397 us -> 372 us
  Pallas kernels: 198 us -> 291 us
  matrix products: 93.5 us -> 9.89 us
  other arithmetic: 29.5 us -> 10.8 us
  local copies, waits for them, and re-layouts: 68.8 us -> 53.7 us
    pallas_call x2 -> x3, Pallas kernels: 162 us -> 255 us  [the longest x1 208 us: backward(): pl.pallas_call(functools.partial(backward_body, dp_size), out_shape=(jax....]
    dot_general x10 -> x0, matrix products: 59.8 us -> none  [the longest x7 39.9 us: nt(): lax.dot_general(left_op, right_op, (((1,), (1,)), ((), ())), preferred_el...]
    dot_general x8 -> x5, matrix products: 33.7 us -> 9.89 us  [nn(): return jnp.dot(left_op, right_op, preferred_element_type=jnp.float32)]
    squeeze x10 -> x0, local copies, waits for them, and re-layouts: 10.4 us -> none  [the longest x6 7.2 us: return_doc(): keep = lax.dynamic_index_in_dim(pair, mine, 0, keepdims=False)]
    reshape x9 -> x0, local copies, waits for them, and re-layouts: 10.2 us -> none  [the longest x4 8.28 us: return_doc(): pair = value.reshape(2, half, width)]
    reduce_sum x6 -> x0, other arithmetic: 9.48 us -> none  [the longest x2 3.48 us: layer_norm(): return center * lax.rsqrt(spread + epsilon) * gain + shift]
    concatenate x0 -> x4, local copies, waits for them, and re-layouts: none -> 4.67 us  [gather_doc(): return jnp.concatenate([head, tail], axis=0)]
    another operation x8 -> x0, other arithmetic: 4.52 us -> none  [return_doc(): jnp.stack([jnp.where(mine == 0, keep, came), jnp.where(mine == 0, came, k...]
  transfers between devices with their start and end apart: 17 -> 13, of which waited for: 1 -> 2; matrix products, arithmetic and copies ran while one was open for 25% -> 15% of each run, Pallas kernels for 50% -> 10%
where the time goes in v4:
time: 374 us; the launch traced here: 372 us
  Pallas kernels  291 us (78%)
  local copies, waits for them, and re-layouts  53.7 us (14%)
  other arithmetic  10.8 us (3%)
  matrix products  9.89 us (3%)
    pallas_call x1, Pallas kernels, backward(): pl.pallas_call(functools.partial(backward_body, dp_size), out_shape=(jax....  208 us
    pallas_call x1, Pallas kernels, attend_forward(): pl.pallas_call(attend_forward_body, out_shape=(jax.ShapeDtypeStruct((docs...  35.7 us
    pallas_call x1, Pallas kernels, feed_forward(): pl.pallas_call(feed_forward_body, out_shape=(jax.ShapeDtypeStruct((width,...  32.1 us
    unnamed x78, local copies, waits for them, and re-layouts  16 us
    pallas_call x1, Pallas kernels, finish(): pl.pallas_call(finish_body, out_shape=(pair, pair, pair, pair, jax.ShapeD...  14.7 us
    concatenate x6, local copies, waits for them, and re-layouts, both(): return jnp.concatenate([value, swap(value)], axis=axis)  11.2 us
    dot_general x5, matrix products, nn(): return jnp.dot(left_op, right_op, preferred_element_type=jnp.float32)  9.89 us
  transfers between devices with their start and end apart: 13, of which 2 were waited for; matrix products, arithmetic and copies ran while one was open for 15% of the time, Pallas kernels for 10%

profile of v4, /device:TPU:0, one launch (start us, length us, event | category | flops | bytes accessed | tf_op | source)
XLA Modules:
  0.0 371.9 jit_solution(14091360023278112229)
XLA Ops:
  0.7 1.4 reshape.181
  8.6 2.0 constant_dynamic-update-slice_fusion.1
  13.0 3.4 constant_dynamic-update-slice_fusion.9
  16.4 1.6 constant_dynamic-update-slice_fusion.11
  23.8 1.2 copy.63
  25.0 1.9 copy.64
  27.8 1.2 copy.61
  31.3 1.3 pad_maximum_fusion.4.up_bias
  33.1 1.3 pad_maximum_fusion.5.embed_ref.refs_7_
  34.4 1.3 fusion.4.bias_ref.refs_6_
  39.7 1.2 copy.73.cot_c
  41.8 1.2 bitcast_select_fusion.1
  43.1 1.2 copy.74.cot_q
  44.2 1.2 copy.72.query
  45.4 1.1 copy.71.content
  46.9 1.9 constant_dynamic-update-slice_fusion.refs_9_
  49.1 1.2 constant_dynamic-update-slice_fusion.2.refs_10_
  50.3 1.7 convolution_convert_fusion.2.refs_3_
  52.5 2.0 fusion.10.refs_2_
  54.5 1.2 constant_dynamic-update-slice_fusion.4.refs_11_
  55.6 2.0 fusion.12.refs_1_
  57.6 1.7 convolution_convert_fusion.1.refs_4_
  59.3 2.5 fusion.rel_ref.refs_5_
  61.9 35.7 %attend_forward.1 = (bf16[1,512,768]{2,1,0:T(8,128)(2,1)}, bf16[1,512,768]{2,1,0:T(8,128)(2,1)}, bf16[1,6,2,2,512,512]{5,4,3,2,1,0:T(8,128)(2,1)}) custom-call(s32[1]{0:T(128)} %dynamic_slice.42.len_ref, s32[1,512,1]{2,1,0:T(8,128)} %copy.66.rank_col, s32[1,1,512]{2,1,0:T(1,128)} %get-tuple-element.108.rank_row, s32[1,1,512]{2,1,0:T(1,128)} %fusion.5.live_row, ...), custom_call_target="tpu_custom_call" | custom-call | tf_op jit(solution)/shard_map/attend_forward/pallas_call | solution.py:99
  97.6 3.6 constant_dynamic-update-slice_fusion.8.up_ref.refs_20_
  101.3 3.2 constant_dynamic-update-slice_fusion.10.down_ref.refs_21_
  104.5 32.1 %feed_forward.1 = (bf16[768,1024]{1,0:T(8,128)(2,1)}, bf16[1024,768]{1,0:T(8,128)(2,1)}, f32[1024,1]{1,0:T(8,128)}, bf16[1024,3072]{1,0:T(8,128)(2,1)}, bf16[102...) custom-call(bf16[512,768]{1,0:T(8,128)(2,1)} %bitcast.46, ...), custom_call_target="tpu_custom_call" | custom-call | tf_op jit(solution)/shard_map/feed_forward/pallas_call | solution.py:216
  136.6 208.4 %backward.1 = (bf16[13,768,384]{2,1,0:T(8,128)(2,1)}, f32[24,384]{1,0:T(8,128)}, bf16[2,256,768]{2,1,0:T(8,128)(2,1)}, bf16[2,256,768]{2,1,0:T(8,128)(2,1)}, bf16[2,256,768]{2,1,0:T(8,128)(2,1)}) custom-call(bf16[512,128]{1,0:T(8,128)(2,1)} %and_convert_fusion.1.refs_0_, f32[512,768]{1,0:T(8,128)} %fusion.12.refs_1_, f32[512,768]{1,0:T(8,128)} %fusion.10.refs_2_, ...), custom_call_target="tpu_custom_call" | custom-call | tf_op jit(solution)/shard_map/backward/pallas_call | solution.py:717
  345.8 1.4 slice_reduce_fusion
  347.2 1.4 fusion.13
  352.2 1.4 copy-done
  357.0 14.7 %finish.1 = (bf16[2,256,768]{2,1,0:T(8,128)(2,1)}, bf16[2,256,768]{2,1,0:T(8,128)(2,1)}, bf16[2,256,768]{2,1,0:T(8,128)(2,1)}, bf16[2,256,768]{2,1,0:T(8,128)(2,...) custom-call(bf16[13,768,384]{2,1,0:T(8,128)(2,1)} %get-tuple-element, ...), custom_call_target="tpu_custom_call" | custom-call | tf_op jit(solution)/shard_map/finish/pallas_call | solution.py:841
  (142 shorter events, 32.2 us)
Async XLA Ops:
  0.7 10.0 %copy-start.23 = (bf16[768,384]{1,0:T(8,128)(2,1)S(1)}, bf16[768,384]{1,0:T(8,128)(2,1)}, u32[]{:S(2)}) copy-start(bf16[768,384]{1,0:T(8,128)(2,1)} %param.34) | copy-start | bytes 1769476
  0.7 10.8 %copy-start.24 = (bf16[768,384]{1,0:T(8,128)(2,1)S(1)}, bf16[768,384]{1,0:T(8,128)(2,1)}, u32[]{:S(2)}) copy-start(bf16[768,384]{1,0:T(8,128)(2,1)} %param.35) | copy-start | bytes 1769476
  2.1 29.1 %collective-permute-start.12 = (f32[1,1536]{1,0:T(1,128)}, f32[1,1536]{1,0:T(1,128)}, u32[]{:S(2)}, u32[]{:S(2)}) collective-permute-start(f32[1,1536]{1,0:T(1,128)} %reshape.181), channel_id=1, source_target_pairs={{0,1},{1,0},{2,3},{3,2},{4,5},{5,4},{6,7},{7,6},{8,9},{9,8},{10,11... | collective-permute-start | bytes 18440 | tf_op jit(solution)/shard_map/ppermute | solution.py:913
  5.3 27.4 %collective-permute-start.6 = (f32[5,384]{1,0:T(8,128)S(1)}, f32[5,384]{1,0:T(8,128)}, u32[]{:S(2)}, u32[]{:S(2)}) collective-permute-start(f32[5,384]{1,0:T(8,128)S(1)} %maximum_convert_fusion), channel_id=1, source_target_pairs={{0,1},{1,0},{2,3},{3,2},{4,5},{5,4},{6,7},{7,6},{8,9},{9,8},{10,11... | collective-permute-start | bytes 23048 | tf_op jit(solution)/shard_map/ppermute | solution.py:913
  5.4 41.2 %collective-permute-start.1 = (bf16[768,384]{1,0:T(8,128)(2,1)}, bf16[768,384]{1,0:T(8,128)(2,1)}, u32[]{:S(2)}, u32[]{:S(2)}) collective-permute-start(bf16[768,384]{1,0:T(8,128)(2,1)} %param.33), channel_id=1, source_target_pairs={{0,1},{1,0},{2,3},{3,2},{4,5},{5,4},{6,7},{7,6},{8,9},{9,8},{10,11... | collective-permute-start | bytes 1769480 | tf_op jit(solution)/shard_map/ppermute | solution.py:913
  5.8 43.0 %collective-permute-start.3 = (bf16[768,384]{1,0:T(8,128)(2,1)}, bf16[768,384]{1,0:T(8,128)(2,1)}, u32[]{:S(2)}, u32[]{:S(2)}) collective-permute-start(bf16[768,384]{1,0:T(8,128)(2,1)} %param.34), channel_id=1, source_target_pairs={{0,1},{1,0},{2,3},{3,2},{4,5},{5,4},{6,7},{7,6},{8,9},{9,8},{10,11... | collective-permute-start | bytes 1769480 | tf_op jit(solution)/shard_map/ppermute | solution.py:913
  5.9 48.5 %collective-permute-start.4 = (bf16[768,384]{1,0:T(8,128)(2,1)}, bf16[768,384]{1,0:T(8,128)(2,1)}, u32[]{:S(2)}, u32[]{:S(2)}) collective-permute-start(bf16[768,384]{1,0:T(8,128)(2,1)} %param.35), channel_id=1, source_target_pairs={{0,1},{1,0},{2,3},{3,2},{4,5},{5,4},{6,7},{7,6},{8,9},{9,8},{10,11... | collective-permute-start | bytes 1769480 | tf_op jit(solution)/shard_map/ppermute | solution.py:913
  8.6 3.8 %copy-start.31 = (s32[2,512]{1,0:T(2,128)S(1)}, s32[2,512]{1,0:T(2,128)}, u32[]{:S(2)}) copy-start(s32[2,512]{1,0:T(2,128)} %param.30) | copy-start | bytes 12292
  8.6 4.3 %copy-start.25 = (bf16[384,768]{1,0:T(8,128)(2,1)S(1)}, bf16[384,768]{1,0:T(8,128)(2,1)}, u32[]{:S(2)}) copy-start(bf16[384,768]{1,0:T(8,128)(2,1)} %param.36) | copy-start | bytes 1769476
  13.0 3.4 copy-start.10
  16.4 2.1 copy-start.20
  20.3 1.9 copy-start.29
  20.3 1.9 copy-start.30
  31.2 4.5 %collective-permute-start = (bf16[256,768]{0,1:T(8,128)(2,1)}, bf16[256,768]{0,1:T(8,128)(2,1)S(1)}, u32[]{:S(2)}, u32[]{:S(2)}) collective-permute-start(bf16[256,768]{0,1:T(8,128)(2,1)} %bitcast.54), channel_id=1, source_target_pairs={{0,1},{1,0},{2,3},{3,2},{4,5},{5,4},{6,7},{7,6},{8,9},{9,8},{10,11... | collective-permute-start | bytes 1179656 | tf_op jit(solution)/shard_map/ppermute | solution.py:913
  32.6 3.2 collective-permute-start.2
  35.7 1.7 collective-permute-start.8
  35.8 2.8 copy-start.11
  35.8 2.8 copy-start.13
  35.9 61.7 %collective-permute-start.10 = (bf16[768,1536]{1,0:T(8,128)(2,1)}, bf16[768,1536]{1,0:T(8,128)(2,1)}, u32[]{:S(2)}, u32[]{:S(2)}) collective-permute-start(bf16[768,1536]{1,0:T(8,128)(2,1)} %param.44), channel_id=1, source_target_pairs={{0,1},{1,0},{2,3},{3,2},{4,5},{5,4},{6,7},{7,6},{8,9},{9,8},{10,11... | collective-permute-start | bytes 7077896 | tf_op jit(solution)/shard_map/ppermute | solution.py:913
  36.4 2.2 copy-start.15
  36.4 2.2 copy-start.17
  37.4 4.3 %collective-permute-start.9 = (bf16[256,768]{0,1:T(8,128)(2,1)}, bf16[256,768]{0,1:T(8,128)(2,1)}, u32[]{:S(2)}, u32[]{:S(2)}) collective-permute-start(bf16[256,768]{0,1:T(8,128)(2,1)} %bitcast.21), channel_id=1, source_target_pairs={{0,1},{1,0},{2,3},{3,2},{4,5},{5,4},{6,7},{7,6},{8,9},{9,8},{10,11... | collective-permute-start | bytes 1179656 | tf_op jit(solution)/shard_map/ppermute | solution.py:913
  41.7 59.6 %collective-permute-start.11 = (bf16[1536,768]{1,0:T(8,128)(2,1)}, bf16[1536,768]{1,0:T(8,128)(2,1)}, u32[]{:S(2)}, u32[]{:S(2)}) collective-permute-start(bf16[1536,768]{1,0:T(8,128)(2,1)} %param.46), channel_id=1, source_target_pairs={{0,1},{1,0},{2,3},{3,2},{4,5},{5,4},{6,7},{7,6},{8,9},{9,8},{10,11... | collective-permute-start | bytes 7077896 | tf_op jit(solution)/shard_map/ppermute | solution.py:913
  45.4 3.7 copy-start.7
  46.5 3.7 copy-start.12
  46.5 3.7 copy-start.14
  46.5 51.0 %collective-permute-start.7 = (bf16[384,768]{1,0:T(8,128)(2,1)}, bf16[384,768]{1,0:T(8,128)(2,1)S(1)}, u32[]{:S(2)}, u32[]{:S(2)}) collective-permute-start(bf16[384,768]{1,0:T(8,128)(2,1)} %param.36), channel_id=1, source_target_pairs={{0,1},{1,0},{2,3},{3,2},{4,5},{5,4},{6,7},{7,6},{8,9},{9,8},{10,11... | collective-permute-start | bytes 1769480 | tf_op jit(solution)/shard_map/ppermute | solution.py:913
  48.9 10.4 %collective-permute-start.5 = (bf16[768,384]{1,0:T(8,128)(2,1)}, bf16[768,384]{1,0:T(8,128)(2,1)S(1)}, u32[]{:S(2)}, u32[]{:S(2)}) collective-permute-start(bf16[768,384]{1,0:T(8,128)(2,1)} %param.37), channel_id=1, source_target_pairs={{0,1},{1,0},{2,3},{3,2},{4,5},{5,4},{6,7},{7,6},{8,9},{9,8},{10,11... | collective-permute-start | bytes 1769480 | tf_op jit(solution)/shard_map/ppermute | solution.py:913
  50.3 2.2 copy-start.18
  52.5 2.0 copy-start.5
  55.6 2.0 copy-start.6
  97.6 3.7 copy-start.4
  (17 other events, 26.0 us)

commit v5 on v4

--- a/solution.py
+++ b/solution.py
@@ -14,6 +14,7 @@
 PAIR = 2 * DH
 ROWS = 256
 NEG = -1e30
+MESH = pl.DeviceIdType.MESH
 
 
 def nt(left_op, right_op):
@@ -30,42 +31,161 @@
     return lax.broadcasted_iota(jnp.int32, (rows, PAIR), 1)
 
 
-def attend_forward_body(
-    len_ref, rank_col, rank_row, live_row, seg_hot, proj_c, proj_q, key_ref, value_ref, rel_ref,
-    bias_ref, embed_ref, vec_c, vec_q, prob_ref, mask_scr, ext_scr,
+def forward_body(
+    content_in, query_in, content_cot, query_cot, query_w, key_w, value_w, rel_w, out_w, up_w, down_w,
+    meta_ref, vector_ref, table_ref,
+    vec_c, vec_q, prob_ref, proj_c, proj_q, key_ref, value_ref, rel_ref, hot_ref, content_t, query_t, vectors_out,
+    content_out, query_out, cots_out, square_out, out_all, up_all, down_all,
+    tokens, squares, vectors, bounce_up, bounce_down, bounce_out, bounce_cot, mask_scr, ext_scr, rank_scr,
+    token_sem, token_send, token_recv, square_sem, square_send, square_recv,
+    bulk_load, bulk_store, bulk_send, bulk_recv, vector_send, vector_recv,
 ):
-    seq_len = key_ref.shape[0]
+    step = pl.program_id(0)
+    core = lax.axis_index("mp")
+    seq_len = proj_c.shape[0]
+    half = seq_len // 2
+    cols = query_w.shape[1]
+    feed = up_w.shape[1]
     blocks = seq_len // ROWS
     wide = seq_len + ROWS
-
-    @pl.when(pl.program_id(1) == 0)
-    def _():
-        length = len_ref[pl.program_id(0)]
+    other = {"mp": 1 - core}
+    mine = pl.ds(pl.multiple_of(core * half, half), half)
+
+    def remote(source, target, send, recv):
+        return pltpu.make_async_remote_copy(
+            src_ref=source, dst_ref=target, send_sem=send, recv_sem=recv,
+            device_id=other, device_id_type=MESH,
+        )
+
+    token_in = (content_in, query_in)
+    square_in = (query_w, key_w, value_w, rel_w)
+    token_load = [
+        pltpu.make_async_copy(token_in[at].at[core], tokens.at[at, mine], token_sem.at[at]) for at in range(2)
+    ]
+    token_swap = [
+        remote(token_in[at].at[1 - core], tokens.at[at, mine], token_send.at[at], token_recv.at[at])
+        for at in range(2)
+    ]
+    square_load = [
+        pltpu.make_async_copy(square_in[at], squares.at[at, :, :cols], square_sem.at[at]) for at in range(4)
+    ]
+    square_swap = [
+        remote(square_in[at], squares.at[at, :, cols:], square_send.at[at], square_recv.at[at])
+        for at in range(4)
+    ]
+    vector_swap = remote(vector_ref, vectors, vector_send, vector_recv)
+    cot_in = (content_cot, query_cot)
+    bulk_loads = [
+        pltpu.make_async_copy(out_w, bounce_out, bulk_load.at[0]),
+        pltpu.make_async_copy(up_w, bounce_up, bulk_load.at[1]),
+        pltpu.make_async_copy(down_w, bounce_down, bulk_load.at[2]),
+    ] + [
+        pltpu.make_async_copy(cot_in[at].at[core], bounce_cot.at[at], bulk_load.at[3 + at]) for at in range(2)
+    ]
+    bulk_stores = [
+        pltpu.make_async_copy(bounce_out, out_all.at[:cols], bulk_store.at[0]),
+        pltpu.make_async_copy(bounce_up, up_all.at[:, :feed], bulk_store.at[1]),
+        pltpu.make_async_copy(bounce_down, down_all.at[:feed], bulk_store.at[2]),
+    ] + [
+        pltpu.make_async_copy(bounce_cot.at[at], cots_out.at[at, mine], bulk_store.at[3 + at]) for at in range(2)
+    ]
+    bulk_swaps = [
+        remote(out_w, out_all.at[cols:], bulk_send.at[0], bulk_recv.at[0]),
+        remote(up_w, up_all.at[:, feed:], bulk_send.at[1], bulk_recv.at[1]),
+        remote(down_w, down_all.at[feed:], bulk_send.at[2], bulk_recv.at[2]),
+    ] + [
+        remote(cot_in[at].at[1 - core], cots_out.at[at, mine], bulk_send.at[3 + at], bulk_recv.at[3 + at])
+        for at in range(2)
+    ]
+    token_store = [
+        pltpu.make_async_copy(tokens.at[at], (content_out, query_out)[at], bulk_store.at[5 + at]) for at in range(2)
+    ]
+    square_store = [
+        pltpu.make_async_copy(squares.at[at], square_out.at[at], bulk_store.at[7 + at]) for at in range(3)
+    ]
+
+    @pl.when(step == 0)
+    def _():
+        for copy in token_load + square_load:
+            copy.start()
+        barrier = pltpu.get_barrier_semaphore()
+        pl.semaphore_signal(barrier, inc=1, device_id=other, device_id_type=MESH)
+        pl.semaphore_wait(barrier, 1)
+        for copy in token_swap + [vector_swap] + square_swap + bulk_swaps + bulk_loads:
+            copy.start()
+        vectors_out[:, :cols] = vector_ref[...]
+        place_j = lax.broadcasted_iota(jnp.int32, (1, seq_len), 1)
+        ranks = meta_ref[pl.ds(core, 1), :]
+        segments = meta_ref[pl.ds(2 + core, 1), :]
+        targets = meta_ref[pl.ds(4 + core, 1), :]
+        length = meta_ref[pl.ds(6 + core, 1), :]
+        live = jnp.where(place_j >= 2, targets, 0.0)
+        rank_scr[...] = jnp.transpose(jnp.broadcast_to(ranks, (PAIR, seq_len)))
+        lane = lane_ids(seq_len)
+        seg_turn = jnp.transpose(jnp.broadcast_to(segments, (PAIR, seq_len)))
+        hot = (seg_turn == (lane % 4).astype(jnp.float32)) & (lane < 8)
+        hot_ref[...] = jnp.where(hot, 1.0, 0.0).astype(jnp.bfloat16)
+        base = jnp.where(place_j.astype(jnp.float32) < length, 0.0, NEG)
         for block in range(blocks):
-            rows = pl.ds(block * ROWS, ROWS)
-            place_j = lax.broadcasted_iota(jnp.int32, (ROWS, seq_len), 1)
-            place_i = lax.broadcasted_iota(jnp.int32, (ROWS, seq_len), 0) + block * ROWS
-            visible = (place_j < length) & (
-                (live_row[...] == 0) | (rank_row[...] < rank_col[rows, :])
-            )
-            diagonal = place_i == place_j
-            mask_scr[0, rows, :] = jnp.where(visible | diagonal, 0.0, NEG)
-            mask_scr[1, rows, :] = jnp.where(visible & jnp.logical_not(diagonal), 0.0, NEG)
-
+            rows = slice(block * ROWS, (block + 1) * ROWS)
+            rank_i = jnp.concatenate([rank_scr[rows, :]] * (seq_len // PAIR), axis=1)
+            seen = jnp.where((live == 0.0) | (ranks < rank_i), base, NEG)
+            column = lax.broadcasted_iota(jnp.int32, (ROWS, seq_len), 1)
+            line = lax.broadcasted_iota(jnp.int32, (ROWS, seq_len), 0) + block * ROWS
+            diagonal = column == line
+            mask_scr[0, rows, :] = jnp.where(diagonal, 0.0, seen)
+            mask_scr[1, rows, :] = jnp.where(diagonal, NEG, seen)
+        for copy in token_load + square_load:
+            copy.wait()
+        for copy in token_swap:
+            copy.wait_recv()
+        for copy in token_store:
+            copy.start()
+
+    @pl.when(step == 1)
+    def _():
+        for copy in bulk_loads:
+            copy.wait()
+        for copy in bulk_stores:
+            copy.start()
+        content_t[...] = jnp.transpose(tokens[0])
+        query_t[...] = jnp.transpose(tokens[1])
+
+    @pl.when(step == pl.num_programs(0) // 2)
+    def _():
+        for copy in square_swap + [vector_swap]:
+            copy.wait_recv()
+        for copy in square_store:
+            copy.start()
+        vectors_out[:, cols:] = vectors[...]
+
+    pair_lanes = pl.ds(pl.multiple_of(step * PAIR, PAIR), PAIR)
+    lines = vectors_out[:, pair_lanes]
+    triple_w = jnp.concatenate([squares[at, :, pair_lanes] for at in range(3)], axis=1)
+    for block in range(blocks):
+        rows = slice(block * ROWS, (block + 1) * ROWS)
+        triple = nn(tokens[0, rows, :], triple_w)
+        proj_c[rows, :] = triple[:, :PAIR]
+        key_ref[rows, :] = triple[:, PAIR : 2 * PAIR].astype(jnp.bfloat16)
+        value_ref[rows, :] = triple[:, 2 * PAIR :].astype(jnp.bfloat16)
+        proj_q[rows, :] = nn(tokens[1, rows, :], squares[0, :, pair_lanes])
+    for block in range(2 * blocks):
+        rows = slice(block * ROWS, (block + 1) * ROWS)
+        rel_ref[rows, :] = nn(table_ref[rows, :], squares[3, :, pair_lanes]).astype(jnp.bfloat16)
     ext_scr[:, :PAIR] = key_ref[...]
-    ext_scr[:, PAIR:] = seg_hot[...]
+    ext_scr[:, PAIR:] = hot_ref[...]
     lane = lane_ids(ROWS)
-    diff = embed_ref[0:1, :] - embed_ref[1:2, :]
+    diff = lines[3:4, :] - lines[4:5, :]
     for stream in range(2):
         proj_ref = (proj_c, proj_q)[stream]
         vec_ref = (vec_c, vec_q)[stream]
         for block in range(blocks):
             rows = pl.ds(block * ROWS, ROWS)
             proj = proj_ref[rows, :]
-            query_c = ((proj + bias_ref[0:1, :]) * 0.125).astype(jnp.bfloat16)
-            query_p = ((proj + bias_ref[1:2, :]) * 0.125).astype(jnp.bfloat16)
-            seg_gap = (proj + bias_ref[2:3, :]) * (diff * 0.125)
-            hot = seg_hot[rows, :].astype(jnp.float32)
+            query_c = ((proj + lines[0:1, :]) * 0.125).astype(jnp.bfloat16)
+            query_p = ((proj + lines[1:2, :]) * 0.125).astype(jnp.bfloat16)
+            seg_gap = (proj + lines[2:3, :]) * (diff * 0.125)
+            hot = hot_ref[rows, :].astype(jnp.float32)
             window = rel_ref[pl.ds(seq_len - (block + 1) * ROWS, wide), :]
             vec_pair = None
             for head in range(2):
@@ -88,45 +208,90 @@
                 vec_pair = part if head == 0 else jnp.where(own, part, vec_pair)
             vec_ref[rows, :] = vec_pair.astype(jnp.bfloat16)
 
-
-def attend_forward(lengths, rank_col, rank_row, live_row, seg_hot, proj_c, proj_q, keys, values, rel_keys, bias, embed):
-    docs, seq_len, width = proj_c.shape
+    @pl.when(step == pl.num_programs(0) - 1)
+    def _():
+        for copy in token_swap + square_swap + [vector_swap]:
+            copy.wait_send()
+        for copy in bulk_swaps:
+            copy.wait()
+        for copy in bulk_stores + token_store + square_store:
+            copy.wait()
+
+
+def forward(content_in, query_in, content_cot, query_cot, query_w, key_w, value_w, rel_w, out_w, up_w, down_w, meta, vectors, table):
+    docs, half, width = content_in.shape
+    seq_len = 2 * half
     pairs = width // PAIR
-    per_doc = lambda d, p, *_: (d, 0, 0)
-    per_pair = lambda d, p, *_: (d, 0, p)
-    shared = lambda d, p, *_: (0, p)
-    tile = pl.BlockSpec((None, seq_len, PAIR), per_pair)
+    cols = query_w.shape[1]
+    feed = up_w.shape[1]
+    lines = vectors.shape[0]
+    low = jnp.bfloat16
+    dma = pltpu.SemaphoreType.DMA
+    whole = lambda p: (0, 0)
+    once = pl.Buffered(1)
+    anywhere = pl.BlockSpec(memory_space=pl.ANY)
+    tile = pl.BlockSpec((seq_len, PAIR), lambda p: (0, p))
+    low_tokens = jax.ShapeDtypeStruct((seq_len, width), low)
+    turned = jax.ShapeDtypeStruct((width, seq_len), low)
     return pl.pallas_call(
-        attend_forward_body,
+        forward_body,
         out_shape=(
-            jax.ShapeDtypeStruct((docs, seq_len, width), jnp.bfloat16),
-            jax.ShapeDtypeStruct((docs, seq_len, width), jnp.bfloat16),
-            jax.ShapeDtypeStruct((docs, pairs, 2, 2, seq_len, seq_len), jnp.bfloat16),
+            low_tokens, low_tokens,
+            jax.ShapeDtypeStruct((pairs, 2, 2, seq_len, seq_len), low),
+            jax.ShapeDtypeStruct((seq_len, width), jnp.float32),
+            jax.ShapeDtypeStruct((seq_len, width), jnp.float32),
+            low_tokens, low_tokens,
+            jax.ShapeDtypeStruct((2 * seq_len, width), low),
+            jax.ShapeDtypeStruct((seq_len, PAIR), low),
+            turned, turned,
+            jax.ShapeDtypeStruct((lines, width), jnp.float32),
+            low_tokens, low_tokens,
+            jax.ShapeDtypeStruct((2, seq_len, width), low),
+            jax.ShapeDtypeStruct((3, width, width), low),
+            jax.ShapeDtypeStruct((width, width), low),
+            jax.ShapeDtypeStruct((width, 2 * feed), low),
+            jax.ShapeDtypeStruct((2 * feed, width), low),
         ),
         grid_spec=pltpu.PrefetchScalarGridSpec(
-            num_scalar_prefetch=1,
-            grid=(docs, pairs),
-            in_specs=[
-                pl.BlockSpec((None, seq_len, 1), per_doc),
-                pl.BlockSpec((None, 1, seq_len), per_doc),
-                pl.BlockSpec((None, 1, seq_len), per_doc),
-                pl.BlockSpec((None, seq_len, PAIR), per_doc),
-                tile, tile, tile, tile,
-                pl.BlockSpec((2 * seq_len, PAIR), shared),
-                pl.BlockSpec((3, PAIR), shared),
-                pl.BlockSpec((2, PAIR), shared),
+            num_scalar_prefetch=0,
+            grid=(pairs,),
+            in_specs=[anywhere] * 11
+            + [
+                pl.BlockSpec(meta.shape, whole, pipeline_mode=once),
+                pl.BlockSpec(vectors.shape, whole, pipeline_mode=once),
+                pl.BlockSpec((2 * seq_len, width), whole, pipeline_mode=once),
             ],
             out_specs=[
                 tile, tile,
-                pl.BlockSpec((None, None, 2, 2, seq_len, seq_len), lambda d, p, *_: (d, p, 0, 0, 0, 0)),
-            ],
+                pl.BlockSpec((None, 2, 2, seq_len, seq_len), lambda p: (p, 0, 0, 0, 0)),
+                tile, tile, tile, tile,
+                pl.BlockSpec((2 * seq_len, PAIR), lambda p: (0, p)),
+                pl.BlockSpec((seq_len, PAIR), whole),
+                pl.BlockSpec((width, seq_len), whole),
+                pl.BlockSpec((width, seq_len), whole),
+                pl.BlockSpec((lines, width), whole),
+            ]
+            + [anywhere] * 7,
             scratch_shapes=[
+                pltpu.VMEM((2, seq_len, width), low),
+                pltpu.VMEM((4, width, width), low),
+                pltpu.VMEM(vectors.shape, jnp.float32),
+                pltpu.VMEM((width, feed), low),
+                pltpu.VMEM((feed, width), low),
+                pltpu.VMEM((cols, width), low),
+                pltpu.VMEM((2, half, width), low),
                 pltpu.VMEM((2, seq_len, seq_len), jnp.float32),
-                pltpu.VMEM((seq_len, 2 * PAIR), jnp.bfloat16),
+                pltpu.VMEM((seq_len, 2 * PAIR), low),
+                pltpu.VMEM((seq_len, PAIR), jnp.float32),
+                dma((2,)), dma((2,)), dma((2,)), dma((4,)), dma((4,)), dma((4,)),
+                dma((5,)), dma((10,)), dma((5,)), dma((5,)), dma, dma,
             ],
         ),
+        compiler_params=pltpu.CompilerParams(
+            collective_id=1, has_side_effects=True, vmem_limit_bytes=60 << 20
+        ),
         name="attend_forward",
-    )(lengths, rank_col, rank_row, live_row, seg_hot, proj_c, proj_q, keys, values, rel_keys, bias, embed)
+    )(content_in, query_in, content_cot, query_cot, query_w, key_w, value_w, rel_w, out_w, up_w, down_w, meta, vectors, table)
 
 
 GELU_A = 0.7978845608028654
@@ -148,7 +313,7 @@
 
 
 def feed_forward_body(
-    vec_c, vec_q, content, query, cot_c, cot_q, out_ref, up_ref, down_ref, up_bias, norms,
+    vec_c, vec_q, content, query, cots, out_ref, up_ref, down_ref, up_bias, norms,
     first_t, normal_ref, scale_ref, act_ref, slope_ref, grad_ref, low_ref, low_t, rows_ref, sums_ref,
     first_scr, total_scr,
 ):
@@ -191,7 +356,7 @@
             there = slice(stream * half_rows + at, stream * half_rows + at + ROWS)
             normal, scale = norm_parts(total_scr[there, :])
             rows_ref[there, :] = (normal * norms[2:3, :] + norms[3:4, :]).astype(jnp.bfloat16)
-            cot = (cot_c, cot_q)[stream][here, :].astype(jnp.float32)
+            cot = cots[stream, here, :].astype(jnp.float32)
             grad = norm_pull(normal, scale, cot * norms[2:3, :])
             grad_ref[there, :] = grad
             low = grad.astype(jnp.bfloat16)
@@ -202,7 +367,7 @@
         sums_ref[...] = jnp.concatenate(sums + [jnp.zeros((5, content.shape[1]), jnp.float32)], axis=0)
 
 
-def feed_forward(vec_c, vec_q, content, query, cot_c, cot_q, out_use, up_use, down_use, up_bias, norms):
+def feed_forward(vec_c, vec_q, content, query, cots, out_use, up_use, down_use, up_bias, norms):
     seq_len, width = content.shape
     hidden = up_use.shape[1]
     cols = width // 2
@@ -229,7 +394,8 @@
         ),
         grid=(hidden // cols,),
         in_specs=[
-            stream, stream, stream, stream, stream, stream,
+            stream, stream, stream, stream,
+            pl.BlockSpec(cots.shape, lambda f: (0, 0, 0), pipeline_mode=once),
             keep((width, width)),
             pl.BlockSpec((width, cols), side),
             pl.BlockSpec((cols, width), lambda f: (f, 0)),
@@ -254,10 +420,9 @@
         ],
         compiler_params=pltpu.CompilerParams(vmem_limit_bytes=60 << 20),
         name="feed_forward",
-    )(vec_c, vec_q, content, query, cot_c, cot_q, out_use, up_use, down_use, up_bias, norms)
-
-
-MESH = pl.DeviceIdType.MESH
+    )(vec_c, vec_q, content, query, cots, out_use, up_use, down_use, up_bias, norms)
+
+
 FOLDS = 4
 LAG = 2
 EARLY = 9
@@ -282,8 +447,8 @@
 
 def backward_body(dp_size, *refs):
     (
-        seg_hot, proj_c, proj_q, key_ref, value_ref, rel_ref, bias_ref, embed_ref, prob_ref,
-        query_w, key_w, value_w, vec_c, vec_q, content_t, query_t, table_t, out_w,
+        seg_hot, proj_c, proj_q, key_ref, value_ref, rel_ref, bias_ref, prob_ref,
+        square_w, vec_c, vec_q, content_t, query_t, table_t, out_w,
         act_ref, slope_ref, up_ref, down_ref, low_ref, low_t, first_t, normal_ref, scale_ref,
         norms, sums_in, grad_in, rows_in,
         sum_out, small_out, keep_out, rows_came, grad_came,
@@ -587,7 +752,7 @@
                 g_position = jnp.where(first, parts[0][1], parts[1][1])
                 g_same = jnp.where(first, parts[0][2], parts[1][2])
                 g_other = jnp.where(first, parts[0][3], parts[1][3])
-                g_segment = g_same * embed_ref[0:1, :] + g_other * embed_ref[1:2, :]
+                g_segment = g_same * bias_ref[3:4, :] + g_other * bias_ref[4:5, :]
                 gproj_ref[where, :PAIR] = (g_content + g_position + g_segment).astype(jnp.bfloat16)
                 terms = (g_content, g_position, g_segment, g_same * query_s, g_other * query_s)
                 sums = [old + jnp.sum(term, axis=0, keepdims=True) for old, term in zip(sums, terms)]
@@ -599,9 +764,9 @@
         g_query = triple[:, :PAIR] + nn(query_t[...], gproj_q[...])
         g_rel = nt(table_t[...], rel_acc[...].astype(jnp.bfloat16))
         vectors = jnp.concatenate(sums, axis=0)
-        weights = jnp.concatenate([query_w[...], key_w[...], value_w[...]], axis=1)
+        weights = jnp.concatenate([square_w[0], square_w[1], square_w[2]], axis=1)
         total[:seq_len, :] += nt(gproj_c[...], weights)
-        total[seq_len:, :] += nt(gproj_q[...], query_w[...])
+        total[seq_len:, :] += nt(gproj_q[...], square_w[0])
         late = turn % half_pairs
         piece = EARLY + late
         rel_piece = EARLY + half_pairs
@@ -686,7 +851,7 @@
 
 
 def backward(
-    dp_size, seg_hot, proj_c, proj_q, keys, values, rel_keys, bias, embed, prob, query_w, key_w, value_w,
+    dp_size, seg_hot, proj_c, proj_q, keys, values, rel_keys, lines, prob, squares,
     vec_c, vec_q, content_t, query_t, table_t, out_w, act, slope, up_w, down_w, low_rows, low_t, first_t,
     normal, scale, norms, sums, grad, rows_in,
 ):
@@ -706,7 +871,6 @@
     turn = lambda g: (jnp.maximum(g - feeds - 1, 0) + pairs // 2) % pairs
     per_pair = lambda g: (0, turn(g))
     tile = pl.BlockSpec((seq_len, PAIR), per_pair)
-    weight = pl.BlockSpec((width, PAIR), per_pair)
 
     def chunk(g):
         at = jnp.minimum(g, feeds - 1)
@@ -730,10 +894,9 @@
                 keep((seq_len, PAIR)),
                 tile, tile, tile, tile,
                 pl.BlockSpec((2 * seq_len, PAIR), per_pair),
-                pl.BlockSpec((3, PAIR), per_pair),
-                pl.BlockSpec((2, PAIR), per_pair),
+                pl.BlockSpec((lines.shape[0], PAIR), per_pair),
                 pl.BlockSpec((None, 2, 2, seq_len, seq_len), lambda g: (turn(g), 0, 0, 0, 0)),
-                weight, weight, weight,
+                pl.BlockSpec((3, width, PAIR), lambda g: (0, 0, turn(g))),
                 keep((seq_len, width)), keep((seq_len, width)),
                 keep((width, seq_len)), keep((width, seq_len)), keep((width, 2 * seq_len)),
                 keep((width, width)),
@@ -774,7 +937,7 @@
         ),
         name="backward",
     )(
-        seg_hot, proj_c, proj_q, keys, values, rel_keys, bias, embed, prob, query_w, key_w, value_w,
+        seg_hot, proj_c, proj_q, keys, values, rel_keys, lines, prob, squares,
         vec_c, vec_q, content_t, query_t, table_t, out_w, act, slope, up_w, down_w, low_rows, low_t, first_t,
         normal, scale, norms, sums, grad, rows_in,
     )
@@ -903,82 +1066,44 @@
     content_cot,
     query_cot,
 ):
-    docs_dev, half, width = content_in.shape
+    half, width = content_in.shape[1:]
     seq_len = order_ranks.shape[1]
-    mine = lax.axis_index("mp")
+    cols = query_weight.shape[1]
+    ff = up_weight.shape[1]
     wide_f = lambda value: value.astype(jnp.float32)
-    low_f = lambda value: value.astype(jnp.bfloat16)
-
-    def swap(value):
-        return lax.ppermute(value, "mp", [(0, 1), (1, 0)])
-
-    def gather_doc(value):
-        keep = lax.dynamic_index_in_dim(value, mine, 0, keepdims=False)
-        came = swap(lax.dynamic_index_in_dim(value, 1 - mine, 0, keepdims=False))
-        head = jnp.where(mine == 0, keep, came)
-        tail = jnp.where(mine == 0, came, keep)
-        return jnp.concatenate([head, tail], axis=0)
-
-    def both(value, axis):
-        return jnp.concatenate([value, swap(value)], axis=axis)
-
-    content = gather_doc(content_in)
-    query = gather_doc(query_in)
-    query_use = both(query_weight, 1)
-    key_use = both(key_weight, 1)
-    value_use = both(value_weight, 1)
-    rel_use = both(rel_weight, 1)
-    vectors = both(
-        jnp.concatenate(
-            [
-                wide_f(content_bias)[None],
-                wide_f(position_bias)[None],
-                wide_f(segment_bias)[None],
-                wide_f(segment_embed),
-            ],
-            axis=0,
-        ),
-        1,
+    meta = jnp.concatenate(
+        [order_ranks, segment_ids, target_flags, jnp.broadcast_to(doc_lengths[:, None], order_ranks.shape)], axis=0
+    ).astype(jnp.float32)
+    up_rows = ff // cols
+    vectors = jnp.concatenate(
+        [
+            content_bias[None], position_bias[None], segment_bias[None], segment_embed,
+            up_bias.reshape(up_rows, cols), jnp.zeros(((-5 - up_rows) % 8, cols), jnp.bfloat16),
+        ],
+        axis=0,
+    ).astype(jnp.float32)
+    table = position_table(seq_len, width)
+    (
+        vec_c, vec_q, prob, proj_c, proj_q, keys, values, rel_keys, seg_hot, content_t, query_t, lines,
+        content, query, cots, squares, out_use, up_use, down_use,
+    ) = forward(
+        content_in, query_in, content_cot, query_cot, query_weight, key_weight, value_weight, rel_weight,
+        out_weight, up_weight, down_weight, meta, vectors, jnp.asarray(table),
     )
-    bias, embed = vectors[:3], vectors[3:]
-    out_use = both(out_weight, 0)
-    up_use = both(up_weight, 1)
-    down_use = both(down_weight, 0)
-    up_bias_use = both(wide_f(up_bias)[None], 1)
-    cot_c = gather_doc(content_cot)
-    cot_q = gather_doc(query_cot)
-
-    lengths = lax.dynamic_slice_in_dim(doc_lengths, mine, 1, 0)
-    ranks = lax.dynamic_slice_in_dim(order_ranks, mine, 1, 0)
-    segments = lax.dynamic_slice_in_dim(segment_ids, mine, 1, 0)
-    targets = lax.dynamic_slice_in_dim(target_flags, mine, 1, 0)
-    live = targets * (jnp.arange(seq_len) >= 2).astype(jnp.int32)[None]
-    lanes = jnp.arange(PAIR)
-    seg_hot = low_f((segments[:, :, None] == lanes % 4) & (lanes < 8))
-    table = jnp.asarray(position_table(seq_len, width))
-    rel_keys = low_f(nn(table, rel_use))
-    proj_c = nn(content, query_use)[None]
-    proj_q = nn(query, query_use)[None]
-    keys = low_f(nn(content, key_use))[None]
-    values = low_f(nn(content, value_use))[None]
-    vec_c, vec_q, prob = attend_forward(
-        lengths, ranks[:, :, None], ranks[:, None, :], live[:, None, :], seg_hot,
-        proj_c, proj_q, keys, values, rel_keys, bias, embed,
+    up_bias_use = jnp.concatenate(
+        [lines[5 : 5 + up_rows, :cols].reshape(1, ff), lines[5 : 5 + up_rows, cols:].reshape(1, ff)], axis=1
     )
     norms = jnp.stack(
         [first_gain, first_shift, second_gain, second_shift, down_bias, down_bias, down_bias, down_bias]
     ).astype(jnp.float32)
     first_t, normal, scale, act, slope, grad, low_rows, low_t, rows_out, sums = feed_forward(
-        vec_c[0], vec_q[0], content, query, cot_c, cot_q, out_use, up_use, down_use, up_bias_use, norms
+        vec_c, vec_q, content, query, cots, out_use, up_use, down_use, up_bias_use, norms
     )
     pieces, tiny, keep_rows, rows_came, grad_came = backward(
-        dp_size, seg_hot[0], proj_c[0], proj_q[0], keys[0], values[0], rel_keys, bias, embed, prob[0],
-        query_use, key_use, value_use, vec_c[0], vec_q[0], jnp.transpose(content), jnp.transpose(query),
-        jnp.asarray(position_table(seq_len, width).T), out_use, act, slope, up_use, down_use,
+        dp_size, seg_hot, proj_c, proj_q, keys, values, rel_keys, lines, prob, squares,
+        vec_c, vec_q, content_t, query_t, jnp.asarray(table.T), out_use, act, slope, up_use, down_use,
         low_rows, low_t, first_t, normal, scale, norms, sums, grad, rows_out,
     )
-    ff = up_weight.shape[1]
-    cols = query_weight.shape[1]
     (
         content_out, query_out, content_grad, query_grad,
         down_sum, up_sum, out_sum, query_sum, key_sum, value_sum, rel_sum,

time: 374 us -> 314 us (0.84)
  local copies, waits for them, and re-layouts: 53.7 us -> 20.6 us
  matrix products: 9.89 us -> 0 us
  other arithmetic: 10.8 us -> 3.23 us
    concatenate x10 -> x2, local copies, waits for them, and re-layouts: 15.8 us -> 1.55 us  [the longest x1 0.82 us: on_device(): jnp.concatenate([content_bias[None], position_bias[None], segment_bias[No...]
    pallas_call x1, Pallas kernels: 208 us -> 195 us  [backward(): pl.pallas_call(functools.partial(backward_body, dp_size), out_shape=(jax....]
    pallas_call x1, Pallas kernels: 35.7 us -> 46.8 us  [forward(): pl.pallas_call(forward_body, out_shape=(low_tokens, low_tokens, jax.Shape...]
    unnamed x78 -> x11, local copies, waits for them, and re-layouts: 16 us -> 5.58 us
    dot_general x5 -> x0, matrix products: 9.89 us -> none  [nn(): return jnp.dot(left_op, right_op, preferred_element_type=jnp.float32)]
    dynamic_slice x12 -> x0, local copies, waits for them, and re-layouts: 9.77 us -> none  [the longest x6 4.57 us: gather_doc(): keep = lax.dynamic_index_in_dim(value, mine, 0, keepdims=False)]
    concatenate x8 -> x1, other arithmetic: 6.74 us -> 0.61 us  [on_device(): jnp.concatenate([lines[5:5 + up_rows, :cols].reshape(1, ff), lines[5:5 +...]
  transfers between devices with their start and end apart: 13 -> 0, of which waited for: 2 -> 0; matrix products, arithmetic and copies ran while one was open for 15% -> 0% of each run, Pallas kernels for 10% -> 0%
where the time goes in v5:
time: 314 us; the launch traced here: 313 us
  Pallas kernels  289 us (92%)
  local copies, waits for them, and re-layouts  20.6 us (7%)
  other arithmetic  3.23 us (1%)
    pallas_call x1, Pallas kernels, backward(): pl.pallas_call(functools.partial(backward_body, dp_size), out_shape=(jax....  195 us
    pallas_call x1, Pallas kernels, forward(): pl.pallas_call(forward_body, out_shape=(low_tokens, low_tokens, jax.Shape...  46.8 us
    pallas_call x1, Pallas kernels, feed_forward(): pl.pallas_call(feed_forward_body, out_shape=(jax.ShapeDtypeStruct((width,...  32.4 us
    pallas_call x1, Pallas kernels, finish(): pl.pallas_call(finish_body, out_shape=(pair, pair, pair, pair, jax.ShapeD...  14.7 us

profile of v5, /device:TPU:0, one launch (start us, length us, event | category | flops | bytes accessed | tf_op | source)
XLA Modules:
  0.0 313.2 jit_solution(10133589986239754068)
XLA Ops:
  0.7 0.7 pad.5.clone
  1.4 0.7 broadcast_in_dim.19
  2.1 0.7 broadcast_in_dim.20
  2.8 0.7 broadcast_in_dim.21
  3.4 0.7 stack.21
  4.1 0.7 stack.22
  4.8 0.7 reshape.69
  5.5 0.7 stack.25
  6.2 0.7 stack.23
  6.9 0.7 stack.24
  7.6 0.8 concatenate.10
  8.4 0.6 convert_element_type.11.norms.refs_24_
  9.1 0.6 convert_element_type.10.vector_ref
  9.7 1.4 add_convert_fusion.meta_ref
  11.1 46.8 %attend_forward.1 = (bf16[512,768]{1,0:T(8,128)(2,1)}, bf16[512,768]{1,0:T(8,128)(2,1)}, bf16[6,2,2,512,512]{4,3,2,1,0:T(8,128)(2,1)}, f32[512,768]{1,0:T(8,128)...) custom-call(bf16[2,256,768]{2,1,0:T(8,128)(2,1)} %content_in.1, ...), custom_call_target="tpu_custom_call" | custom-call | tf_op jit(solution)/shard_map/attend_forward/pallas_call | solution.py:236
  57.9 0.8 slice_bitcast_fusion.1
  58.7 0.6 pad_maximum_fusion.up_bias
  59.3 32.4 %feed_forward.1 = (bf16[768,1024]{1,0:T(8,128)(2,1)}, bf16[1024,768]{1,0:T(8,128)(2,1)}, f32[1024,1]{1,0:T(8,128)}, bf16[1024,3072]{1,0:T(8,128)(2,1)}, bf16[102...) custom-call(bf16[512,768]{1,0:T(8,128)(2,1)} %get-tuple-element.75.v, ...), custom_call_target="tpu_custom_call" | custom-call | tf_op jit(solution)/shard_map/feed_forward/pallas_call | solution.py:381
  91.7 194.8 %backward.1 = (bf16[13,768,384]{2,1,0:T(8,128)(2,1)}, f32[24,384]{1,0:T(8,128)}, bf16[2,256,768]{2,1,0:T(8,128)(2,1)}, bf16[2,256,768]{2,1,0:T(8,128)(2,1)}, bf16[2,256,768]{2,1,0:T(8,128)(2,1)}) custom-call(bf16[512,128]{1,0:T(8,128)(2,1)} %get-tuple-element.66.refs_0_, f32[512,768]{1,0:T(8,128)} %get-tuple-element.67.refs_1_, ...), custom_call_target="tpu_custom_call" | custom-call | tf_op jit(solution)/shard_map/backward/pallas_call | solution.py:881
  286.5 0.7 slice.60
  287.3 0.6 reshape.73
  287.9 1.4 slice_reduce_fusion
  289.3 1.4 fusion
  290.7 0.6 squeeze.31
  291.3 0.6 squeeze.29
  291.9 0.6 squeeze.28
  292.5 0.6 squeeze.27
  293.7 1.4 copy-done
  295.2 1.1 copy-done.1
  296.3 1.1 copy-done.2
  297.4 1.1 copy-done.3
  298.6 14.7 %finish.1 = (bf16[2,256,768]{2,1,0:T(8,128)(2,1)}, bf16[2,256,768]{2,1,0:T(8,128)(2,1)}, bf16[2,256,768]{2,1,0:T(8,128)(2,1)}, bf16[2,256,768]{2,1,0:T(8,128)(2,...) custom-call(bf16[13,768,384]{2,1,0:T(8,128)(2,1)} %get-tuple-element, ...), custom_call_target="tpu_custom_call" | custom-call | tf_op jit(solution)/shard_map/finish/pallas_call | solution.py:1004
  (9 shorter events, 0.7 us)
Async XLA Ops:
  293.7 1.4 copy-start
  295.2 1.1 copy-start.1
  296.3 1.1 copy-start.2
  297.4 1.1 copy-start.3

commit v6 on v5

--- a/solution.py
+++ b/solution.py
@@ -33,10 +33,10 @@
 
 def forward_body(
     content_in, query_in, content_cot, query_cot, query_w, key_w, value_w, rel_w, out_w, up_w, down_w,
-    meta_ref, vector_ref, table_ref,
-    vec_c, vec_q, prob_ref, proj_c, proj_q, key_ref, value_ref, rel_ref, hot_ref, content_t, query_t, vectors_out,
+    length_ref, order_ref, segment_ref, target_ref, cbias_ref, pbias_ref, sbias_ref, embed_ref, ubias_ref, table_ref,
+    vec_c, vec_q, prob_ref, proj_c, proj_q, key_ref, value_ref, rel_ref, hot_ref, content_t, query_t, vectors_out, ubias_out,
     content_out, query_out, cots_out, square_out, out_all, up_all, down_all,
-    tokens, squares, vectors, bounce_up, bounce_down, bounce_out, bounce_cot, mask_scr, ext_scr, rank_scr,
+    tokens, squares, near_pack, far_pack, bounce_up, bounce_down, bounce_out, bounce_cot, mask_scr, ext_scr, rank_scr,
     token_sem, token_send, token_recv, square_sem, square_send, square_recv,
     bulk_load, bulk_store, bulk_send, bulk_recv, vector_send, vector_recv,
 ):
@@ -73,7 +73,7 @@
         remote(square_in[at], squares.at[at, :, cols:], square_send.at[at], square_recv.at[at])
         for at in range(4)
     ]
-    vector_swap = remote(vector_ref, vectors, vector_send, vector_recv)
+    vector_swap = remote(near_pack, far_pack, vector_send, vector_recv)
     cot_in = (content_cot, query_cot)
     bulk_loads = [
         pltpu.make_async_copy(out_w, bounce_out, bulk_load.at[0]),
@@ -108,24 +108,30 @@
     def _():
         for copy in token_load + square_load:
             copy.start()
+        near_pack[...] = jnp.zeros_like(near_pack)
+        for at, part in enumerate((cbias_ref, pbias_ref, sbias_ref)):
+            near_pack[at : at + 1, :cols] = part[...].astype(jnp.float32).reshape(1, cols)
+        near_pack[3:5, :cols] = embed_ref[...].astype(jnp.float32)
+        near_pack[5:6, :] = ubias_ref[...].astype(jnp.float32).reshape(1, feed)
+        vectors_out[:, :cols] = near_pack[:, :cols]
+        ubias_out[:, :feed] = near_pack[5:6, :]
         barrier = pltpu.get_barrier_semaphore()
         pl.semaphore_signal(barrier, inc=1, device_id=other, device_id_type=MESH)
         pl.semaphore_wait(barrier, 1)
         for copy in token_swap + [vector_swap] + square_swap + bulk_swaps + bulk_loads:
             copy.start()
-        vectors_out[:, :cols] = vector_ref[...]
         place_j = lax.broadcasted_iota(jnp.int32, (1, seq_len), 1)
-        ranks = meta_ref[pl.ds(core, 1), :]
-        segments = meta_ref[pl.ds(2 + core, 1), :]
-        targets = meta_ref[pl.ds(4 + core, 1), :]
-        length = meta_ref[pl.ds(6 + core, 1), :]
+        ranks = order_ref[pl.ds(core, 1), :].astype(jnp.float32)
+        segments = segment_ref[pl.ds(core, 1), :].astype(jnp.float32)
+        targets = target_ref[pl.ds(core, 1), :].astype(jnp.float32)
+        length = length_ref[core]
         live = jnp.where(place_j >= 2, targets, 0.0)
         rank_scr[...] = jnp.transpose(jnp.broadcast_to(ranks, (PAIR, seq_len)))
         lane = lane_ids(seq_len)
         seg_turn = jnp.transpose(jnp.broadcast_to(segments, (PAIR, seq_len)))
         hot = (seg_turn == (lane % 4).astype(jnp.float32)) & (lane < 8)
         hot_ref[...] = jnp.where(hot, 1.0, 0.0).astype(jnp.bfloat16)
-        base = jnp.where(place_j.astype(jnp.float32) < length, 0.0, NEG)
+        base = jnp.where(place_j < length, 0.0, NEG)
         for block in range(blocks):
             rows = slice(block * ROWS, (block + 1) * ROWS)
             rank_i = jnp.concatenate([rank_scr[rows, :]] * (seq_len // PAIR), axis=1)
@@ -157,7 +163,8 @@
             copy.wait_recv()
         for copy in square_store:
             copy.start()
-        vectors_out[:, cols:] = vectors[...]
+        vectors_out[:, cols:] = far_pack[:, :cols]
+        ubias_out[:, feed:] = far_pack[5:6, :]
 
     pair_lanes = pl.ds(pl.multiple_of(step * PAIR, PAIR), PAIR)
     lines = vectors_out[:, pair_lanes]
@@ -218,17 +225,21 @@
             copy.wait()
 
 
-def forward(content_in, query_in, content_cot, query_cot, query_w, key_w, value_w, rel_w, out_w, up_w, down_w, meta, vectors, table):
-    docs, half, width = content_in.shape
+def forward(
+    content_in, query_in, content_cot, query_cot, query_w, key_w, value_w, rel_w, out_w, up_w, down_w,
+    lengths, orders, segments, targets, cbias, pbias, sbias, embed, ubias, table,
+):
+    once = pl.Buffered(1)
+    half, width = content_in.shape[1:]
     seq_len = 2 * half
     pairs = width // PAIR
     cols = query_w.shape[1]
     feed = up_w.shape[1]
-    lines = vectors.shape[0]
+    lines = 8
+    keep = lambda shape: pl.BlockSpec(shape, lambda p: (0,) * len(shape), pipeline_mode=once)
     low = jnp.bfloat16
     dma = pltpu.SemaphoreType.DMA
     whole = lambda p: (0, 0)
-    once = pl.Buffered(1)
     anywhere = pl.BlockSpec(memory_space=pl.ANY)
     tile = pl.BlockSpec((seq_len, PAIR), lambda p: (0, p))
     low_tokens = jax.ShapeDtypeStruct((seq_len, width), low)
@@ -245,6 +256,7 @@
             jax.ShapeDtypeStruct((seq_len, PAIR), low),
             turned, turned,
             jax.ShapeDtypeStruct((lines, width), jnp.float32),
+            jax.ShapeDtypeStruct((1, 2 * feed), jnp.float32),
             low_tokens, low_tokens,
             jax.ShapeDtypeStruct((2, seq_len, width), low),
             jax.ShapeDtypeStruct((3, width, width), low),
@@ -257,9 +269,10 @@
             grid=(pairs,),
             in_specs=[anywhere] * 11
             + [
-                pl.BlockSpec(meta.shape, whole, pipeline_mode=once),
-                pl.BlockSpec(vectors.shape, whole, pipeline_mode=once),
-                pl.BlockSpec((2 * seq_len, width), whole, pipeline_mode=once),
+                pl.BlockSpec(memory_space=pltpu.SMEM),
+                keep(orders.shape), keep(orders.shape), keep(orders.shape),
+                keep(cbias.shape), keep(cbias.shape), keep(cbias.shape), keep(embed.shape), keep(ubias.shape),
+                keep((2 * seq_len, width)),
             ],
             out_specs=[
                 tile, tile,
@@ -270,12 +283,14 @@
                 pl.BlockSpec((width, seq_len), whole),
                 pl.BlockSpec((width, seq_len), whole),
                 pl.BlockSpec((lines, width), whole),
+                pl.BlockSpec((1, 2 * feed), whole),
             ]
             + [anywhere] * 7,
             scratch_shapes=[
                 pltpu.VMEM((2, seq_len, width), low),
                 pltpu.VMEM((4, width, width), low),
-                pltpu.VMEM(vectors.shape, jnp.float32),
+                pltpu.VMEM((lines, feed), jnp.float32),
+                pltpu.VMEM((lines, feed), jnp.float32),
                 pltpu.VMEM((width, feed), low),
                 pltpu.VMEM((feed, width), low),
                 pltpu.VMEM((cols, width), low),
@@ -291,7 +306,10 @@
             collective_id=1, has_side_effects=True, vmem_limit_bytes=60 << 20
         ),
         name="attend_forward",
-    )(content_in, query_in, content_cot, query_cot, query_w, key_w, value_w, rel_w, out_w, up_w, down_w, meta, vectors, table)
+    )(
+        content_in, query_in, content_cot, query_cot, query_w, key_w, value_w, rel_w, out_w, up_w, down_w,
+        lengths, orders, segments, targets, cbias, pbias, sbias, embed, ubias, table,
+    )
 
 
 GELU_A = 0.7978845608028654
@@ -313,8 +331,9 @@
 
 
 def feed_forward_body(
-    vec_c, vec_q, content, query, cots, out_ref, up_ref, down_ref, up_bias, norms,
-    first_t, normal_ref, scale_ref, act_ref, slope_ref, grad_ref, low_ref, low_t, rows_ref, sums_ref,
+    vec_c, vec_q, content, query, cots, out_ref, up_ref, down_ref, up_bias,
+    gain1_ref, shift1_ref, gain2_ref, shift2_ref, dbias_ref,
+    first_t, normal_ref, scale_ref, act_ref, slope_ref, grad_ref, low_ref, low_t, rows_ref, sums_ref, norms,
     first_scr, total_scr,
 ):
     step = pl.program_id(0)
@@ -323,6 +342,9 @@
 
     @pl.when(step == 0)
     def _():
+        norms[...] = jnp.zeros_like(norms)
+        for at, part in enumerate((gain1_ref, shift1_ref, gain2_ref, shift2_ref, dbias_ref)):
+            norms[at : at + 1, :] = part[...].astype(jnp.float32).reshape(1, part.shape[0])
         for stream, at in chunks:
             here = pl.ds(at, ROWS)
             there = slice(stream * half_rows + at, stream * half_rows + at + ROWS)
@@ -367,10 +389,10 @@
         sums_ref[...] = jnp.concatenate(sums + [jnp.zeros((5, content.shape[1]), jnp.float32)], axis=0)
 
 
-def feed_forward(vec_c, vec_q, content, query, cots, out_use, up_use, down_use, up_bias, norms):
+def feed_forward(vec_c, vec_q, content, query, cots, out_use, up_use, down_use, up_bias, vectors):
     seq_len, width = content.shape
     hidden = up_use.shape[1]
-    cols = width // 2
+    cols = 512
     rows = 2 * seq_len
     low = jnp.bfloat16
     once = pl.Buffered(1)
@@ -391,6 +413,7 @@
             jax.ShapeDtypeStruct((width, rows), low),
             jax.ShapeDtypeStruct((rows, width), low),
             jax.ShapeDtypeStruct((8, width), jnp.float32),
+            jax.ShapeDtypeStruct((8, width), jnp.float32),
         ),
         grid=(hidden // cols,),
         in_specs=[
@@ -400,7 +423,8 @@
             pl.BlockSpec((width, cols), side),
             pl.BlockSpec((cols, width), lambda f: (f, 0)),
             pl.BlockSpec((1, cols), side),
-            keep((8, width)),
+            pl.BlockSpec((width,), lambda f: (0,)), pl.BlockSpec((width,), lambda f: (0,)), pl.BlockSpec((width,), lambda f: (0,)),
+            pl.BlockSpec((width,), lambda f: (0,)), pl.BlockSpec((width,), lambda f: (0,)),
         ],
         out_specs=[
             pl.BlockSpec((width, rows), whole),
@@ -413,6 +437,7 @@
             pl.BlockSpec((width, rows), whole),
             pl.BlockSpec((rows, width), whole),
             pl.BlockSpec((8, width), whole),
+            pl.BlockSpec((8, width), whole),
         ],
         scratch_shapes=[
             pltpu.VMEM((rows, width), low),
@@ -420,53 +445,37 @@
         ],
         compiler_params=pltpu.CompilerParams(vmem_limit_bytes=60 << 20),
         name="feed_forward",
-    )(vec_c, vec_q, content, query, cots, out_use, up_use, down_use, up_bias, norms)
+    )(vec_c, vec_q, content, query, cots, out_use, up_use, down_use, up_bias, *vectors)
 
 
 FOLDS = 4
-LAG = 2
-EARLY = 9
-COUNT = 13
-
-
-def shear_left(value_in):
-    rows, wide = value_in.shape
-    pack = 16
-    groups = []
-    for group in range(rows // pack):
-        piece = value_in[group * pack : (group + 1) * pack]
-        groups.append(pltpu.roll(piece, wide - 1 - group * pack, 1))
-    moved = jnp.concatenate(groups, axis=0)
-    place = lax.broadcasted_iota(jnp.int32, (rows, wide), 0)
-    step = 1
-    while step < pack:
-        moved = jnp.where((place & step) != 0, pltpu.roll(moved, wide - step, 1), moved)
-        step = step * 2
-    return moved
+EARLY = 7
+COUNT = 10
+CHUNK = 512
 
 
 def backward_body(dp_size, *refs):
     (
         seg_hot, proj_c, proj_q, key_ref, value_ref, rel_ref, bias_ref, prob_ref,
-        square_w, vec_c, vec_q, content_t, query_t, table_t, out_w,
-        act_ref, slope_ref, up_ref, down_ref, low_ref, low_t, first_t, normal_ref, scale_ref,
-        norms, sums_in, grad_in, rows_in,
+        square_w, vec_c, vec_q, out_w, act_ref, slope_ref, up_ref, down_ref, low_ref, scale_ref, norms, sums_in,
+        content_t, query_t, table_t, low_t, first_t, normal_in, grad_in, rows_in,
         sum_out, small_out, keep_out, rows_came, grad_came,
-        vt_scr, key_acc, value_acc, rel_acc, total, vec_grad, hid_scr,
+        vt_scr, key_acc, value_acc, rel_acc, total, vec_grad, hid_scr, turn_a, turn_b, flip_scr,
         work, swapped, landed, extra, small_work, small_far, small_land,
         store_sem, swap_send, swap_recv, fold_send, fold_recv, spread_send, spread_recv,
-        more_send, more_recv, tiny_send, tiny_recv, grad_sem, keep_sem, back_send, back_recv,
+        more_send, more_recv, tiny_send, tiny_recv, side_sem, keep_sem, back_send, back_recv,
     ) = refs
-    gproj_c = hid_scr.at[: key_ref.shape[0], :]
-    gproj_q = hid_scr.at[key_ref.shape[0] :, :PAIR]
-    ext_scr = hid_scr.at[key_ref.shape[0] :, PAIR:]
+    seq_len = key_ref.shape[0]
+    gproj_c = hid_scr.at[:seq_len, : 3 * PAIR]
+    gproj_q = hid_scr.at[seq_len:, :PAIR]
+    ext_scr = hid_scr.at[seq_len:, PAIR : 3 * PAIR]
     grid_at = pl.program_id(0)
-    feeds = 8
+    feeds = 6
     pairs = 6
     half_pairs = pairs // 2
     last = pl.num_programs(0) - 1
-    rows, cols = work.shape[1:]
-    seq_len = key_ref.shape[0]
+    rows, width = total.shape[1], work.shape[2]
+    cols = rows // 2
     place = lax.axis_index("dp")
     core = lax.axis_index("mp")
     strides = [1 + core, 2 - core, 4, 8]
@@ -480,8 +489,8 @@
         begin = begin + bit * length
         starts.append(begin)
     land_at = [rows - 2 * length for length in lengths]
-    offsets = [number * LAG for number in range(2 * FOLDS + 1)]
-    final_slot = 20
+    offsets = [0, 3, 5, 7, 9, 11, 13, 15, 18]
+    final_slot = 25
 
     def kept(fold):
         return pl.ds(pl.multiple_of(starts[fold], 16), lengths[fold])
@@ -561,7 +570,20 @@
             keep_out.at[stream], keep_sem.at[stream],
         )
 
-    grad_load = pltpu.make_async_copy(grad_in, total, grad_sem)
+    side_loads = [
+        pltpu.make_async_copy(source, target, side_sem.at[at])
+        for at, (source, target) in enumerate(
+            (
+                (grad_in, total),
+                (first_t, turn_a),
+                (low_t, turn_b),
+                (normal_in, vec_grad),
+                (table_t, turn_a),
+                (content_t, turn_b.at[:, :seq_len]),
+                (query_t, turn_b.at[:, seq_len:]),
+            )
+        )
+    ]
 
     def stage(number, piece):
         if number == 0:
@@ -593,12 +615,11 @@
     def advance(tick):
         for number in reversed(range(2 * FOLDS + 1)):
             slot = tick - offsets[number]
-            piece = jnp.where(slot < EARLY, slot, EARLY + (slot - 14) // 2)
-
-            @pl.when(
-                (slot >= 0)
-                & ((slot < EARLY) | (slot == 15) | (slot == 17) | (slot == 19) | (slot == final_slot))
-            )
+            early = (slot == 3) | (slot == 4) | (slot == 7) | (slot == 8) | (slot == 11) | (slot == 12)
+            late = (slot == 13) | (slot == 17) | (slot == 21) | (slot == final_slot)
+            piece = jnp.where(slot < 13, 2 * ((slot - 3) // 4) + (slot - 3) % 4, EARLY - 1 + (slot - 13) // 4)
+
+            @pl.when(early | late)
             def _():
                 stage(number, piece)
 
@@ -612,7 +633,8 @@
         for device in tiny_devices:
             pl.semaphore_signal(barrier, inc=1, device_id=device, device_id_type=MESH)
         pl.semaphore_wait(barrier, len(tiny_devices))
-        grad_load.start()
+        for copy in side_loads[:4]:
+            copy.start()
         rows_copy(0).start()
         rows_copy(1).start()
         small_work[0] = jnp.zeros_like(small_work[0])
@@ -620,16 +642,20 @@
         for at in range(3):
             for side in range(2):
                 line = sums_in[at : at + 1, side * cols : (side + 1) * cols]
-                spot = slice(13 + 2 * at + side, 14 + 2 * at + side)
-                small_work[0, spot, :] = line
-                small_far[spot, :] = line
-        grad_load.wait()
+                spot = slice(12 + 2 * at + side, 13 + 2 * at + side)
+                small_work[0, spot, :cols] = line
+                small_far[spot, :cols] = line
+        line_at = lax.broadcasted_iota(jnp.int32, (ROWS, ROWS), 0)
+        lane_at = lax.broadcasted_iota(jnp.int32, (ROWS, ROWS), 1)
+        flip_scr[...] = jnp.where(line_at + lane_at == ROWS - 1, 1.0, 0.0).astype(jnp.bfloat16)
+        for copy in side_loads[:3]:
+            copy.wait()
 
     @pl.when(grid_at < feeds)
     def _():
         chunk = grid_at // 2
         near = grid_at % 2 == 1
-        bias_sum = jnp.zeros((1, cols), jnp.float32)
+        bias_sum = jnp.zeros((1, width), jnp.float32)
         for at in range(0, total.shape[0], ROWS):
             here = slice(at, at + ROWS)
             grad_act = nt(low_ref[here, :], down_ref[...])
@@ -638,6 +664,8 @@
             bias_sum = bias_sum + jnp.sum(hid.astype(jnp.float32), axis=0, keepdims=True)
             total[here, :] += nt(hid, up_ref[...])
 
+        advance(2 * grid_at)
+
         @pl.when(near)
         def _():
             swap_copy(2 * chunk).wait_send()
@@ -645,8 +673,8 @@
 
         for at in range(0, rows, ROWS):
             here = slice(at, at + ROWS)
-            work[2 * chunk, here, :] = nn(low_t[here, :], act_ref[...]).astype(jnp.bfloat16)
-            work[2 * chunk + 1, here, :] = nn(first_t[here, :], hid_scr[...]).astype(jnp.bfloat16)
+            work[2 * chunk, here, :] = nn(turn_b[here, :], act_ref[...]).astype(jnp.bfloat16)
+            work[2 * chunk + 1, here, :] = nn(turn_a[here, :], hid_scr[...]).astype(jnp.bfloat16)
 
         @pl.when(near)
         def _():
@@ -662,21 +690,23 @@
 
     @pl.when(grid_at == feeds)
     def _():
-        sums = [jnp.zeros((1, 2 * cols), jnp.float32) for _ in range(2)]
+        advance(2 * grid_at)
+        for copy in side_loads[4:]:
+            copy.start()
+        side_loads[3].wait()
+        sums = [jnp.zeros((1, rows), jnp.float32) for _ in range(2)]
         out_piece = EARLY - 1
         near_sum = jnp.zeros((rows, cols), jnp.float32)
         far_sum = jnp.zeros((rows, cols), jnp.float32)
         for at in range(0, total.shape[0], ROWS):
             here = slice(at, at + ROWS)
-            normal = normal_ref[here, :].astype(jnp.float32)
+            normal = vec_grad[here, :].astype(jnp.float32)
             grad = total[here, :]
             sums[0] = sums[0] + jnp.sum(grad * normal, axis=0, keepdims=True)
             sums[1] = sums[1] + jnp.sum(grad, axis=0, keepdims=True)
             grad = norm_pull(normal, scale_ref[here, :], grad * norms[0:1, :])
             total[here, :] = grad
-            low = grad.astype(jnp.bfloat16)
-            hid_scr[here, :] = low[:, :cols]
-            vec_grad[here, :] = low
+            vec_grad[here, :] = grad.astype(jnp.bfloat16)
         for at in range(0, total.shape[0], ROWS):
             here = slice(at, at + ROWS)
             low = vec_grad[here, :]
@@ -685,21 +715,31 @@
             far_sum = far_sum + nn(low_turn, vec[:, cols:])
             near_sum = near_sum + nn(low_turn, vec[:, :cols])
             vec_grad[here, :] = nt(low, out_w[...]).astype(jnp.bfloat16)
-        work[out_piece] = far_sum.astype(jnp.bfloat16)
+        work[out_piece, :, :cols] = far_sum.astype(jnp.bfloat16)
+        work[out_piece, :, cols:] = jnp.zeros((rows, width - cols), jnp.bfloat16)
         swap_copy(out_piece).start()
         for at in range(2):
             for side in range(2):
                 line = sums[at][:, side * cols : (side + 1) * cols]
-                spot = slice(9 + 2 * at + side, 10 + 2 * at + side)
-                small_work[0, spot, :] = line
-                small_far[spot, :] = line
+                spot = slice(8 + 2 * at + side, 9 + 2 * at + side)
+                small_work[0, spot, :cols] = line
+                small_far[spot, :cols] = line
         swap_copy(out_piece).wait()
-        work[out_piece] = (near_sum + swapped[out_piece].astype(jnp.float32)).astype(jnp.bfloat16)
+        near_sum = near_sum + swapped[out_piece, :, :cols].astype(jnp.float32)
+        work[out_piece, :, :cols] = near_sum.astype(jnp.bfloat16)
 
     @pl.when(grid_at > feeds)
     def _():
         turn = grid_at - feeds - 1
-        pair = (turn + half_pairs) % pairs
+        late = turn // 2
+        near = turn % 2 == 1
+        pair = late + (1 - turn % 2) * half_pairs
+
+        @pl.when(turn == 0)
+        def _():
+            for copy in side_loads[4:]:
+                copy.wait()
+
         pair_lanes = pl.ds(pl.multiple_of(pair * PAIR, PAIR), PAIR)
         blocks = seq_len // ROWS
         wide = seq_len + ROWS
@@ -721,7 +761,8 @@
                 start = seq_len - (block + 1) * ROWS
                 proj = proj_ref[where, :]
                 query_ct = jnp.transpose(((proj + bias_ref[0:1, :]) * 0.125).astype(jnp.bfloat16))
-                query_pt = jnp.transpose(((proj + bias_ref[1:2, :]) * 0.125).astype(jnp.bfloat16))
+                query_p = ((proj + bias_ref[1:2, :]) * 0.125).astype(jnp.bfloat16)
+                query_pt = jnp.transpose(nn(flip_scr[...], query_p).astype(jnp.bfloat16))
                 query_s = proj + bias_ref[2:3, :]
                 hot = jnp.where(lane < 4, seg_hot[where, :].astype(jnp.float32), 0.0)
                 grad = vec_grad[pl.ds(stream * seq_len + block * ROWS, ROWS), pair_lanes]
@@ -739,8 +780,9 @@
                     value_acc[low:high, :] += nn(grad_t[low:high, :], prob)
                     key_acc[low:high, :] += nn(query_ct[low:high, :], gscore)
                     both = nn(gscore, ext_scr[...])
-                    table = jnp.concatenate([jnp.zeros((ROWS, ROWS), jnp.bfloat16), gscore], axis=1)
-                    table = shear_left(table)
+                    table = nn(flip_scr[...], gscore).astype(jnp.bfloat16)
+                    table = jnp.concatenate([table, jnp.zeros((ROWS, ROWS), jnp.bfloat16)], axis=1)
+                    table = pltpu.roll(table, 0, 1, stride=1, stride_axis=0)
                     gpos = nn(table, window)
                     rel_acc[low:high, start : start + wide] += nn(query_pt[low:high, :], table)
                     tail = both[:, PAIR:]
@@ -749,7 +791,8 @@
                     g_other = jnp.sum(tail, axis=1, keepdims=True) - g_same
                     parts.append((both[:, :PAIR], gpos, g_same, g_other))
                 g_content = jnp.where(first, parts[0][0], parts[1][0])
-                g_position = jnp.where(first, parts[0][1], parts[1][1])
+                g_position = jnp.where(first, parts[0][1], parts[1][1]).astype(jnp.bfloat16)
+                g_position = nn(flip_scr[...], g_position)
                 g_same = jnp.where(first, parts[0][2], parts[1][2])
                 g_other = jnp.where(first, parts[0][3], parts[1][3])
                 g_segment = g_same * bias_ref[3:4, :] + g_other * bias_ref[4:5, :]
@@ -757,63 +800,53 @@
                 terms = (g_content, g_position, g_segment, g_same * query_s, g_other * query_s)
                 sums = [old + jnp.sum(term, axis=0, keepdims=True) for old, term in zip(sums, terms)]
             if stream == 0:
-                advance(2 * grid_at - 10)
+                advance(2 * grid_at)
         gproj_c[:, PAIR : 2 * PAIR] = jnp.transpose(key_acc[...]).astype(jnp.bfloat16)
         gproj_c[:, 2 * PAIR :] = jnp.transpose(value_acc[...]).astype(jnp.bfloat16)
-        triple = nn(content_t[...], gproj_c[...])
-        g_query = triple[:, :PAIR] + nn(query_t[...], gproj_q[...])
-        g_rel = nt(table_t[...], rel_acc[...].astype(jnp.bfloat16))
+        triple = nn(turn_b[:, :seq_len], gproj_c[...])
+        g_query = triple[:, :PAIR] + nn(turn_b[:, seq_len:], gproj_q[...])
+        g_rel = nt(turn_a[...], rel_acc[...].astype(jnp.bfloat16))
         vectors = jnp.concatenate(sums, axis=0)
+        piece = EARLY + late
+        lanes = pl.ds(pl.multiple_of(late * PAIR, PAIR), PAIR)
+
+        @pl.when(near)
+        def _():
+            swap_copy(piece).wait_send()
+
+        work[piece, :, :PAIR] = g_query.astype(jnp.bfloat16)
+        work[piece, :, PAIR : 3 * PAIR] = triple[:, PAIR:].astype(jnp.bfloat16)
+        work[piece, :, 3 * PAIR :] = g_rel.astype(jnp.bfloat16)
+
+        @pl.when(jnp.logical_not(near))
+        def _():
+            small_far[0:5, lanes] = vectors
+            swap_copy(piece).start()
+
+            @pl.when(turn == pairs - 2)
+            def _():
+                tiny_copy(0).start()
+
+        @pl.when(near)
+        def _():
+            small_work[0, 0:5, lanes] = vectors
+            settle(piece)
+
         weights = jnp.concatenate([square_w[0], square_w[1], square_w[2]], axis=1)
         total[:seq_len, :] += nt(gproj_c[...], weights)
         total[seq_len:, :] += nt(gproj_q[...], square_w[0])
-        late = turn % half_pairs
-        piece = EARLY + late
-        rel_piece = EARLY + half_pairs
-        lanes = pl.ds(pl.multiple_of(late * PAIR, PAIR), PAIR)
-
-        @pl.when(turn >= half_pairs)
-        def _():
-            swap_copy(piece).wait_send()
-
-            @pl.when(turn == half_pairs)
-            def _():
-                swap_copy(rel_piece).wait_send()
-
-        work[piece, :, :PAIR] = g_query.astype(jnp.bfloat16)
-        work[piece, :, PAIR:] = triple[:, PAIR:].astype(jnp.bfloat16)
-        work[rel_piece, :, lanes] = g_rel.astype(jnp.bfloat16)
-
-        @pl.when(turn < half_pairs)
-        def _():
-            small_far[0:5, lanes] = vectors
-            swap_copy(piece).start()
-
-            @pl.when(turn == half_pairs - 1)
-            def _():
-                swap_copy(rel_piece).start()
-                tiny_copy(0).start()
-
-        @pl.when(turn >= half_pairs)
-        def _():
-            small_work[0, 0:5, lanes] = vectors
-            settle(piece)
-
-            @pl.when(turn == pairs - 1)
-            def _():
-                settle(rel_piece)
-
-    advance(grid_at - 1 + (grid_at // (feeds + 1)) * (grid_at - feeds))
+
+    advance(2 * grid_at + 1)
 
     @pl.when(grid_at == last)
     def _():
         for at in range(0, total.shape[0], ROWS):
             vec_grad[at : at + ROWS, :] = total[at : at + ROWS, :].astype(jnp.bfloat16)
-        begin_tick = final_slot
+        begin_tick = final_slot + 1
 
         def finish_tick(tick, carry):
             for step in range(len(tiny_devices)):
-                @pl.when(tick == begin_tick + 1 + step)
+                @pl.when(tick == begin_tick + step)
                 def _():
                     tiny_copy(step).wait_recv()
                     small_work[step + 1] = small_work[step] + small_land[step]
@@ -857,8 +890,7 @@
 ):
     seq_len, width = proj_c.shape
     pairs = width // PAIR
-    cols = width // 2
-    feeds = up_w.shape[1] // cols
+    feeds = up_w.shape[1] // CHUNK
     rows = 2 * seq_len
     small_rows = 24
     more = max(1, dp_size.bit_length() - 1 - FOLDS)
@@ -868,21 +900,25 @@
     once = pl.Buffered(1)
     anywhere = pl.BlockSpec(memory_space=pl.ANY)
     whole = lambda g: (0, 0)
-    turn = lambda g: (jnp.maximum(g - feeds - 1, 0) + pairs // 2) % pairs
-    per_pair = lambda g: (0, turn(g))
-    tile = pl.BlockSpec((seq_len, PAIR), per_pair)
+
+    def turn(g):
+        at = jnp.maximum(g - feeds - 1, 0)
+        return at // 2 + (1 - at % 2) * (pairs // 2)
 
     def chunk(g):
         at = jnp.minimum(g, feeds - 1)
         return (1 - at % 2) * (feeds // 2) + at // 2
 
+    per_pair = lambda g: (0, turn(g))
+    tile = pl.BlockSpec((seq_len, PAIR), per_pair)
     side = lambda g: (0, chunk(g))
     keep = lambda shape: pl.BlockSpec(shape, whole, pipeline_mode=once)
+    pieces = pltpu.VMEM((COUNT, width, CHUNK), low)
     return pl.pallas_call(
         functools.partial(backward_body, dp_size),
         out_shape=(
-            jax.ShapeDtypeStruct((COUNT, width, cols), low),
-            jax.ShapeDtypeStruct((small_rows, cols), jnp.float32),
+            jax.ShapeDtypeStruct((COUNT, width, CHUNK), low),
+            jax.ShapeDtypeStruct((small_rows, CHUNK), jnp.float32),
             jax.ShapeDtypeStruct((2, ROWS, width), low),
             jax.ShapeDtypeStruct((2, ROWS, width), low),
             jax.ShapeDtypeStruct((2, ROWS, width), low),
@@ -897,18 +933,15 @@
                 pl.BlockSpec((lines.shape[0], PAIR), per_pair),
                 pl.BlockSpec((None, 2, 2, seq_len, seq_len), lambda g: (turn(g), 0, 0, 0, 0)),
                 pl.BlockSpec((3, width, PAIR), lambda g: (0, 0, turn(g))),
-                keep((seq_len, width)), keep((seq_len, width)),
-                keep((width, seq_len)), keep((width, seq_len)), keep((width, 2 * seq_len)),
-                keep((width, width)),
-                pl.BlockSpec((rows, cols), side), pl.BlockSpec((rows, cols), side),
-                pl.BlockSpec((width, cols), side), pl.BlockSpec((cols, width), lambda g: (chunk(g), 0)),
-                keep((rows, width)), keep((width, rows)), keep((width, rows)), keep((rows, width)),
-                keep((rows, 1)), keep((8, width)), keep((8, width)),
-                anywhere, anywhere,
-            ],
+                keep((seq_len, width)), keep((seq_len, width)), keep((width, width)),
+                pl.BlockSpec((rows, CHUNK), side), pl.BlockSpec((rows, CHUNK), side),
+                pl.BlockSpec((width, CHUNK), side), pl.BlockSpec((CHUNK, width), lambda g: (chunk(g), 0)),
+                keep((rows, width)), keep((rows, 1)), keep((8, width)), keep((8, width)),
+            ]
+            + [anywhere] * 8,
             out_specs=[
                 anywhere,
-                pl.BlockSpec((small_rows, cols), whole),
+                pl.BlockSpec((small_rows, CHUNK), whole),
                 anywhere, anywhere, anywhere,
             ],
             scratch_shapes=[
@@ -918,18 +951,19 @@
                 pltpu.VMEM((PAIR, 2 * seq_len), jnp.float32),
                 pltpu.VMEM((rows, width), jnp.float32),
                 pltpu.VMEM((rows, width), low),
-                pltpu.VMEM((rows, cols), low),
-                pltpu.VMEM((COUNT, width, cols), low),
-                pltpu.VMEM((COUNT, width, cols), low),
-                pltpu.VMEM((COUNT, width, cols), low),
-                pltpu.VMEM((max(1, more - 1), COUNT if dp_size > 32 else 1, width >> FOLDS, cols), low),
-                pltpu.VMEM((tiny + 1, small_rows, cols), jnp.float32),
-                pltpu.VMEM((small_rows, cols), jnp.float32),
-                pltpu.VMEM((tiny, small_rows, cols), jnp.float32),
+                pltpu.VMEM((rows, CHUNK), low),
+                pltpu.VMEM((width, rows), low),
+                pltpu.VMEM((width, rows), low),
+                pltpu.VMEM((ROWS, ROWS), low),
+                pieces, pieces, pieces,
+                pltpu.VMEM((max(1, more - 1), COUNT if dp_size > 32 else 1, width >> FOLDS, CHUNK), low),
+                pltpu.VMEM((tiny + 1, small_rows, CHUNK), jnp.float32),
+                pltpu.VMEM((small_rows, CHUNK), jnp.float32),
+                pltpu.VMEM((tiny, small_rows, CHUNK), jnp.float32),
                 dma((COUNT,)), dma((COUNT,)), dma((COUNT,)),
                 dma((FOLDS, COUNT)), dma((FOLDS, COUNT)), dma((FOLDS, COUNT)), dma((FOLDS, COUNT)),
                 dma((more, COUNT)), dma((more, COUNT)), dma((tiny,)), dma((tiny,)),
-                dma, dma((2,)), dma((4,)), dma((4,)),
+                dma((7,)), dma((2,)), dma((4,)), dma((4,)),
             ],
         ),
         compiler_params=pltpu.CompilerParams(
@@ -938,44 +972,37 @@
         name="backward",
     )(
         seg_hot, proj_c, proj_q, keys, values, rel_keys, lines, prob, squares,
-        vec_c, vec_q, content_t, query_t, table_t, out_w, act, slope, up_w, down_w, low_rows, low_t, first_t,
-        normal, scale, norms, sums, grad, rows_in,
+        vec_c, vec_q, out_w, act, slope, up_w, down_w, low_rows, scale, norms, sums,
+        content_t, query_t, table_t, low_t, first_t, normal, grad, rows_in,
     )
 
 
 def finish_body(
-    piece_ref, rows_ref, rows_came, keep_ref, grad_came,
-    content_out, query_out, content_grad, query_grad, down_ref, up_ref, out_ref, query_ref, key_ref, value_ref, rel_ref,
+    piece_ref, rows_ref, rows_came, keep_ref, grad_came, tiny_ref,
+    content_out, query_out, content_grad, query_grad, down_ref, up_ref, out_ref, query_ref, key_ref, value_ref,
+    rel_ref, cbias_ref, pbias_ref, sbias_ref, embed_ref, gain1_ref, shift1_ref, ubias_ref, dbias_ref,
+    gain2_ref, shift2_ref,
 ):
     at = pl.program_id(0)
     core = lax.axis_index("mp")
-    cols = piece_ref.shape[1]
-    feeds = 8
-
-    @pl.when((at < feeds) & (at % 2 == 0))
-    def _():
-        down_ref[...] = jnp.transpose(piece_ref[...].astype(jnp.float32))
-
-    @pl.when((at < feeds) & (at % 2 == 1))
+    cols = out_ref.shape[0]
+
+    @pl.when((at < EARLY - 1) & (at % 2 == 0))
+    def _():
+        down_ref[...] = jnp.transpose(piece_ref[...]).astype(jnp.float32)
+
+    @pl.when((at < EARLY - 1) & (at % 2 == 1))
     def _():
         up_ref[...] = piece_ref[...].astype(jnp.float32)
 
-    @pl.when(at == feeds)
-    def _():
-        out_ref[...] = jnp.transpose(piece_ref[...].astype(jnp.float32))
-
-    for turn in range(3):
-        lanes = slice(turn * PAIR, (turn + 1) * PAIR)
-
-        @pl.when(at == EARLY + turn)
-        def _():
-            query_ref[:, lanes] = piece_ref[:, :PAIR].astype(jnp.float32)
-            key_ref[:, lanes] = piece_ref[:, PAIR : 2 * PAIR].astype(jnp.float32)
-            value_ref[:, lanes] = piece_ref[:, 2 * PAIR :].astype(jnp.float32)
-
-    @pl.when(at == EARLY + 3)
-    def _():
-        rel_ref[...] = piece_ref[...].astype(jnp.float32)
+    @pl.when(at == EARLY - 1)
+    def _():
+        out_ref[...] = jnp.transpose(piece_ref[:, :cols]).astype(jnp.float32)
+
+    @pl.when(at >= EARLY)
+    def _():
+        for turn, target in enumerate((query_ref, key_ref, value_ref, rel_ref)):
+            target[...] = piece_ref[:, turn * PAIR : (turn + 1) * PAIR].astype(jnp.float32)
 
     @pl.when(at == 0)
     def _():
@@ -987,20 +1014,31 @@
         content_grad[1 - core] = grad_came[0]
         query_grad[core] = keep_ref[1]
         query_grad[1 - core] = grad_came[1]
-
-
-def finish(pieces, rows_out, rows_came, keep_rows, grad_came, half_ff):
-    count, rows, cols = pieces.shape
-    feeds = 2 * (half_ff // cols)
+        for line, target in enumerate((cbias_ref, pbias_ref, sbias_ref)):
+            target[...] = tiny_ref[line : line + 1, :cols].reshape(cols)
+        embed_ref[...] = tiny_ref[3:5, :cols]
+        for line in range(ubias_ref.shape[0] // CHUNK):
+            ubias_ref[line * CHUNK : (line + 1) * CHUNK] = tiny_ref[5 + line : 6 + line, :].reshape(CHUNK)
+        for line, target in enumerate((gain1_ref, shift1_ref, gain2_ref, shift2_ref, dbias_ref)):
+            for side in range(2):
+                spot = 8 + 2 * line + side
+                target[side * cols : (side + 1) * cols] = tiny_ref[spot : spot + 1, :cols].reshape(cols)
+
+
+def finish(pieces, rows_out, rows_came, keep_rows, grad_came, tiny, half_ff):
+    count, rows, chunk = pieces.shape
+    cols = rows // 2
+    flat = lambda size: jax.ShapeDtypeStruct((size,), jnp.float32)
     square = jax.ShapeDtypeStruct((rows, cols), jnp.float32)
     pair = jax.ShapeDtypeStruct(rows_came.shape, jnp.bfloat16)
     whole = lambda p: (0, 0)
-    block = pl.BlockSpec((rows, cols), whole)
     lead = lambda p: (0, 0, 0)
+    flat_at = lambda size: pl.BlockSpec((size,), lambda p: (0,))
     once = pl.Buffered(1)
     token = pl.BlockSpec(rows_came.shape, lead)
     token_in = pl.BlockSpec(rows_came.shape, lead, pipeline_mode=once)
-    at_chunk = lambda p: jnp.minimum(p // 2, feeds // 2 - 1)
+    at_chunk = lambda p: jnp.minimum(p // 2, half_ff // chunk - 1)
+    thin = pl.BlockSpec((rows, PAIR), lambda p: (0, jnp.maximum(p - EARLY, 0)))
     return pl.pallas_call(
         finish_body,
         out_shape=(
@@ -1009,23 +1047,28 @@
             jax.ShapeDtypeStruct((rows, half_ff), jnp.float32),
             jax.ShapeDtypeStruct((cols, rows), jnp.float32),
             square, square, square, square,
+            flat(cols), flat(cols), flat(cols), jax.ShapeDtypeStruct((2, cols), jnp.float32),
+            flat(rows), flat(rows), flat(half_ff), flat(rows), flat(rows), flat(rows),
         ),
         grid=(count,),
         in_specs=[
-            pl.BlockSpec((None, rows, cols), lambda p: (p, 0, 0)),
+            pl.BlockSpec((None, rows, chunk), lambda p: (p, 0, 0)),
             pl.BlockSpec(rows_out.shape, lead, pipeline_mode=once),
             token_in, token_in, token_in,
+            pl.BlockSpec(tiny.shape, whole, pipeline_mode=once),
         ],
         out_specs=[
             token, token, token, token,
-            pl.BlockSpec((cols, rows), lambda p: (at_chunk(p), 0)),
-            pl.BlockSpec((rows, cols), lambda p: (0, at_chunk(p))),
+            pl.BlockSpec((chunk, rows), lambda p: (at_chunk(p), 0)),
+            pl.BlockSpec((rows, chunk), lambda p: (0, at_chunk(p))),
             pl.BlockSpec((cols, rows), whole),
-            block, block, block, block,
+            thin, thin, thin, thin,
+            flat_at(cols), flat_at(cols), flat_at(cols), pl.BlockSpec((2, cols), whole),
+            flat_at(rows), flat_at(rows), flat_at(half_ff), flat_at(rows), flat_at(rows), flat_at(rows),
         ],
-        compiler_params=pltpu.CompilerParams(vmem_limit_bytes=48 << 20),
+        compiler_params=pltpu.CompilerParams(vmem_limit_bytes=60 << 20),
         name="finish",
-    )(pieces, rows_out, rows_came, keep_rows, grad_came)
+    )(pieces, rows_out, rows_came, keep_rows, grad_came, tiny)
 
 
 def position_table(seq_len, width):
@@ -1068,36 +1111,19 @@
 ):
     half, width = content_in.shape[1:]
     seq_len = order_ranks.shape[1]
-    cols = query_weight.shape[1]
     ff = up_weight.shape[1]
-    wide_f = lambda value: value.astype(jnp.float32)
-    meta = jnp.concatenate(
-        [order_ranks, segment_ids, target_flags, jnp.broadcast_to(doc_lengths[:, None], order_ranks.shape)], axis=0
-    ).astype(jnp.float32)
-    up_rows = ff // cols
-    vectors = jnp.concatenate(
-        [
-            content_bias[None], position_bias[None], segment_bias[None], segment_embed,
-            up_bias.reshape(up_rows, cols), jnp.zeros(((-5 - up_rows) % 8, cols), jnp.bfloat16),
-        ],
-        axis=0,
-    ).astype(jnp.float32)
     table = position_table(seq_len, width)
     (
-        vec_c, vec_q, prob, proj_c, proj_q, keys, values, rel_keys, seg_hot, content_t, query_t, lines,
+        vec_c, vec_q, prob, proj_c, proj_q, keys, values, rel_keys, seg_hot, content_t, query_t, lines, up_bias_use,
         content, query, cots, squares, out_use, up_use, down_use,
     ) = forward(
         content_in, query_in, content_cot, query_cot, query_weight, key_weight, value_weight, rel_weight,
-        out_weight, up_weight, down_weight, meta, vectors, jnp.asarray(table),
+        out_weight, up_weight, down_weight, doc_lengths, order_ranks, segment_ids, target_flags,
+        content_bias, position_bias, segment_bias, segment_embed, up_bias, jnp.asarray(table),
     )
-    up_bias_use = jnp.concatenate(
-        [lines[5 : 5 + up_rows, :cols].reshape(1, ff), lines[5 : 5 + up_rows, cols:].reshape(1, ff)], axis=1
-    )
-    norms = jnp.stack(
-        [first_gain, first_shift, second_gain, second_shift, down_bias, down_bias, down_bias, down_bias]
-    ).astype(jnp.float32)
-    first_t, normal, scale, act, slope, grad, low_rows, low_t, rows_out, sums = feed_forward(
-        vec_c, vec_q, content, query, cots, out_use, up_use, down_use, up_bias_use, norms
+    first_t, normal, scale, act, slope, grad, low_rows, low_t, rows_out, sums, norms = feed_forward(
+        vec_c, vec_q, content, query, cots, out_use, up_use, down_use, up_bias_use,
+        (first_gain, first_shift, second_gain, second_shift, down_bias),
     )
     pieces, tiny, keep_rows, rows_came, grad_came = backward(
         dp_size, seg_hot, proj_c, proj_q, keys, values, rel_keys, lines, prob, squares,
@@ -1105,34 +1131,14 @@
         low_rows, low_t, first_t, normal, scale, norms, sums, grad, rows_out,
     )
     (
+        content_out, query_out, content_grad, query_grad, down_sum, up_sum, out_sum,
+        query_sum, key_sum, value_sum, rel_sum, cbias_sum, pbias_sum, sbias_sum, embed_sum,
+        gain1_sum, shift1_sum, ubias_sum, dbias_sum, gain2_sum, shift2_sum,
+    ) = finish(pieces, rows_out.reshape(4, half, width), rows_came, keep_rows, grad_came, tiny, ff)
+    return (
         content_out, query_out, content_grad, query_grad,
-        down_sum, up_sum, out_sum, query_sum, key_sum, value_sum, rel_sum,
-    ) = finish(pieces, rows_out.reshape(4, half, width), rows_came, keep_rows, grad_came, ff)
-    split_rows = 5 + ff // cols
-    same_part = tiny[split_rows : split_rows + 10].reshape(5, width)
-    split_part = tiny[:5]
-    return (
-        content_out,
-        query_out,
-        content_grad,
-        query_grad,
-        query_sum,
-        key_sum,
-        value_sum,
-        out_sum,
-        rel_sum,
-        split_part[0],
-        split_part[1],
-        split_part[2],
-        split_part[3:5],
-        same_part[0],
-        same_part[1],
-        up_sum,
-        tiny[5:split_rows].reshape(ff),
-        down_sum,
-        same_part[4],
-        same_part[2],
-        same_part[3],
+        query_sum, key_sum, value_sum, out_sum, rel_sum, cbias_sum, pbias_sum, sbias_sum, embed_sum,
+        gain1_sum, shift1_sum, up_sum, ubias_sum, down_sum, dbias_sum, gain2_sum, shift2_sum,
     )
 
 

time: 314 us -> 264 us (0.84)
  Pallas kernels: 289 us -> 263 us
  local copies, waits for them, and re-layouts: 20.6 us -> 0 us
  other arithmetic: 3.23 us -> 0 us
    pallas_call x1, Pallas kernels: 195 us -> 172 us  [backward(): pl.pallas_call(functools.partial(backward_body, dp_size), out_shape=(jax....]
    unnamed x11 -> x0, local copies, waits for them, and re-layouts: 5.58 us -> none
    slice x3 -> x0, local copies, waits for them, and re-layouts: 3.6 us -> none  [the longest x1 1.44 us: on_device(): same_part[3]]
    another operation x6 -> x0, local copies, waits for them, and re-layouts: 3.47 us -> none  [on_device(): jnp.stack([first_gain, first_shift, second_gain, second_shift, down_bias,...]
where the time goes in v6:
time: 264 us; the launch traced here: 263 us
  Pallas kernels  263 us (100%)
    pallas_call x1, Pallas kernels, backward(): pl.pallas_call(functools.partial(backward_body, dp_size), out_shape=(jax....  172 us
    pallas_call x1, Pallas kernels, forward(): pl.pallas_call(forward_body, out_shape=(low_tokens, low_tokens, jax.Shape...  47.4 us
    pallas_call x1, Pallas kernels, feed_forward(): pl.pallas_call(feed_forward_body, out_shape=(jax.ShapeDtypeStruct((width,...  29.4 us
    pallas_call x1, Pallas kernels, finish(): pl.pallas_call(finish_body, out_shape=(pair, pair, pair, pair, jax.ShapeD...  14 us

profile of v6, /device:TPU:0, one launch (start us, length us, event | category | flops | bytes accessed | tf_op | source)
XLA Modules:
  0.0 263.5 jit_solution(2070780252514740298)
XLA Ops:
  0.7 47.4 %attend_forward.1 = (bf16[512,768]{1,0:T(8,128)(2,1)}, bf16[512,768]{1,0:T(8,128)(2,1)}, bf16[6,2,2,512,512]{4,3,2,1,0:T(8,128)(2,1)}, f32[512,768]{1,0:T(8,128)...) custom-call(bf16[2,256,768]{2,1,0:T(8,128)(2,1)} %content_in.1, ...), custom_call_target="tpu_custom_call" | custom-call | tf_op jit(solution)/shard_map/attend_forward/pallas_call | solution.py:247
  48.1 29.4 %feed_forward.1 = (bf16[768,1024]{1,0:T(8,128)(2,1)}, bf16[1024,768]{1,0:T(8,128)(2,1)}, f32[1024,1]{1,0:T(8,128)}, bf16[1024,3072]{1,0:T(8,128)(2,1)}, bf16[102...) custom-call(bf16[512,768]{1,0:T(8,128)(2,1)} %get-tuple-element.87.v, ...), custom_call_target="tpu_custom_call" | custom-call | tf_op jit(solution)/shard_map/feed_forward/pallas_call | solution.py:403
  77.5 171.8 %backward.1 = (bf16[10,768,512]{2,1,0:T(8,128)(2,1)}, f32[24,512]{1,0:T(8,128)}, bf16[2,256,768]{2,1,0:T(8,128)(2,1)}, bf16[2,256,768]{2,1,0:T(8,128)(2,1)}, bf16[2,256,768]{2,1,0:T(8,128)(2,1)}) custom-call(bf16[512,128]{1,0:T(8,128)(2,1)} %get-tuple-element.78.refs_0_, f32[512,768]{1,0:T(8,128)} %get-tuple-element.79.refs_1_, ...), custom_call_target="tpu_custom_call" | custom-call | tf_op jit(solution)/shard_map/backward/pallas_call | solution.py:917
  249.3 14.0 %finish.1 = (bf16[2,256,768]{2,1,0:T(8,128)(2,1)}, bf16[2,256,768]{2,1,0:T(8,128)(2,1)}, bf16[2,256,768]{2,1,0:T(8,128)(2,1)}, bf16[2,256,768]{2,1,0:T(8,128)(2,...) custom-call(bf16[10,768,512]{2,1,0:T(8,128)(2,1)} %get-tuple-element, ...), custom_call_target="tpu_custom_call" | custom-call | tf_op jit(solution)/shard_map/finish/pallas_call | solution.py:1042

commit v7 on v6

--- a/solution.py
+++ b/solution.py
@@ -36,7 +36,7 @@
     length_ref, order_ref, segment_ref, target_ref, cbias_ref, pbias_ref, sbias_ref, embed_ref, ubias_ref, table_ref,
     vec_c, vec_q, prob_ref, proj_c, proj_q, key_ref, value_ref, rel_ref, hot_ref, content_t, query_t, vectors_out, ubias_out,
     content_out, query_out, cots_out, square_out, out_all, up_all, down_all,
-    tokens, squares, near_pack, far_pack, bounce_up, bounce_down, bounce_out, bounce_cot, mask_scr, ext_scr, rank_scr,
+    tokens, squares, near_pack, far_pack, bounce_up, bounce_down, bounce_out, bounce_cot, mask_scr, ext_scr, rank_scr, proj_next, low_next, rel_next,
     token_sem, token_send, token_recv, square_sem, square_send, square_recv,
     bulk_load, bulk_store, bulk_send, bulk_recv, vector_send, vector_recv,
 ):
@@ -157,7 +157,7 @@
         content_t[...] = jnp.transpose(tokens[0])
         query_t[...] = jnp.transpose(tokens[1])
 
-    @pl.when(step == pl.num_programs(0) // 2)
+    @pl.when(step == pl.num_programs(0) // 2 - 1)
     def _():
         for copy in square_swap + [vector_swap]:
             copy.wait_recv()
@@ -168,52 +168,83 @@
 
     pair_lanes = pl.ds(pl.multiple_of(step * PAIR, PAIR), PAIR)
     lines = vectors_out[:, pair_lanes]
-    triple_w = jnp.concatenate([squares[at, :, pair_lanes] for at in range(3)], axis=1)
-    for block in range(blocks):
-        rows = slice(block * ROWS, (block + 1) * ROWS)
-        triple = nn(tokens[0, rows, :], triple_w)
-        proj_c[rows, :] = triple[:, :PAIR]
-        key_ref[rows, :] = triple[:, PAIR : 2 * PAIR].astype(jnp.bfloat16)
-        value_ref[rows, :] = triple[:, 2 * PAIR :].astype(jnp.bfloat16)
-        proj_q[rows, :] = nn(tokens[1, rows, :], squares[0, :, pair_lanes])
-    for block in range(2 * blocks):
-        rows = slice(block * ROWS, (block + 1) * ROWS)
-        rel_ref[rows, :] = nn(table_ref[rows, :], squares[3, :, pair_lanes]).astype(jnp.bfloat16)
+    double = pl.ds(pl.multiple_of((step // 2) * 2 * PAIR, 2 * PAIR), 2 * PAIR)
+
+    @pl.when(step % 2 == 0)
+    def _():
+        six_w = jnp.concatenate([squares[at, :, double] for at in range(3)], axis=1)
+        for block in range(blocks):
+            rows = slice(block * ROWS, (block + 1) * ROWS)
+            six = nn(tokens[0, rows, :], six_w)
+            proj_c[rows, :] = six[:, :PAIR]
+            proj_next[0, rows, :] = six[:, PAIR : 2 * PAIR]
+            key_ref[rows, :] = six[:, 2 * PAIR : 3 * PAIR].astype(jnp.bfloat16)
+            low_next[0, rows, :] = six[:, 3 * PAIR : 4 * PAIR].astype(jnp.bfloat16)
+            value_ref[rows, :] = six[:, 4 * PAIR : 5 * PAIR].astype(jnp.bfloat16)
+            low_next[1, rows, :] = six[:, 5 * PAIR :].astype(jnp.bfloat16)
+            two = nn(tokens[1, rows, :], squares[0, :, double])
+            proj_q[rows, :] = two[:, :PAIR]
+            proj_next[1, rows, :] = two[:, PAIR:]
+        for block in range(2 * blocks):
+            rows = slice(block * ROWS, (block + 1) * ROWS)
+            two = nn(table_ref[rows, :], squares[3, :, double]).astype(jnp.bfloat16)
+            rel_ref[rows, :] = two[:, :PAIR]
+            rel_next[rows, :] = two[:, PAIR:]
+
+    @pl.when(step % 2 == 1)
+    def _():
+        proj_c[...] = proj_next[0]
+        proj_q[...] = proj_next[1]
+        key_ref[...] = low_next[0]
+        value_ref[...] = low_next[1]
+        rel_ref[...] = rel_next[...]
+
     ext_scr[:, :PAIR] = key_ref[...]
     ext_scr[:, PAIR:] = hot_ref[...]
     lane = lane_ids(ROWS)
     diff = lines[3:4, :] - lines[4:5, :]
-    for stream in range(2):
-        proj_ref = (proj_c, proj_q)[stream]
-        vec_ref = (vec_c, vec_q)[stream]
-        for block in range(blocks):
+    zero = jnp.zeros((), jnp.bfloat16)
+
+    def rough(stream, block, head):
+        rows = pl.ds(block * ROWS, ROWS)
+        own = (lane >= DH) if head else (lane < DH)
+        proj = (proj_c, proj_q)[stream][rows, :]
+        query_c = ((proj + lines[0:1, :]) * 0.125).astype(jnp.bfloat16)
+        query_p = ((proj + lines[1:2, :]) * 0.125).astype(jnp.bfloat16)
+        seg_gap = (proj + lines[2:3, :]) * (diff * 0.125)
+        gap = jnp.sum(jnp.where(own, seg_gap, 0.0), axis=1, keepdims=True)
+        gap_high = gap.astype(jnp.bfloat16).astype(jnp.float32)
+        seg_part = jnp.where(lane < 4, gap_high, gap - gap_high) * hot_ref[rows, :].astype(jnp.float32)
+        left = jnp.concatenate([jnp.where(own, query_c, zero), seg_part.astype(jnp.bfloat16)], axis=1)
+        window = rel_ref[pl.ds(seq_len - (block + 1) * ROWS, wide), :]
+        scores = nt(left, ext_scr[...])
+        table = nt(jnp.where(own, query_p, zero), window)
+        return scores, table
+
+    def settle(stream, block, head, scores, table):
+        rows = pl.ds(block * ROWS, ROWS)
+        table = pltpu.roll(table, 1, 1, stride=1, stride_axis=0)
+        scores = scores + table[:, ROWS:] + mask_scr[stream, rows, :]
+        top = jnp.max(scores, axis=1, keepdims=True)
+        terms = jnp.exp(scores - top)
+        total = jnp.sum(terms, axis=1, keepdims=True)
+        prob = (terms * (1.0 / total)).astype(jnp.bfloat16)
+        prob_ref[stream, head, rows, :] = prob
+        return nn(prob, value_ref[...])
+
+    turns = [(stream, block, head) for stream in range(2) for block in range(blocks) for head in range(2)]
+    ahead = rough(*turns[0])
+    part_first = None
+    for at, (stream, block, head) in enumerate(turns):
+        now = ahead
+        if at + 1 < len(turns):
+            ahead = rough(*turns[at + 1])
+        part = settle(stream, block, head, *now)
+        if head == 0:
+            part_first = part
+        else:
             rows = pl.ds(block * ROWS, ROWS)
-            proj = proj_ref[rows, :]
-            query_c = ((proj + lines[0:1, :]) * 0.125).astype(jnp.bfloat16)
-            query_p = ((proj + lines[1:2, :]) * 0.125).astype(jnp.bfloat16)
-            seg_gap = (proj + lines[2:3, :]) * (diff * 0.125)
-            hot = hot_ref[rows, :].astype(jnp.float32)
-            window = rel_ref[pl.ds(seq_len - (block + 1) * ROWS, wide), :]
-            vec_pair = None
-            for head in range(2):
-                own = (lane >= DH) if head else (lane < DH)
-                zero = jnp.zeros((), jnp.bfloat16)
-                gap = jnp.sum(jnp.where(own, seg_gap, 0.0), axis=1, keepdims=True)
-                gap_high = gap.astype(jnp.bfloat16).astype(jnp.float32)
-                seg_part = (jnp.where(lane < 4, gap_high, gap - gap_high) * hot).astype(jnp.bfloat16)
-                left = jnp.concatenate([jnp.where(own, query_c, zero), seg_part], axis=1)
-                scores = nt(left, ext_scr[...])
-                table = nt(jnp.where(own, query_p, zero), window)
-                table = pltpu.roll(table, 1, 1, stride=1, stride_axis=0)
-                scores = scores + table[:, ROWS:] + mask_scr[stream, rows, :]
-                top = jnp.max(scores, axis=1, keepdims=True)
-                terms = jnp.exp(scores - top)
-                total = jnp.sum(terms, axis=1, keepdims=True)
-                prob = (terms * (1.0 / total)).astype(jnp.bfloat16)
-                prob_ref[stream, head, rows, :] = prob
-                part = nn(prob, value_ref[...])
-                vec_pair = part if head == 0 else jnp.where(own, part, vec_pair)
-            vec_ref[rows, :] = vec_pair.astype(jnp.bfloat16)
+            (vec_c, vec_q)[stream][rows, :] = jnp.where(lane < DH, part_first, part).astype(jnp.bfloat16)
 
     @pl.when(step == pl.num_programs(0) - 1)
     def _():
@@ -298,6 +329,9 @@
                 pltpu.VMEM((2, seq_len, seq_len), jnp.float32),
                 pltpu.VMEM((seq_len, 2 * PAIR), low),
                 pltpu.VMEM((seq_len, PAIR), jnp.float32),
+                pltpu.VMEM((2, seq_len, PAIR), jnp.float32),
+                pltpu.VMEM((2, seq_len, PAIR), low),
+                pltpu.VMEM((2 * seq_len, PAIR), low),
                 dma((2,)), dma((2,)), dma((2,)), dma((4,)), dma((4,)), dma((4,)),
                 dma((5,)), dma((10,)), dma((5,)), dma((5,)), dma, dma,
             ],
@@ -331,17 +365,40 @@
 
 
 def feed_forward_body(
-    vec_c, vec_q, content, query, cots, out_ref, up_ref, down_ref, up_bias,
-    gain1_ref, shift1_ref, gain2_ref, shift2_ref, dbias_ref,
-    first_t, normal_ref, scale_ref, act_ref, slope_ref, grad_ref, low_ref, low_t, rows_ref, sums_ref, norms,
-    first_scr, total_scr,
+    vec_c, vec_q, content, query, out_ref, up_ref, down_ref, up_bias,
+    gain1_ref, shift1_ref, gain2_ref, shift2_ref, dbias_ref, cots_in,
+    act_ref, slope_ref, scale_ref, sums_ref, norms,
+    first_t_out, normal_out, grad_out, low_out, low_t_out, rows_out,
+    first_scr, total_scr, cots, first_t, normal_ref, grad_ref, low_ref, low_t, rows_ref, cot_sem, out_sem,
 ):
     step = pl.program_id(0)
     half_rows = vec_c.shape[0]
+    last = pl.num_programs(0) - 1
+    cot_copy = pltpu.make_async_copy(cots_in, cots, cot_sem)
+
+    def lines_copy(at, source, target, start):
+        here = pl.ds(start, ROWS)
+        return pltpu.make_async_copy(source.at[here], target.at[here], out_sem.at[at, start // ROWS])
+
+    first_copies = [pltpu.make_async_copy(first_t, first_t_out, out_sem.at[0, 0])] + [
+        lines_copy(1, normal_ref, normal_out, start) for start in range(0, 2 * half_rows, ROWS)
+    ]
+    late_copies = [
+        [
+            lines_copy(2, grad_ref, grad_out, start),
+            lines_copy(3, low_ref, low_out, start),
+            lines_copy(4, rows_ref, rows_out, start),
+            pltpu.make_async_copy(
+                low_t.at[:, pl.ds(start, ROWS)], low_t_out.at[:, pl.ds(start, ROWS)], out_sem.at[5, start // ROWS]
+            ),
+        ]
+        for start in range(0, 2 * half_rows, ROWS)
+    ]
     chunks = [(s, at) for s in range(2) for at in range(0, half_rows, ROWS)]
 
     @pl.when(step == 0)
     def _():
+        cot_copy.start()
         norms[...] = jnp.zeros_like(norms)
         for at, part in enumerate((gain1_ref, shift1_ref, gain2_ref, shift2_ref, dbias_ref)):
             norms[at : at + 1, :] = part[...].astype(jnp.float32).reshape(1, part.shape[0])
@@ -357,6 +414,8 @@
             normal_ref[there, :] = normal.astype(jnp.bfloat16)
             scale_ref[there, :] = scale
             total_scr[there, :] = first.astype(jnp.float32) + norms[4:5, :]
+        for copy in first_copies:
+            copy.start()
 
     for stream, at in chunks:
         there = slice(stream * half_rows + at, stream * half_rows + at + ROWS)
@@ -370,8 +429,9 @@
         slope_ref[there, :] = slope.astype(jnp.bfloat16)
         total_scr[there, :] += nn(act, down_ref[...])
 
-    @pl.when(step == pl.num_programs(0) - 1)
-    def _():
+    @pl.when(step == last)
+    def _():
+        cot_copy.wait()
         sums = [jnp.zeros((1, content.shape[1]), jnp.float32) for _ in range(3)]
         for stream, at in chunks:
             here = pl.ds(at, ROWS)
@@ -386,7 +446,11 @@
             low_t[:, there] = jnp.transpose(low)
             for at_sum, term in enumerate((cot * normal, cot, grad)):
                 sums[at_sum] = sums[at_sum] + jnp.sum(term, axis=0, keepdims=True)
+            for copy in late_copies[(stream * half_rows + at) // ROWS]:
+                copy.start()
         sums_ref[...] = jnp.concatenate(sums + [jnp.zeros((5, content.shape[1]), jnp.float32)], axis=0)
+        for copy in first_copies + sum(late_copies, []):
+            copy.wait()
 
 
 def feed_forward(vec_c, vec_q, content, query, cots, out_use, up_use, down_use, up_bias, vectors):
@@ -400,52 +464,57 @@
     side = lambda f: (0, f)
     keep = lambda shape: pl.BlockSpec(shape, whole, pipeline_mode=once)
     stream = keep((seq_len, width))
+    flat = pl.BlockSpec((width,), lambda f: (0,))
+    anywhere = pl.BlockSpec(memory_space=pl.ANY)
     return pl.pallas_call(
         feed_forward_body,
         out_shape=(
+            jax.ShapeDtypeStruct((rows, hidden), low),
+            jax.ShapeDtypeStruct((rows, hidden), low),
+            jax.ShapeDtypeStruct((rows, 1), jnp.float32),
+            jax.ShapeDtypeStruct((8, width), jnp.float32),
+            jax.ShapeDtypeStruct((8, width), jnp.float32),
             jax.ShapeDtypeStruct((width, rows), low),
             jax.ShapeDtypeStruct((rows, width), low),
-            jax.ShapeDtypeStruct((rows, 1), jnp.float32),
-            jax.ShapeDtypeStruct((rows, hidden), low),
-            jax.ShapeDtypeStruct((rows, hidden), low),
             jax.ShapeDtypeStruct((rows, width), jnp.float32),
             jax.ShapeDtypeStruct((rows, width), low),
             jax.ShapeDtypeStruct((width, rows), low),
             jax.ShapeDtypeStruct((rows, width), low),
-            jax.ShapeDtypeStruct((8, width), jnp.float32),
-            jax.ShapeDtypeStruct((8, width), jnp.float32),
         ),
         grid=(hidden // cols,),
         in_specs=[
             stream, stream, stream, stream,
-            pl.BlockSpec(cots.shape, lambda f: (0, 0, 0), pipeline_mode=once),
             keep((width, width)),
             pl.BlockSpec((width, cols), side),
             pl.BlockSpec((cols, width), lambda f: (f, 0)),
             pl.BlockSpec((1, cols), side),
-            pl.BlockSpec((width,), lambda f: (0,)), pl.BlockSpec((width,), lambda f: (0,)), pl.BlockSpec((width,), lambda f: (0,)),
-            pl.BlockSpec((width,), lambda f: (0,)), pl.BlockSpec((width,), lambda f: (0,)),
+            flat, flat, flat, flat, flat,
+            anywhere,
         ],
         out_specs=[
-            pl.BlockSpec((width, rows), whole),
-            pl.BlockSpec((rows, width), whole),
-            pl.BlockSpec((rows, 1), whole),
             pl.BlockSpec((rows, cols), side),
             pl.BlockSpec((rows, cols), side),
-            pl.BlockSpec((rows, width), whole),
-            pl.BlockSpec((rows, width), whole),
-            pl.BlockSpec((width, rows), whole),
-            pl.BlockSpec((rows, width), whole),
+            pl.BlockSpec((rows, 1), whole),
             pl.BlockSpec((8, width), whole),
             pl.BlockSpec((8, width), whole),
-        ],
+        ]
+        + [anywhere] * 6,
         scratch_shapes=[
             pltpu.VMEM((rows, width), low),
             pltpu.VMEM((rows, width), jnp.float32),
+            pltpu.VMEM(cots.shape, low),
+            pltpu.VMEM((width, rows), low),
+            pltpu.VMEM((rows, width), low),
+            pltpu.VMEM((rows, width), jnp.float32),
+            pltpu.VMEM((rows, width), low),
+            pltpu.VMEM((width, rows), low),
+            pltpu.VMEM((rows, width), low),
+            pltpu.SemaphoreType.DMA,
+            pltpu.SemaphoreType.DMA((6, rows // ROWS)),
         ],
         compiler_params=pltpu.CompilerParams(vmem_limit_bytes=60 << 20),
         name="feed_forward",
-    )(vec_c, vec_q, content, query, cots, out_use, up_use, down_use, up_bias, *vectors)
+    )(vec_c, vec_q, content, query, out_use, up_use, down_use, up_bias, *vectors, cots)
 
 
 FOLDS = 4
@@ -457,10 +526,10 @@
 def backward_body(dp_size, *refs):
     (
         seg_hot, proj_c, proj_q, key_ref, value_ref, rel_ref, bias_ref, prob_ref,
-        square_w, vec_c, vec_q, out_w, act_ref, slope_ref, up_ref, down_ref, low_ref, scale_ref, norms, sums_in,
-        content_t, query_t, table_t, low_t, first_t, normal_in, grad_in, rows_in,
+        square_w, act_ref, slope_ref, up_ref, down_ref, low_ref, scale_ref, norms, sums_in,
+        content_t, query_t, table_t, low_t, first_t, normal_in, grad_in, rows_in, vec_c_in, vec_q_in, out_in,
         sum_out, small_out, keep_out, rows_came, grad_came,
-        vt_scr, key_acc, value_acc, rel_acc, total, vec_grad, hid_scr, turn_a, turn_b, flip_scr,
+        vt_scr, key_acc, value_acc, rel_acc, total, vec_grad, hid_scr, turn_a, turn_b, flip_scr, vec_c, vec_q, out_w,
         work, swapped, landed, extra, small_work, small_far, small_land,
         store_sem, swap_send, swap_recv, fold_send, fold_recv, spread_send, spread_recv,
         more_send, more_recv, tiny_send, tiny_recv, side_sem, keep_sem, back_send, back_recv,
@@ -489,7 +558,7 @@
         begin = begin + bit * length
         starts.append(begin)
     land_at = [rows - 2 * length for length in lengths]
-    offsets = [0, 3, 5, 7, 9, 11, 13, 15, 18]
+    offsets = [0, 3, 6, 8, 10, 12, 14, 16, 19]
     final_slot = 25
 
     def kept(fold):
@@ -581,6 +650,9 @@
                 (table_t, turn_a),
                 (content_t, turn_b.at[:, :seq_len]),
                 (query_t, turn_b.at[:, seq_len:]),
+                (vec_c_in, vec_c),
+                (vec_q_in, vec_q),
+                (out_in, out_w),
             )
         )
     ]
@@ -615,9 +687,9 @@
     def advance(tick):
         for number in reversed(range(2 * FOLDS + 1)):
             slot = tick - offsets[number]
-            early = (slot == 3) | (slot == 4) | (slot == 7) | (slot == 8) | (slot == 11) | (slot == 12)
+            early = (slot == 2) | (slot == 3) | (slot == 6) | (slot == 7) | (slot == 10) | (slot == 11)
             late = (slot == 13) | (slot == 17) | (slot == 21) | (slot == final_slot)
-            piece = jnp.where(slot < 13, 2 * ((slot - 3) // 4) + (slot - 3) % 4, EARLY - 1 + (slot - 13) // 4)
+            piece = jnp.where(slot < 13, 2 * ((slot - 2) // 4) + (slot - 2) % 4, EARLY - 1 + (slot - 13) // 4)
 
             @pl.when(early | late)
             def _():
@@ -633,8 +705,8 @@
         for device in tiny_devices:
             pl.semaphore_signal(barrier, inc=1, device_id=device, device_id_type=MESH)
         pl.semaphore_wait(barrier, len(tiny_devices))
-        for copy in side_loads[:4]:
-            copy.start()
+        for at in (2, 0, 1, 3, 7, 8, 9):
+            side_loads[at].start()
         rows_copy(0).start()
         rows_copy(1).start()
         small_work[0] = jnp.zeros_like(small_work[0])
@@ -648,14 +720,39 @@
         line_at = lax.broadcasted_iota(jnp.int32, (ROWS, ROWS), 0)
         lane_at = lax.broadcasted_iota(jnp.int32, (ROWS, ROWS), 1)
         flip_scr[...] = jnp.where(line_at + lane_at == ROWS - 1, 1.0, 0.0).astype(jnp.bfloat16)
-        for copy in side_loads[:3]:
-            copy.wait()
 
     @pl.when(grid_at < feeds)
     def _():
         chunk = grid_at // 2
         near = grid_at % 2 == 1
         bias_sum = jnp.zeros((1, width), jnp.float32)
+
+        @pl.when(near)
+        def _():
+            swap_copy(2 * chunk).wait_send()
+
+        @pl.when(grid_at == 0)
+        def _():
+            side_loads[2].wait()
+
+        for at in range(0, rows, ROWS):
+            here = slice(at, at + ROWS)
+            work[2 * chunk, here, :] = nn(turn_b[here, :], act_ref[...]).astype(jnp.bfloat16)
+
+        @pl.when(near)
+        def _():
+            settle(2 * chunk)
+
+        @pl.when(jnp.logical_not(near))
+        def _():
+            swap_copy(2 * chunk).start()
+
+        @pl.when(grid_at == 0)
+        def _():
+            side_loads[0].wait()
+            side_loads[1].wait()
+
+        advance(2 * grid_at)
         for at in range(0, total.shape[0], ROWS):
             here = slice(at, at + ROWS)
             grad_act = nt(low_ref[here, :], down_ref[...])
@@ -664,36 +761,31 @@
             bias_sum = bias_sum + jnp.sum(hid.astype(jnp.float32), axis=0, keepdims=True)
             total[here, :] += nt(hid, up_ref[...])
 
-        advance(2 * grid_at)
-
         @pl.when(near)
         def _():
-            swap_copy(2 * chunk).wait_send()
             swap_copy(2 * chunk + 1).wait_send()
 
         for at in range(0, rows, ROWS):
             here = slice(at, at + ROWS)
-            work[2 * chunk, here, :] = nn(turn_b[here, :], act_ref[...]).astype(jnp.bfloat16)
             work[2 * chunk + 1, here, :] = nn(turn_a[here, :], hid_scr[...]).astype(jnp.bfloat16)
 
         @pl.when(near)
         def _():
             small_work[0, pl.ds(5 + chunk, 1), :] = bias_sum
-            settle(2 * chunk)
             settle(2 * chunk + 1)
 
         @pl.when(jnp.logical_not(near))
         def _():
             small_far[pl.ds(5 + chunk, 1), :] = bias_sum
-            swap_copy(2 * chunk).start()
             swap_copy(2 * chunk + 1).start()
 
     @pl.when(grid_at == feeds)
     def _():
         advance(2 * grid_at)
-        for copy in side_loads[4:]:
+        for copy in side_loads[4:7]:
             copy.start()
-        side_loads[3].wait()
+        for at in (3, 7, 8, 9):
+            side_loads[at].wait()
         sums = [jnp.zeros((1, rows), jnp.float32) for _ in range(2)]
         out_piece = EARLY - 1
         near_sum = jnp.zeros((rows, cols), jnp.float32)
@@ -737,7 +829,7 @@
 
         @pl.when(turn == 0)
         def _():
-            for copy in side_loads[4:]:
+            for copy in side_loads[4:7]:
                 copy.wait()
 
         pair_lanes = pl.ds(pl.multiple_of(pair * PAIR, PAIR), PAIR)
@@ -832,11 +924,13 @@
             small_work[0, 0:5, lanes] = vectors
             settle(piece)
 
+    advance(2 * grid_at + 1)
+
+    @pl.when(grid_at > feeds)
+    def _():
         weights = jnp.concatenate([square_w[0], square_w[1], square_w[2]], axis=1)
         total[:seq_len, :] += nt(gproj_c[...], weights)
         total[seq_len:, :] += nt(gproj_q[...], square_w[0])
-
-    advance(2 * grid_at + 1)
 
     @pl.when(grid_at == last)
     def _():
@@ -933,12 +1027,11 @@
                 pl.BlockSpec((lines.shape[0], PAIR), per_pair),
                 pl.BlockSpec((None, 2, 2, seq_len, seq_len), lambda g: (turn(g), 0, 0, 0, 0)),
                 pl.BlockSpec((3, width, PAIR), lambda g: (0, 0, turn(g))),
-                keep((seq_len, width)), keep((seq_len, width)), keep((width, width)),
                 pl.BlockSpec((rows, CHUNK), side), pl.BlockSpec((rows, CHUNK), side),
                 pl.BlockSpec((width, CHUNK), side), pl.BlockSpec((CHUNK, width), lambda g: (chunk(g), 0)),
                 keep((rows, width)), keep((rows, 1)), keep((8, width)), keep((8, width)),
             ]
-            + [anywhere] * 8,
+            + [anywhere] * 11,
             out_specs=[
                 anywhere,
                 pl.BlockSpec((small_rows, CHUNK), whole),
@@ -955,6 +1048,9 @@
                 pltpu.VMEM((width, rows), low),
                 pltpu.VMEM((width, rows), low),
                 pltpu.VMEM((ROWS, ROWS), low),
+                pltpu.VMEM((seq_len, width), low),
+                pltpu.VMEM((seq_len, width), low),
+                pltpu.VMEM((width, width), low),
                 pieces, pieces, pieces,
                 pltpu.VMEM((max(1, more - 1), COUNT if dp_size > 32 else 1, width >> FOLDS, CHUNK), low),
                 pltpu.VMEM((tiny + 1, small_rows, CHUNK), jnp.float32),
@@ -963,7 +1059,7 @@
                 dma((COUNT,)), dma((COUNT,)), dma((COUNT,)),
                 dma((FOLDS, COUNT)), dma((FOLDS, COUNT)), dma((FOLDS, COUNT)), dma((FOLDS, COUNT)),
                 dma((more, COUNT)), dma((more, COUNT)), dma((tiny,)), dma((tiny,)),
-                dma((7,)), dma((2,)), dma((4,)), dma((4,)),
+                dma((10,)), dma((2,)), dma((4,)), dma((4,)),
             ],
         ),
         compiler_params=pltpu.CompilerParams(
@@ -972,48 +1068,86 @@
         name="backward",
     )(
         seg_hot, proj_c, proj_q, keys, values, rel_keys, lines, prob, squares,
-        vec_c, vec_q, out_w, act, slope, up_w, down_w, low_rows, scale, norms, sums,
-        content_t, query_t, table_t, low_t, first_t, normal, grad, rows_in,
+        act, slope, up_w, down_w, low_rows, scale, norms, sums,
+        content_t, query_t, table_t, low_t, first_t, normal, grad, rows_in, vec_c, vec_q, out_w,
     )
 
 
 def finish_body(
-    piece_ref, rows_ref, rows_came, keep_ref, grad_came, tiny_ref,
-    content_out, query_out, content_grad, query_grad, down_ref, up_ref, out_ref, query_ref, key_ref, value_ref,
-    rel_ref, cbias_ref, pbias_ref, sbias_ref, embed_ref, gain1_ref, shift1_ref, ubias_ref, dbias_ref,
-    gain2_ref, shift2_ref,
+    piece_ref, tiny_ref, rows_in, came_in, keep_in, grad_in,
+    down_ref, up_ref, out_ref, cbias_ref, pbias_ref, sbias_ref, embed_ref, gain1_ref, shift1_ref, ubias_ref,
+    dbias_ref, gain2_ref, shift2_ref,
+    content_out, query_out, content_grad, query_grad, query_out_w, key_out_w, value_out_w, rel_out_w,
+    tokens, squares, load_sem, store_sem,
 ):
     at = pl.program_id(0)
     core = lax.axis_index("mp")
     cols = out_ref.shape[0]
-
-    @pl.when((at < EARLY - 1) & (at % 2 == 0))
+    late = COUNT - EARLY
+    sources = (
+        (rows_in.at[core], came_in.at[0]),
+        (rows_in.at[2 + core], came_in.at[1]),
+        (keep_in.at[0], grad_in.at[0]),
+        (keep_in.at[1], grad_in.at[1]),
+    )
+    loads = [
+        pltpu.make_async_copy(source, tokens.at[index, side], load_sem.at[index, side])
+        for index, pair in enumerate(sources)
+        for side, source in enumerate(pair)
+    ]
+    stores = [
+        pltpu.make_async_copy(
+            tokens.at[index, side], target.at[core if side == 0 else 1 - core], store_sem.at[index, side]
+        )
+        for index, target in enumerate((content_out, query_out, content_grad, query_grad))
+        for side in range(2)
+    ]
+    square_stores = [
+        pltpu.make_async_copy(squares.at[index], target, store_sem.at[index, 2])
+        for index, target in enumerate((query_out_w, key_out_w, value_out_w, rel_out_w))
+    ]
+
+    @pl.when(at == 0)
+    def _():
+        for copy in loads:
+            copy.start()
+
+    for turn in range(late):
+        lanes = slice(turn * PAIR, (turn + 1) * PAIR)
+
+        @pl.when(at == turn)
+        def _():
+            for index in range(4):
+                part = piece_ref[:, index * PAIR : (index + 1) * PAIR]
+                squares[index, :, lanes] = part.astype(jnp.float32)
+
+    @pl.when(at == late - 1)
+    def _():
+        for copy in square_stores:
+            copy.start()
+        for copy in loads:
+            copy.wait()
+        for copy in stores:
+            copy.start()
+
+    early = at - late
+
+    @pl.when((early >= 0) & (early < EARLY - 1) & (early % 2 == 0))
     def _():
         down_ref[...] = jnp.transpose(piece_ref[...]).astype(jnp.float32)
 
-    @pl.when((at < EARLY - 1) & (at % 2 == 1))
+    @pl.when((early >= 0) & (early < EARLY - 1) & (early % 2 == 1))
     def _():
         up_ref[...] = piece_ref[...].astype(jnp.float32)
 
-    @pl.when(at == EARLY - 1)
+    @pl.when(early == EARLY - 1)
     def _():
         out_ref[...] = jnp.transpose(piece_ref[:, :cols]).astype(jnp.float32)
-
-    @pl.when(at >= EARLY)
-    def _():
-        for turn, target in enumerate((query_ref, key_ref, value_ref, rel_ref)):
-            target[...] = piece_ref[:, turn * PAIR : (turn + 1) * PAIR].astype(jnp.float32)
+        for copy in stores + square_stores:
+            copy.wait()
 
     @pl.when(at == 0)
     def _():
-        content_out[core] = rows_ref[core]
-        content_out[1 - core] = rows_came[0]
-        query_out[core] = rows_ref[2 + core]
-        query_out[1 - core] = rows_came[1]
-        content_grad[core] = keep_ref[0]
-        content_grad[1 - core] = grad_came[0]
-        query_grad[core] = keep_ref[1]
-        query_grad[1 - core] = grad_came[1]
         for line, target in enumerate((cbias_ref, pbias_ref, sbias_ref)):
             target[...] = tiny_ref[line : line + 1, :cols].reshape(cols)
         embed_ref[...] = tiny_ref[3:5, :cols]
@@ -1028,47 +1162,48 @@
 def finish(pieces, rows_out, rows_came, keep_rows, grad_came, tiny, half_ff):
     count, rows, chunk = pieces.shape
     cols = rows // 2
+    late = COUNT - EARLY
     flat = lambda size: jax.ShapeDtypeStruct((size,), jnp.float32)
     square = jax.ShapeDtypeStruct((rows, cols), jnp.float32)
     pair = jax.ShapeDtypeStruct(rows_came.shape, jnp.bfloat16)
     whole = lambda p: (0, 0)
-    lead = lambda p: (0, 0, 0)
     flat_at = lambda size: pl.BlockSpec((size,), lambda p: (0,))
-    once = pl.Buffered(1)
-    token = pl.BlockSpec(rows_came.shape, lead)
-    token_in = pl.BlockSpec(rows_came.shape, lead, pipeline_mode=once)
-    at_chunk = lambda p: jnp.minimum(p // 2, half_ff // chunk - 1)
-    thin = pl.BlockSpec((rows, PAIR), lambda p: (0, jnp.maximum(p - EARLY, 0)))
-    return pl.pallas_call(
+    anywhere = pl.BlockSpec(memory_space=pl.ANY)
+    at_chunk = lambda p: jnp.clip((p - late) // 2, 0, half_ff // chunk - 1)
+    results = pl.pallas_call(
         finish_body,
         out_shape=(
-            pair, pair, pair, pair,
             jax.ShapeDtypeStruct((half_ff, rows), jnp.float32),
             jax.ShapeDtypeStruct((rows, half_ff), jnp.float32),
             jax.ShapeDtypeStruct((cols, rows), jnp.float32),
-            square, square, square, square,
             flat(cols), flat(cols), flat(cols), jax.ShapeDtypeStruct((2, cols), jnp.float32),
             flat(rows), flat(rows), flat(half_ff), flat(rows), flat(rows), flat(rows),
+            pair, pair, pair, pair, square, square, square, square,
         ),
         grid=(count,),
         in_specs=[
-            pl.BlockSpec((None, rows, chunk), lambda p: (p, 0, 0)),
-            pl.BlockSpec(rows_out.shape, lead, pipeline_mode=once),
-            token_in, token_in, token_in,
-            pl.BlockSpec(tiny.shape, whole, pipeline_mode=once),
+            pl.BlockSpec((None, rows, chunk), lambda p: ((p + EARLY) % COUNT, 0, 0)),
+            pl.BlockSpec(tiny.shape, whole, pipeline_mode=pl.Buffered(1)),
+            anywhere, anywhere, anywhere, anywhere,
         ],
         out_specs=[
-            token, token, token, token,
             pl.BlockSpec((chunk, rows), lambda p: (at_chunk(p), 0)),
             pl.BlockSpec((rows, chunk), lambda p: (0, at_chunk(p))),
             pl.BlockSpec((cols, rows), whole),
-            thin, thin, thin, thin,
             flat_at(cols), flat_at(cols), flat_at(cols), pl.BlockSpec((2, cols), whole),
             flat_at(rows), flat_at(rows), flat_at(half_ff), flat_at(rows), flat_at(rows), flat_at(rows),
+        ]
+        + [anywhere] * 8,
+        scratch_shapes=[
+            pltpu.VMEM((4,) + rows_came.shape, jnp.bfloat16),
+            pltpu.VMEM((4, rows, cols), jnp.float32),
+            pltpu.SemaphoreType.DMA((4, 2)),
+            pltpu.SemaphoreType.DMA((4, 3)),
         ],
         compiler_params=pltpu.CompilerParams(vmem_limit_bytes=60 << 20),
         name="finish",
-    )(pieces, rows_out, rows_came, keep_rows, grad_came, tiny)
+    )(pieces, tiny, rows_out, rows_came, keep_rows, grad_came)
+    return results[13:17] + results[:3] + results[17:21] + results[3:13]
 
 
 def position_table(seq_len, width):
@@ -1121,7 +1256,7 @@
         out_weight, up_weight, down_weight, doc_lengths, order_ranks, segment_ids, target_flags,
         content_bias, position_bias, segment_bias, segment_embed, up_bias, jnp.asarray(table),
     )
-    first_t, normal, scale, act, slope, grad, low_rows, low_t, rows_out, sums, norms = feed_forward(
+    act, slope, scale, sums, norms, first_t, normal, grad, low_rows, low_t, rows_out = feed_forward(
         vec_c, vec_q, content, query, cots, out_use, up_use, down_use, up_bias_use,
         (first_gain, first_shift, second_gain, second_shift, down_bias),
     )

time: 264 us -> 251 us (0.951)
  Pallas kernels: 263 us -> 249 us
    pallas_call x1, Pallas kernels: 172 us -> 165 us  [backward(): pl.pallas_call(functools.partial(backward_body, dp_size), out_shape=(jax....]
    pallas_call x1, Pallas kernels: 47.4 us -> 42.7 us  [forward(): pl.pallas_call(forward_body, out_shape=(low_tokens, low_tokens, jax.Shape...]
where the time goes in v7:
time: 251 us; the launch traced here: 250 us
  Pallas kernels  249 us (99%)
    pallas_call x1, Pallas kernels, backward(): pl.pallas_call(functools.partial(backward_body, dp_size), out_shape=(jax....  165 us
    pallas_call x1, Pallas kernels, forward(): pl.pallas_call(forward_body, out_shape=(low_tokens, low_tokens, jax.Shape...  42.7 us
    pallas_call x1, Pallas kernels, feed_forward(): pl.pallas_call(feed_forward_body, out_shape=(jax.ShapeDtypeStruct((rows,...  28 us
    pallas_call x1, Pallas kernels, finish(): pl.pallas_call(finish_body, out_shape=(jax.ShapeDtypeStruct((half_ff, row...  13.3 us

profile of v7, /device:TPU:0, one launch (start us, length us, event | category | flops | bytes accessed | tf_op | source)
XLA Modules:
  0.0 250.3 jit_solution(6212609657002300803)
XLA Ops:
  0.7 42.7 %attend_forward.1 = (bf16[512,768]{1,0:T(8,128)(2,1)}, bf16[512,768]{1,0:T(8,128)(2,1)}, bf16[6,2,2,512,512]{4,3,2,1,0:T(8,128)(2,1)}, f32[512,768]{1,0:T(8,128)...) custom-call(bf16[2,256,768]{2,1,0:T(8,128)(2,1)} %content_in.1, ...), custom_call_target="tpu_custom_call" | custom-call | tf_op jit(solution)/shard_map/attend_forward/pallas_call | solution.py:278
  43.3 28.0 %feed_forward.1 = (bf16[1024,3072]{1,0:T(8,128)(2,1)}, bf16[1024,3072]{1,0:T(8,128)(2,1)}, f32[1024,1]{1,0:T(8,128)}, f32[8,768]{1,0:T(8,128)}, f32[8,768]{1,0:T...) custom-call(bf16[512,768]{1,0:T(8,128)(2,1)} %get-tuple-element.87.v, ...), custom_call_target="tpu_custom_call" | custom-call | tf_op jit(solution)/shard_map/feed_forward/pallas_call | solution.py:469
  71.3 165.5 %backward.1 = (bf16[10,768,512]{2,1,0:T(8,128)(2,1)}, f32[24,512]{1,0:T(8,128)}, bf16[2,256,768]{2,1,0:T(8,128)(2,1)}, bf16[2,256,768]{2,1,0:T(8,128)(2,1)}, bf16[2,256,768]{2,1,0:T(8,128)(2,1)}) custom-call(bf16[512,128]{1,0:T(8,128)(2,1)} %get-tuple-element.78.refs_0_, f32[512,768]{1,0:T(8,128)} %get-tuple-element.79.refs_1_, ...), custom_call_target="tpu_custom_call" | custom-call | tf_op jit(solution)/shard_map/backward/pallas_call | solution.py:1011
  236.8 13.3 %finish.1 = (f32[1536,768]{1,0:T(8,128)}, f32[768,1536]{1,0:T(8,128)}, f32[384,768]{1,0:T(8,128)}, f32[384]{0:T(512)}, f32[384]{0:T(512)}, /*index=5*/f32[384]{0...) custom-call(bf16[10,768,512]{2,1,0:T(8,128)(2,1)} %get-tuple-element, ...), custom_call_target="tpu_custom_call" | custom-call | tf_op jit(solution)/shard_map/finish/pallas_call | solution.py:1173

commit v8 on v7

--- a/solution.py
+++ b/solution.py
@@ -417,9 +417,12 @@
         for copy in first_copies:
             copy.start()
 
-    for stream, at in chunks:
-        there = slice(stream * half_rows + at, stream * half_rows + at + ROWS)
-        value = nn(first_scr[there, :], up_ref[...]) + up_bias[...]
+    spots = [slice(s * half_rows + at, s * half_rows + at + ROWS) for s, at in chunks]
+    ahead = nn(first_scr[spots[0], :], up_ref[...])
+    for turn, there in enumerate(spots):
+        value = ahead + up_bias[...]
+        if turn + 1 < len(spots):
+            ahead = nn(first_scr[spots[turn + 1], :], up_ref[...])
         square = value * value
         half = 0.5 + 0.5 * jnp.tanh(value * (GELU_A + (GELU_A * GELU_B) * square))
         wide = value * half
@@ -526,10 +529,10 @@
 def backward_body(dp_size, *refs):
     (
         seg_hot, proj_c, proj_q, key_ref, value_ref, rel_ref, bias_ref, prob_ref,
-        square_w, act_ref, slope_ref, up_ref, down_ref, low_ref, scale_ref, norms, sums_in,
-        content_t, query_t, table_t, low_t, first_t, normal_in, grad_in, rows_in, vec_c_in, vec_q_in, out_in,
+        square_w, act_ref, slope_ref, up_ref, down_ref, scale_ref, norms, sums_in,
+        content_t, query_t, table_t, low_t, first_t, normal_in, grad_in, rows_in, vec_c_in, vec_q_in, out_in, low_in,
         sum_out, small_out, keep_out, rows_came, grad_came,
-        vt_scr, key_acc, value_acc, rel_acc, total, vec_grad, hid_scr, turn_a, turn_b, flip_scr, vec_c, vec_q, out_w,
+        vt_scr, key_acc, value_acc, rel_acc, total, vec_grad, hid_scr, turn_a, turn_b, flip_scr, vec_c, vec_q, out_w, low_ref,
         work, swapped, landed, extra, small_work, small_far, small_land,
         store_sem, swap_send, swap_recv, fold_send, fold_recv, spread_send, spread_recv,
         more_send, more_recv, tiny_send, tiny_recv, side_sem, keep_sem, back_send, back_recv,
@@ -578,17 +581,17 @@
             work.at[piece], swapped.at[piece], swap_send.at[piece], swap_recv.at[piece], {"mp": 1 - core}
         )
 
-    def fold_copy(fold, piece):
+    def fold_copy(fold, piece, lanes):
         return remote(
-            work.at[piece, given(fold)],
-            landed.at[piece, pl.ds(land_at[fold], lengths[fold])],
+            work.at[piece, given(fold), :lanes],
+            landed.at[piece, pl.ds(land_at[fold], lengths[fold]), :lanes],
             fold_send.at[fold, piece], fold_recv.at[fold, piece], {"dp": partners[fold]},
         )
 
-    def spread_copy(fold, piece):
+    def spread_copy(fold, piece, lanes):
         return remote(
-            swapped.at[piece, kept(fold)],
-            swapped.at[piece, kept(fold)],
+            swapped.at[piece, kept(fold), :lanes],
+            swapped.at[piece, kept(fold), :lanes],
             spread_send.at[fold, piece], spread_recv.at[fold, piece], {"dp": partners[fold]},
         )
 
@@ -596,6 +599,21 @@
         if step == 0:
             return landed.at[piece, pl.ds(rows - lengths[-1], lengths[-1])]
         return extra.at[step - 1, piece]
+
+    def spread_away(fold, piece, lanes):
+        return remote(
+            swapped.at[piece, kept(fold), :lanes], swapped.at[piece, given(fold), :lanes],
+            spread_send.at[fold, piece], spread_recv.at[fold, piece], {"dp": partners[fold]},
+        )
+
+    def sized(piece, act):
+        @pl.when(piece == EARLY - 1)
+        def _():
+            act(cols)
+
+        @pl.when(piece != EARLY - 1)
+        def _():
+            act(width)
 
     def more_copy(step, piece):
         return remote(
@@ -653,34 +671,32 @@
                 (vec_c_in, vec_c),
                 (vec_q_in, vec_q),
                 (out_in, out_w),
+                (low_in, low_ref),
             )
         )
     ]
 
     def stage(number, piece):
         if number == 0:
-            fold_copy(0, piece).start()
+            sized(piece, lambda lanes: fold_copy(0, piece, lanes).start())
         elif number <= FOLDS:
             fold = number - 1
-            fold_copy(fold, piece).wait_recv()
+            sized(piece, lambda lanes: fold_copy(fold, piece, lanes).wait_recv())
             add_rows(piece, kept(fold), landed[piece, pl.ds(land_at[fold], lengths[fold]), :])
             if fold + 1 < FOLDS:
-                fold_copy(fold + 1, piece).start()
+                sized(piece, lambda lanes: fold_copy(fold + 1, piece, lanes).start())
                 return
             for step in range(len(more)):
                 more_copy(step, piece).start()
                 more_copy(step, piece).wait()
                 add_rows(piece, kept(fold), extra_ref(step, piece)[...])
             swapped[piece, kept(fold), :] = work[piece, kept(fold), :]
-            spread_copy(fold, piece).start()
+            sized(piece, lambda lanes: spread_copy(fold, piece, lanes).start())
         else:
             fold = 2 * FOLDS - number
-            remote(
-                swapped.at[piece, kept(fold)], swapped.at[piece, given(fold)],
-                spread_send.at[fold, piece], spread_recv.at[fold, piece], {"dp": partners[fold]},
-            ).wait_recv()
+            sized(piece, lambda lanes: spread_away(fold, piece, lanes).wait_recv())
             if fold > 0:
-                spread_copy(fold - 1, piece).start()
+                sized(piece, lambda lanes: spread_copy(fold - 1, piece, lanes).start())
             else:
                 store(piece).start()
 
@@ -705,7 +721,7 @@
         for device in tiny_devices:
             pl.semaphore_signal(barrier, inc=1, device_id=device, device_id_type=MESH)
         pl.semaphore_wait(barrier, len(tiny_devices))
-        for at in (2, 0, 1, 3, 7, 8, 9):
+        for at in (2, 10, 0, 1, 3, 7, 8, 9):
             side_loads[at].start()
         rows_copy(0).start()
         rows_copy(1).start()
@@ -749,8 +765,8 @@
 
         @pl.when(grid_at == 0)
         def _():
-            side_loads[0].wait()
-            side_loads[1].wait()
+            for at in (10, 0, 1):
+                side_loads[at].wait()
 
         advance(2 * grid_at)
         for at in range(0, total.shape[0], ROWS):
@@ -969,8 +985,8 @@
 
         def drain(piece, carry):
             for fold in range(FOLDS):
-                fold_copy(fold, piece).wait_send()
-                spread_copy(fold, piece).wait_send()
+                sized(piece, lambda lanes: fold_copy(fold, piece, lanes).wait_send())
+                sized(piece, lambda lanes: spread_copy(fold, piece, lanes).wait_send())
             store(piece).wait()
             return carry
 
@@ -1029,9 +1045,9 @@
                 pl.BlockSpec((3, width, PAIR), lambda g: (0, 0, turn(g))),
                 pl.BlockSpec((rows, CHUNK), side), pl.BlockSpec((rows, CHUNK), side),
                 pl.BlockSpec((width, CHUNK), side), pl.BlockSpec((CHUNK, width), lambda g: (chunk(g), 0)),
-                keep((rows, width)), keep((rows, 1)), keep((8, width)), keep((8, width)),
+                keep((rows, 1)), keep((8, width)), keep((8, width)),
             ]
-            + [anywhere] * 11,
+            + [anywhere] * 12,
             out_specs=[
                 anywhere,
                 pl.BlockSpec((small_rows, CHUNK), whole),
@@ -1051,6 +1067,7 @@
                 pltpu.VMEM((seq_len, width), low),
                 pltpu.VMEM((seq_len, width), low),
                 pltpu.VMEM((width, width), low),
+                pltpu.VMEM((rows, width), low),
                 pieces, pieces, pieces,
                 pltpu.VMEM((max(1, more - 1), COUNT if dp_size > 32 else 1, width >> FOLDS, CHUNK), low),
                 pltpu.VMEM((tiny + 1, small_rows, CHUNK), jnp.float32),
@@ -1059,7 +1076,7 @@
                 dma((COUNT,)), dma((COUNT,)), dma((COUNT,)),
                 dma((FOLDS, COUNT)), dma((FOLDS, COUNT)), dma((FOLDS, COUNT)), dma((FOLDS, COUNT)),
                 dma((more, COUNT)), dma((more, COUNT)), dma((tiny,)), dma((tiny,)),
-                dma((10,)), dma((2,)), dma((4,)), dma((4,)),
+                dma((11,)), dma((2,)), dma((4,)), dma((4,)),
             ],
         ),
         compiler_params=pltpu.CompilerParams(
@@ -1068,8 +1085,8 @@
         name="backward",
     )(
         seg_hot, proj_c, proj_q, keys, values, rel_keys, lines, prob, squares,
-        act, slope, up_w, down_w, low_rows, scale, norms, sums,
-        content_t, query_t, table_t, low_t, first_t, normal, grad, rows_in, vec_c, vec_q, out_w,
+        act, slope, up_w, down_w, scale, norms, sums,
+        content_t, query_t, table_t, low_t, first_t, normal, grad, rows_in, vec_c, vec_q, out_w, low_rows,
     )
 
 

time: 251 us -> 250 us (level)
  no operation moved by 1% of the time
where the time goes in v8:
time: 250 us
  Pallas kernels  249 us (100%)
    pallas_call x1, Pallas kernels, backward(): pl.pallas_call(functools.partial(backward_body, dp_size), out_shape=(jax....  165 us
    pallas_call x1, Pallas kernels, forward(): pl.pallas_call(forward_body, out_shape=(low_tokens, low_tokens, jax.Shape...  42.7 us
    pallas_call x1, Pallas kernels, feed_forward(): pl.pallas_call(feed_forward_body, out_shape=(jax.ShapeDtypeStruct((rows,...  27.9 us
    pallas_call x1, Pallas kernels, finish(): pl.pallas_call(finish_body, out_shape=(jax.ShapeDtypeStruct((half_ff, row...  13.3 us

profile of v8, /device:TPU:0, one launch (start us, length us, event | category | flops | bytes accessed | tf_op | source)
XLA Modules:
  0.0 249.7 jit_solution(10681476791588579068)
XLA Ops:
  0.7 42.7 %attend_forward.1 = (bf16[512,768]{1,0:T(8,128)(2,1)}, bf16[512,768]{1,0:T(8,128)(2,1)}, bf16[6,2,2,512,512]{4,3,2,1,0:T(8,128)(2,1)}, f32[512,768]{1,0:T(8,128)...) custom-call(bf16[2,256,768]{2,1,0:T(8,128)(2,1)} %content_in.1, ...), custom_call_target="tpu_custom_call" | custom-call | tf_op jit(solution)/shard_map/attend_forward/pallas_call | solution.py:278
  43.3 27.9 %feed_forward.1 = (bf16[1024,3072]{1,0:T(8,128)(2,1)}, bf16[1024,3072]{1,0:T(8,128)(2,1)}, f32[1024,1]{1,0:T(8,128)}, f32[8,768]{1,0:T(8,128)}, f32[8,768]{1,0:T...) custom-call(bf16[512,768]{1,0:T(8,128)(2,1)} %get-tuple-element.87.v, ...), custom_call_target="tpu_custom_call" | custom-call | tf_op jit(solution)/shard_map/feed_forward/pallas_call | solution.py:472
  71.3 164.9 %backward.1 = (bf16[10,768,512]{2,1,0:T(8,128)(2,1)}, f32[24,512]{1,0:T(8,128)}, bf16[2,256,768]{2,1,0:T(8,128)(2,1)}, bf16[2,256,768]{2,1,0:T(8,128)(2,1)}, bf16[2,256,768]{2,1,0:T(8,128)(2,1)}) custom-call(bf16[512,128]{1,0:T(8,128)(2,1)} %get-tuple-element.78.refs_0_, f32[512,768]{1,0:T(8,128)} %get-tuple-element.79.refs_1_, ...), custom_call_target="tpu_custom_call" | custom-call | tf_op jit(solution)/shard_map/backward/pallas_call | solution.py:1027
  236.2 13.3 %finish.1 = (f32[1536,768]{1,0:T(8,128)}, f32[768,1536]{1,0:T(8,128)}, f32[384,768]{1,0:T(8,128)}, f32[384]{0:T(512)}, f32[384]{0:T(512)}, /*index=5*/f32[384]{0...) custom-call(bf16[10,768,512]{2,1,0:T(8,128)(2,1)} %get-tuple-element, ...), custom_call_target="tpu_custom_call" | custom-call | tf_op jit(solution)/shard_map/finish/pallas_call | solution.py:1190
